TPU v7x, 32 devices: a whole 2x2x4 slice. The times are simulated.
32 devices in a mesh: dp: 8 (over z, y), tensor: 4 (over x, core).
Axes of the slice: x: 2, y: 2, z: 4, core: 2. Of those that a mesh axis runs over, the one named last changes fastest.
Arguments:
- layer_in: bfloat16 [8192, 2048], P(('dp', 'tensor')), may hold values from -6 to 6
- cotangent: bfloat16 [8192, 2048], P(('dp', 'tensor')), may hold values from -6 to 6
- segments: int32 [8, 1024], P('dp'), may hold values from 0 to 3, never falling along the last dimension, each value on 1 to 800 neighbouring positions
- gain_attn: bfloat16 [2048], replicated, may hold values from 0.099609375 to 1.8984375
- w_query: bfloat16 [2048, 2048], P(None, 'tensor'), may hold values from -0.5 to 0.5
- key_weight: bfloat16 [2048, 512], P(None, 'tensor'), may hold values from -0.5 to 0.5
- value_weight: bfloat16 [2048, 512], P(None, 'tensor'), may hold values from -0.125 to 0.125
- w_out: bfloat16 [2048, 2048], P('tensor'), may hold values from -1 to 1
- gain_ffn: bfloat16 [2048], replicated, may hold values from 0.099609375 to 1.8984375
- w_gate: bfloat16 [2048, 8192], P(None, 'tensor'), may hold values from -0.125 to 0.125
- w_up: bfloat16 [2048, 8192], P(None, 'tensor'), may hold values from -0.125 to 0.125
- w_down: bfloat16 [8192, 2048], P('tensor'), may hold values from -0.25 to 0.25
Outputs:
- layer_out: bfloat16 [8192, 2048], P(('dp', 'tensor'))
- grad_in: bfloat16 [8192, 2048], P(('dp', 'tensor'))
- grad_gain_attn: float32 [2048], P('dp')
- grad_query: float32 [2048, 2048], P('dp', 'tensor')
- grad_key: float32 [2048, 512], P('dp', 'tensor')
- grad_value: float32 [2048, 512], P('dp', 'tensor')
- grad_out: float32 [2048, 2048], P('tensor', 'dp')
- grad_gain_ffn: float32 [2048], P('dp')
- grad_gate: float32 [2048, 8192], P('dp', 'tensor')
- grad_up: float32 [2048, 8192], P('dp', 'tensor')
- grad_down: float32 [8192, 2048], P('tensor', 'dp')
Inputs may be any that keep to these rules, and one draw needn't show every extreme that they name: `segments`: within each sequence the numbers never fall; a document holds at most 800 tokens and some document holds exactly 800.
All inputs are finite; a program needn't handle non-finite values.
Results may differ from a plain program's by a relative error of at most 0.023.
Values may be sent and summed in bfloat16 or wider, within the bound.
A program may use at most 320 MiB of HBM per device.

v0:
```python
import jax
import jax.numpy as jnp
from jax import lax
from jax.sharding import PartitionSpec as P

HEAD_SIZE = 64


EPSILON = 1e-05
MULTIPLIER = 0.015625
RESIDUAL_SCALE = 0.22
THETA_BASE = 10000.0
MASK_VALUE = -1e30


def positions_of(seg_ids):
    length = seg_ids.shape[-1]
    index = jnp.broadcast_to(jnp.arange(length, dtype=jnp.int32), seg_ids.shape)
    before = jnp.concatenate([seg_ids[:, :1] - 1, seg_ids[:, :-1]], axis=1)
    starts = jnp.where(seg_ids != before, index, jnp.zeros_like(index))
    return index - lax.cummax(starts, axis=1)


def rope_tables(positions):
    half = HEAD_SIZE // 2
    freq = THETA_BASE ** (-2.0 * jnp.arange(half, dtype=jnp.float32) / HEAD_SIZE)
    angle = positions.astype(jnp.float32)[:, None] * freq[None, :]
    return (jnp.cos(angle), jnp.sin(angle))


def apply_rotary(value_rows, cosine_table, sine_table):
    half = HEAD_SIZE // 2
    first = value_rows[..., :half]
    second = value_rows[..., half:]
    cos_b = cosine_table[:, None, :]
    sin_b = sine_table[:, None, :]
    return jnp.concatenate(
        [first * cos_b - second * sin_b, second * cos_b + first * sin_b], axis=-1
    )


def masked_scores(query_rows, key_rows, seg_ids):
    length = seg_ids.shape[0]
    raw = jnp.einsum("qhgd,khd->hgqk", query_rows, key_rows, preferred_element_type=jnp.float32)
    index = jnp.arange(length, dtype=jnp.int32)
    allowed = (seg_ids[:, None] == seg_ids[None, :]) & (index[None, :] <= index[:, None])
    return jnp.where(allowed, MULTIPLIER * raw, MASK_VALUE)


def probabilities(query_rows, key_rows, seg_ids):
    scores = masked_scores(query_rows, key_rows, seg_ids)
    top = jnp.max(scores, axis=-1, keepdims=True)
    lse = top + jnp.log(jnp.sum(jnp.exp(scores - top), axis=-1, keepdims=True))
    return (jnp.exp(scores - lse), lse)


def attend(probs, value_rows):
    return jnp.einsum(
        "hgqk,khd->qhgd", probs.astype(jnp.bfloat16), value_rows, preferred_element_type=jnp.float32
    )


def attend_back(probs, query_rows, key_rows, value_rows, d_attn):
    d_prob = jnp.einsum("qhgd,khd->hgqk", d_attn, value_rows, preferred_element_type=jnp.float32)
    inner = jnp.sum(probs * d_prob, axis=-1, keepdims=True)
    d_score = (probs * (d_prob - inner)).astype(jnp.bfloat16)
    d_query = MULTIPLIER * jnp.einsum(
        "hgqk,khd->qhgd", d_score, key_rows, preferred_element_type=jnp.float32
    )
    d_keys = MULTIPLIER * jnp.einsum(
        "hgqk,qhgd->khd", d_score, query_rows, preferred_element_type=jnp.float32
    )
    d_values = jnp.einsum(
        "hgqk,qhgd->khd", probs.astype(jnp.bfloat16), d_attn, preferred_element_type=jnp.float32
    )
    return (d_query, d_keys, d_values)


def norm_back(d_normed, value_rows, inverse, gain):
    grad_gain = jnp.sum(d_normed * value_rows * inverse, axis=0)
    scaled = d_normed * gain
    d_values = inverse * scaled - value_rows * inverse**3 * jnp.mean(
        scaled * value_rows, axis=-1, keepdims=True
    )
    return (d_values, grad_gain)


def body(
    layer_in,
    cotangent,
    segments,
    gain_attn,
    w_query,
    key_weight,
    value_weight,
    w_out,
    gain_ffn,
    w_gate,
    w_up,
    w_down,
):
    share = layer_in.shape[0]
    full_in, full_cot = (
        lax.all_gather(layer_in, "tensor", axis=0, tiled=True),
        lax.all_gather(cotangent, "tensor", axis=0, tiled=True),
    )
    inputs = full_in.astype(jnp.float32)
    token_rows = inputs.shape[0]
    seqs, length = segments.shape
    heads = w_query.shape[1] // HEAD_SIZE
    kv_heads = key_weight.shape[1] // HEAD_SIZE
    query_group = heads // kv_heads
    positions = positions_of(segments).reshape(-1)
    cosine_table, sine_table = rope_tables(positions)
    gain_one = gain_attn.astype(jnp.float32)
    gain_two = gain_ffn.astype(jnp.float32)
    rank = lax.axis_index("tensor")
    inverse_one = lax.rsqrt(jnp.mean(inputs * inputs, axis=-1, keepdims=True) + EPSILON)
    normalized_input = (inputs * inverse_one * gain_one).astype(jnp.bfloat16)
    query_rows = jnp.dot(normalized_input, w_query, preferred_element_type=jnp.float32).reshape(
        token_rows, heads, HEAD_SIZE
    )
    key_rows = jnp.dot(normalized_input, key_weight, preferred_element_type=jnp.float32).reshape(
        token_rows, kv_heads, HEAD_SIZE
    )
    value_rows = jnp.dot(normalized_input, value_weight, preferred_element_type=jnp.float32).astype(
        jnp.bfloat16
    )
    rotated_query = (
        apply_rotary(query_rows, cosine_table, sine_table)
        .astype(jnp.bfloat16)
        .reshape(seqs, length, kv_heads, query_group, HEAD_SIZE)
    )
    rotated_keys = (
        apply_rotary(key_rows, cosine_table, sine_table)
        .astype(jnp.bfloat16)
        .reshape(seqs, length, kv_heads, HEAD_SIZE)
    )
    values_seq = value_rows.reshape(seqs, length, kv_heads, HEAD_SIZE)

    def forward_one(items):
        probs, lse = probabilities(items[0], items[1], items[3])
        return (attend(probs, items[2]), probs)

    attended, saved = lax.map(forward_one, (rotated_query, rotated_keys, values_seq, segments))
    attn_low = attended.reshape(token_rows, heads * HEAD_SIZE).astype(jnp.bfloat16)
    attn_total = lax.psum(jnp.dot(attn_low, w_out, preferred_element_type=jnp.float32), "tensor")
    hidden = inputs + RESIDUAL_SCALE * attn_total
    inverse_two = lax.rsqrt(jnp.mean(hidden * hidden, axis=-1, keepdims=True) + EPSILON)
    normed_two = (hidden * inverse_two * gain_two).astype(jnp.bfloat16)
    gate = jnp.dot(normed_two, w_gate, preferred_element_type=jnp.float32)
    upper = jnp.dot(normed_two, w_up, preferred_element_type=jnp.float32)
    sigma = jax.nn.sigmoid(gate)
    active = gate * sigma
    mixed = (active * upper).astype(jnp.bfloat16)
    ffn_part = jnp.dot(mixed, w_down, preferred_element_type=jnp.float32)
    ffn_total = lax.psum(ffn_part.astype(jnp.bfloat16), "tensor").astype(jnp.float32)
    out_full = hidden + RESIDUAL_SCALE * ffn_total
    out_rows = lax.dynamic_slice_in_dim(out_full, rank * share, share, 0).astype(jnp.bfloat16)
    d_out = full_cot.astype(jnp.float32)
    d_branch = (RESIDUAL_SCALE * d_out).astype(jnp.bfloat16)
    grad_down = jnp.einsum("tf,td->fd", mixed, d_branch, preferred_element_type=jnp.float32)
    d_mixed = jnp.einsum("td,fd->tf", d_branch, w_down, preferred_element_type=jnp.float32)
    d_gate = (d_mixed * upper * sigma * (1.0 + gate * (1.0 - sigma))).astype(jnp.bfloat16)
    d_upper = (d_mixed * active).astype(jnp.bfloat16)
    grad_gate = jnp.einsum("td,tf->df", normed_two, d_gate, preferred_element_type=jnp.float32)
    grad_up = jnp.einsum("td,tf->df", normed_two, d_upper, preferred_element_type=jnp.float32)
    d_norm_part = jnp.einsum("tf,df->td", d_gate, w_gate, preferred_element_type=jnp.float32)
    d_norm_part = d_norm_part + jnp.einsum(
        "tf,df->td", d_upper, w_up, preferred_element_type=jnp.float32
    )
    d_normed_two = lax.psum(d_norm_part, "tensor")
    d_hidden_norm, grad_gain_two = norm_back(d_normed_two, hidden, inverse_two, gain_two)
    d_hidden = d_out + d_hidden_norm
    d_attn_total = (RESIDUAL_SCALE * d_hidden).astype(jnp.bfloat16)
    grad_wout = jnp.einsum("tc,td->cd", attn_low, d_attn_total, preferred_element_type=jnp.float32)
    d_attn = jnp.einsum("td,cd->tc", d_attn_total, w_out, preferred_element_type=jnp.float32)
    d_attn = d_attn.astype(jnp.bfloat16).reshape(seqs, length, kv_heads, query_group, HEAD_SIZE)

    def back_one(items):
        return attend_back(items[5], items[0], items[1], items[2], items[4])

    d_query_rot, d_keys_rot, d_values = lax.map(
        back_one, (rotated_query, rotated_keys, values_seq, segments, d_attn, saved)
    )
    d_query = (
        apply_rotary(d_query_rot.reshape(token_rows, heads, HEAD_SIZE), cosine_table, -sine_table)
        .astype(jnp.bfloat16)
        .reshape(token_rows, heads * HEAD_SIZE)
    )
    d_keys = (
        apply_rotary(d_keys_rot.reshape(token_rows, kv_heads, HEAD_SIZE), cosine_table, -sine_table)
        .astype(jnp.bfloat16)
        .reshape(token_rows, kv_heads * HEAD_SIZE)
    )
    d_values_low = d_values.astype(jnp.bfloat16).reshape(token_rows, kv_heads * HEAD_SIZE)
    grad_wquery = jnp.einsum(
        "td,tc->dc", normalized_input, d_query, preferred_element_type=jnp.float32
    )
    grad_wkey = jnp.einsum(
        "td,tc->dc", normalized_input, d_keys, preferred_element_type=jnp.float32
    )
    grad_wvalue = jnp.einsum(
        "td,tc->dc", normalized_input, d_values_low, preferred_element_type=jnp.float32
    )
    d_norm_one = jnp.einsum("tc,dc->td", d_query, w_query, preferred_element_type=jnp.float32)
    d_norm_one = d_norm_one + jnp.einsum(
        "tc,dc->td", d_keys, key_weight, preferred_element_type=jnp.float32
    )
    d_norm_one = d_norm_one + jnp.einsum(
        "tc,dc->td", d_values_low, value_weight, preferred_element_type=jnp.float32
    )
    d_normed = lax.psum(d_norm_one.astype(jnp.bfloat16), "tensor").astype(jnp.float32)
    d_input_norm, grad_gain_one = norm_back(d_normed, inputs, inverse_one, gain_one)
    d_input = d_hidden + d_input_norm
    grad_rows = lax.dynamic_slice_in_dim(d_input, rank * share, share, 0).astype(jnp.bfloat16)
    summed = (
        lax.psum_scatter(
            grad_wquery.astype(jnp.bfloat16), "dp", scatter_dimension=0, tiled=True
        ).astype(jnp.float32),
        lax.psum_scatter(
            grad_wkey.astype(jnp.bfloat16), "dp", scatter_dimension=0, tiled=True
        ).astype(jnp.float32),
        lax.psum_scatter(
            grad_wvalue.astype(jnp.bfloat16), "dp", scatter_dimension=0, tiled=True
        ).astype(jnp.float32),
        lax.psum_scatter(
            grad_wout.astype(jnp.bfloat16), "dp", scatter_dimension=1, tiled=True
        ).astype(jnp.float32),
        lax.psum_scatter(
            grad_gain_one.astype(jnp.bfloat16), "dp", scatter_dimension=0, tiled=True
        ).astype(jnp.float32),
        lax.psum_scatter(
            grad_gain_two.astype(jnp.bfloat16), "dp", scatter_dimension=0, tiled=True
        ).astype(jnp.float32),
        lax.psum_scatter(
            grad_gate.astype(jnp.bfloat16), "dp", scatter_dimension=0, tiled=True
        ).astype(jnp.float32),
        lax.psum_scatter(
            grad_up.astype(jnp.bfloat16), "dp", scatter_dimension=0, tiled=True
        ).astype(jnp.float32),
        lax.psum_scatter(
            grad_down.astype(jnp.bfloat16), "dp", scatter_dimension=1, tiled=True
        ).astype(jnp.float32),
    )
    return (
        out_rows,
        grad_rows,
        summed[4],
        summed[0],
        summed[1],
        summed[2],
        summed[3],
        summed[5],
        summed[6],
        summed[7],
        summed[8],
    )


def solution(mesh):
    return jax.shard_map(
        body,
        mesh=mesh,
        in_specs=(
            P(("dp", "tensor"), None),
            P(("dp", "tensor"), None),
            P("dp", None),
            P(),
            P(None, "tensor"),
            P(None, "tensor"),
            P(None, "tensor"),
            P("tensor", None),
            P(),
            P(None, "tensor"),
            P(None, "tensor"),
            P("tensor", None),
        ),
        out_specs=(
            P(("dp", "tensor"), None),
            P(("dp", "tensor"), None),
            P("dp"),
            P("dp", "tensor"),
            P("dp", "tensor"),
            P("dp", "tensor"),
            P("tensor", "dp"),
            P("dp"),
            P("dp", "tensor"),
            P("dp", "tensor"),
            P("tensor", "dp"),
        ),
        check_vma=False,
    )
```

profile of v0, /device:TPU:16, one launch (start us, length us, event | category | flops | bytes accessed | tf_op | source)
XLA Modules:
  0.0 1490.0 jit_solution(3022676472786269194)
XLA Ops:
  13.3 2.3 fusion.16
  15.6 29.5 %all-gather.3.cloned.1.call-done = bf16[1024,2048]{1,0:T(8,128)(2,1)} async-done(((bf16[256,2048]{1,0:T(8,128)(2,1)}), bf16[1024,2048]{1,0:T(8,128)(2,1)}) %all-gather.3.cloned.1.call-update) | async-done | bytes 4194320 | tf_op jit(solution)/shard_map/all_gather | solution.py:104
  45.2 3.1 fusion.4
  48.9 3.3 fusion.6
  55.4 2.4 fusion.49
  58.3 13.8 fusion.47
  72.2 13.1 exponential_reduce_fusion
  85.3 13.4 fusion.25
  99.7 5.6 fusion.50
  106.1 152.2 %all-reduce.8.cloned.1.call-done = f32[1024,2048]{1,0:T(8,128)} async-done(((f32[1024,2048]{1,0:T(8,128)}), f32[1024,2048]{1,0:T(8,128)}) %all-reduce.8.cloned.1.call-update) | async-done | bytes 8388624 | tf_op jit(solution)/shard_map/psum | solution.py:147
  258.3 6.0 multiply_reduce_fusion.2
  265.1 17.0 %fusion.52 = f32[1024,2048]{1,0:T(8,128)} fusion(bf16[1024,2048]{1,0:T(8,128)(2,1)S(1)} %multiply_convert_fusion.4, bf16[2048,2048]{1,0:T(8,128)(2,1)} %param.22), kind=kOutput, calls=%fused_computation.110 | convolution fusion | flops 8589934592 | bytes 20971520 | tf_op jit(solution)/shard_map/dot_general | solution.py:152
  282.1 13.3 fusion.51
  295.4 21.9 %multiply_convert_fusion.1 = (bf16[1024,2048]{1,0:T(8,128)(2,1)}, bf16[1024,2048]{1,0:T(8,128)(2,1)}, bf16[1024,2048]{1,0:T(8,128)(2,1)}) fusion(f32[1024,2048]{1,0:T(8,128)} %fusion.51, f32[1024,2048]{1,0:T(8,128)} %fusion.52, bf16[2048,2048]{1,0:T(8,128)(2,1)} %param.23, bf16[1024,2048]{1,0:T(8,128)(2,1)} %all-gather.5.cloned.1.call-done), kind=kOutput, calls=%fused_computation.28 | convolution fusion | flops 8627683328 | bytes 41943040 | tf_op jit(solution)/shard_map/td,fd->tf/dot_general | solution.py:163
  317.3 12.9 fusion.53
  330.2 13.5 convolution_add_fusion
  343.7 14.1 convolution_convert_fusion.3
  357.8 139.0 %all-reduce.10.cloned.1.call-done = f32[1024,2048]{1,0:T(8,128)} async-done(((f32[1024,2048]{1,0:T(8,128)}), f32[1024,2048]{1,0:T(8,128)}) %all-reduce.10.cloned.1.call-update) | async-done | bytes 8388624 | tf_op jit(solution)/shard_map/psum | solution.py:172
  496.8 7.8 multiply_reduce_fusion
  506.2 4.7 convert_add_fusion
  510.9 2.4 fusion.28
  514.2 13.3 fusion.34
  527.6 21.6 %fusion = (f32[2,4,1024]{2,1,0:T(4,128)S(1)}, f32[2,1024,1024,4]{2,1,3,0:T(8,128)}) fusion(f32[2,4,1024,1024]{2,3,1,0:T(8,128)} %get-tuple-element.89, f32[2,4,1024]{2,1,0:T(4,128)S(1)} %bitcast.124, bf16[1024,2,64,1]{0,2,3,1:T(8,128)(2,1)S(1)} %bitcast.121, bf16[1024,2,4,64]{0,3,2,1:T(8,128)(2,1)S(1)} %bitcast.116), kind=kOutput, calls=%fused_computation.2 | convolution fusion | flops 1098899456 | bytes 68485120 | tf_op jit(solution)/shard_map/while/body/eval_jaxpr/qhgd,khd->hgqk/dot_general | solution.py:64
  549.2 28.4 %fusion.2 = bf16[2,4,1024,1024]{2,3,1,0:T(8,128)(2,1)} fusion(f32[2,1024,1024,4]{2,1,3,0:T(8,128)} %get-tuple-element.91, f32[2,4,1024,1024]{2,3,1,0:T(8,128)} %get-tuple-element.89, f32[2,4,1024]{2,1,0:T(4,128)S(1)} %get-tuple-element.90, f32[2,4,1024]{2,1,0:T(4,128)S(1)} %bitcast.125), kind=kLoop, calls=%fused_computation.4 | loop fusion | flops 33554432 | bytes 83951616 | tf_op jit(solution)/shard_map/while/body/eval_jaxpr/convert_element_type | solution.py:66
  577.6 11.0 fusion.30
  588.6 9.0 convolution_multiply_fusion
  600.6 4.4 convolution_convert_fusion.7
  605.0 7.2 fusion.54
  615.9 3.4 add_convert_fusion
  620.5 7.1 convolution_convert_fusion.4
  627.6 5.9 convolution_convert_fusion.5
  633.8 14.2 convolution_convert_fusion
  648.1 14.0 convolution_convert_fusion.1
  662.4 14.1 convolution_convert_fusion.2
  679.3 6.5 convert_element_type.157
  687.3 38.9 %reduce-scatter.10.cloned.1.call-done = bf16[256,128]{1,0:T(8,128)(2,1)} async-done(((bf16[2048,128]{1,0:T(8,128)(2,1)}), bf16[256,128]{1,0:T(8,128)(2,1)}) %reduce-scatter.10.cloned.1.call-update) | async-done | bytes 65552 | tf_op jit(solution)/shard_map/reduce_scatter | solution.py:221
  727.8 154.3 %all-reduce.12.cloned.1.call-done = (bf16[1024,2048]{1,0:T(8,128)(2,1)}, bf16[1024,2048]{1,0:T(8,128)(2,1)}) async-done(((bf16[1024,2048]{1,0:T(8,128)(2,1)}, bf16[1024,2048]{1,0:T(8,128)(2,1)}), (bf16[1024,2048]{1,0:T(8,128)(2,1)}, bf16[1024,2048]{1,0:T(8,128)(2,1)})) %all-reduce.12.cloned.1.call-update) | async-done | bytes 8388624 | tf_op jit(solution)/shard_map/psum | solution.py:157
  882.1 7.6 fusion.10
  889.7 63.9 %reduce-scatter.14.cloned.1.call-done = bf16[512,256]{1,0:T(8,128)(2,1)} async-done(((bf16[512,2048]{1,0:T(8,128)(2,1)}), bf16[512,256]{1,0:T(8,128)(2,1)}) %reduce-scatter.14.cloned.1.call-update) | async-done | bytes 262160 | tf_op jit(solution)/shard_map/reduce_scatter | solution.py:227
  955.3 68.9 %reduce-scatter.8.cloned.1.call-done = bf16[256,512]{1,0:T(8,128)(2,1)} async-done(((bf16[2048,512]{1,0:T(8,128)(2,1)}), bf16[256,512]{1,0:T(8,128)(2,1)}) %reduce-scatter.8.cloned.1.call-update) | async-done | bytes 262160 | tf_op jit(solution)/shard_map/reduce_scatter | solution.py:218
  1026.1 16.8 %all-reduce.2 = (bf16[2048]{0:T(1024)(128)(2,1)S(1)}, bf16[2048]{0:T(1024)(128)(2,1)S(1)}) all-reduce(bf16[2048]{0:T(1024)(128)(2,1)S(1)} %get-tuple-element.52, bf16[2048]{0:T(1024)(128)(2,1)S(1)} %copy-done.35), channel_id=2, replica_groups=mesh['dp'=8,'tensor'=4] {'dp'}, use_global_device_ids=true, to_apply=%region_14.15.clone | all-reduce | flops 4096 | bytes 16384
  1043.6 5.8 fusion.20
  1049.4 127.0 %reduce-scatter.20.cloned.1.call-done = bf16[2048,256]{1,0:T(8,128)(2,1)} async-done(((bf16[2048,2048]{1,0:T(8,128)(2,1)}), bf16[2048,256]{1,0:T(8,128)(2,1)}) %reduce-scatter.20.cloned.1.call-update) | async-done | bytes 1048592 | tf_op jit(solution)/shard_map/reduce_scatter | solution.py:242
  1176.3 2.7 convert_element_type.203
  1179.0 149.4 %reduce-scatter.18.cloned.1.call-done = bf16[256,2048]{1,0:T(8,128)(2,1)} async-done(((bf16[2048,2048]{1,0:T(8,128)(2,1)}), bf16[256,2048]{1,0:T(8,128)(2,1)}) %reduce-scatter.18.cloned.1.call-update) | async-done | bytes 1048592 | tf_op jit(solution)/shard_map/reduce_scatter | solution.py:239
  1328.4 2.8 convert_element_type.201
  1331.2 148.7 %reduce-scatter.16.cloned.1.call-done = bf16[256,2048]{1,0:T(8,128)(2,1)} async-done(((bf16[2048,2048]{1,0:T(8,128)(2,1)}), bf16[256,2048]{1,0:T(8,128)(2,1)}) %reduce-scatter.16.cloned.1.call-update) | async-done | bytes 1048592 | tf_op jit(solution)/shard_map/reduce_scatter | solution.py:236
  1480.0 2.8 convert_element_type.199
  (143 shorter events, 32.5 us)
Async XLA Ops:
  7.2 92.5 %copy-start = (bf16[512,2048]{1,0:T(8,128)(2,1)S(1)}, bf16[512,2048]{1,0:T(8,128)(2,1)}, u32[]{:S(2)}) copy-start(bf16[512,2048]{1,0:T(8,128)(2,1)} %param.19) | copy-start | bytes 6291460
  7.2 45.0 %copy-start.18 = (bf16[2048,128]{1,0:T(8,128)(2,1)S(1)}, bf16[2048,128]{1,0:T(8,128)(2,1)}, u32[]{:S(2)}) copy-start(bf16[2048,128]{1,0:T(8,128)(2,1)} %param.18) | copy-start | bytes 1572868
  7.2 38.0 %all-gather.3.cloned.1.call-start = ((), (), s32[]{:S(2)}) async-start(), calls=%async_computation.7 | async-start | bytes 5242880 | tf_op jit(solution)/shard_map/all_gather | solution.py:104
  7.9 250.4 %all-reduce.8.cloned.1.call-start = ((), (), s32[]{:S(2)}) async-start(), calls=%async_computation.8 | async-start | bytes 16777216 | tf_op jit(solution)/shard_map/psum | solution.py:147
  12.0 41.8 %copy-start.31 = (f32[2048]{0:T(1024)}, f32[2048]{0:T(1024)S(1)}, u32[]{:S(2)}) copy-start(f32[2048]{0:T(1024)S(1)} %convert_element_type.158) | copy-start | bytes 24580
  13.3 44.6 %copy-start.10 = (f32[1024,32]{0,1:T(8,128)}, f32[1024,32]{0,1:T(8,128)S(1)}, u32[]{:S(2)}) copy-start(f32[1024,32]{0,1:T(8,128)S(1)} %get-tuple-element.83) | copy-start | bytes 393220
  15.6 38.1 %copy-start.16 = (bf16[2048,128]{1,0:T(8,128)(2,1)S(1)}, bf16[2048,128]{1,0:T(8,128)(2,1)}, u32[]{:S(2)}) copy-start(bf16[2048,128]{1,0:T(8,128)(2,1)} %param.17) | copy-start | bytes 1572868
  48.9 6.5 copy-start.33
  48.9 6.5 copy-start.37
  52.2 5.6 copy-start.3
  53.8 31.5 %copy-start.12 = (bf16[1024,128]{0,1:T(8,128)(2,1)}, bf16[1024,128]{0,1:T(8,128)(2,1)S(1)}, u32[]{:S(2)}) copy-start(bf16[1024,128]{0,1:T(8,128)(2,1)S(1)} %convolution_convert_fusion.8) | copy-start | bytes 786436
  55.3 3.0 copy-start.27
  57.9 14.2 copy-start.28
  57.9 14.2 copy-start.30
  58.3 13.9 copy-start.20
  58.3 13.9 copy-start.22
  85.3 13.4 copy-start.14
  99.7 6.4 copy-start.36
  105.3 190.1 %all-gather.5.cloned.1.call-start = ((), (), s32[]{:S(2)}) async-start(), calls=%async_computation.9 | async-start | bytes 5242880 | tf_op jit(solution)/shard_map/all_gather | solution.py:105
  106.0 390.7 %all-reduce.10.cloned.1.call-start = ((), (), s32[]{:S(2)}) async-start(), calls=%async_computation.10 | async-start | bytes 16777216 | tf_op jit(solution)/shard_map/psum | solution.py:172
  264.3 17.8 %copy-start.2 = (f32[1024,2048]{1,0:T(8,128)}, f32[1024,2048]{1,0:T(8,128)S(1)}, u32[]{:S(2)}) copy-start(f32[1024,2048]{1,0:T(8,128)S(1)} %get-tuple-element.68) | copy-start | bytes 25165828
  265.1 17.0 %copy-start.8 = (bf16[1024,2048]{1,0:T(8,128)(2,1)}, bf16[1024,2048]{1,0:T(8,128)(2,1)S(1)}, u32[]{:S(2)}) copy-start(bf16[1024,2048]{1,0:T(8,128)(2,1)S(1)} %multiply_convert_fusion.4) | copy-start | bytes 12582916
  317.3 12.9 copy-start.39
  343.7 342.1 %reduce-scatter.12.cloned.1.call-start = ((), (), s32[]{:S(2)}) async-start(), calls=%async_computation.13 | async-start | bytes 589824 | tf_op jit(solution)/shard_map/reduce_scatter | solution.py:224
  496.8 8.2 copy-start.5
  496.8 9.4 copy-start.9
  510.9 3.3 copy-start.6
  510.9 3.3 copy-start.15
  514.2 13.3 copy-start.13
  549.2 28.5 %copy-start.21 = (bf16[1024,8,32]{0,2,1:T(8,128)(2,1)S(1)}, bf16[1024,8,32]{0,2,1:T(8,128)(2,1)}, u32[]{:S(2)}) copy-start(bf16[1024,8,32]{0,2,1:T(8,128)(2,1)} %copy-done.20) | copy-start | bytes 1572868
  549.2 28.4 %copy-start.23 = (bf16[1024,8,32]{0,2,1:T(8,128)(2,1)S(1)}, bf16[1024,8,32]{0,2,1:T(8,128)(2,1)}, u32[]{:S(2)}) copy-start(bf16[1024,8,32]{0,2,1:T(8,128)(2,1)} %copy-done.22) | copy-start | bytes 1572868
  577.6 11.0 copy-start.29
  588.6 9.1 copy-start.4
  588.6 11.4 copy-start.11
  588.6 11.4 copy-start.24
  599.8 126.4 %reduce-scatter.10.cloned.1.call-start = ((), (), s32[]{:S(2)}) async-start(), calls=%async_computation.12 | async-start | bytes 589824 | tf_op jit(solution)/shard_map/reduce_scatter | solution.py:221
  600.6 11.7 copy-start.17
  612.3 269.8 %all-reduce.12.cloned.1.call-start = ((), (), s32[]{:S(2)}) async-start(), calls=%async_computation.18 | async-start | bytes 16777216 | tf_op jit(solution)/shard_map/psum | solution.py:157
  612.3 3.5 copy-start.7
  619.2 334.3 %reduce-scatter.14.cloned.1.call-start = ((), (), s32[]{:S(2)}) async-start(), calls=%async_computation.14 | async-start | bytes 2359296 | tf_op jit(solution)/shard_map/reduce_scatter | solution.py:227
  627.6 396.7 %reduce-scatter.8.cloned.1.call-start = ((), (), s32[]{:S(2)}) async-start(), calls=%async_computation.11 | async-start | bytes 2359296 | tf_op jit(solution)/shard_map/reduce_scatter | solution.py:218
  633.6 542.7 %reduce-scatter.20.cloned.1.call-start = ((), (), s32[]{:S(2)}) async-start(), calls=%async_computation.17 | async-start | bytes 9437184 | tf_op jit(solution)/shard_map/reduce_scatter | solution.py:242
  648.0 680.4 %reduce-scatter.18.cloned.1.call-start = ((), (), s32[]{:S(2)}) async-start(), calls=%async_computation.16 | async-start | bytes 9437184 | tf_op jit(solution)/shard_map/reduce_scatter | solution.py:239
  662.1 817.8 %reduce-scatter.16.cloned.1.call-start = ((), (), s32[]{:S(2)}) async-start(), calls=%async_computation.15 | async-start | bytes 9437184 | tf_op jit(solution)/shard_map/reduce_scatter | solution.py:236
  676.6 1.9 copy-start.34
  676.6 205.5 %copy-start.32 = (f32[2048]{0:T(1024)S(1)}, f32[2048]{0:T(1024)}, u32[]{:S(2)}) copy-start(f32[2048]{0:T(1024)} %copy-done.31) | copy-start | bytes 24580
  882.1 144.0 %copy-start.35 = (bf16[2048]{0:T(1024)(128)(2,1)S(1)}, bf16[2048]{0:T(1024)(128)(2,1)}, u32[]{:S(2)}) copy-start(bf16[2048]{0:T(1024)(128)(2,1)} %get-tuple-element.50) | copy-start | bytes 12292
  1043.6 439.1 %copy-start.1 = (bf16[512,2048]{1,0:T(8,128)(2,1)S(1)}, bf16[512,2048]{1,0:T(8,128)(2,1)}, u32[]{:S(2)}) copy-start(bf16[512,2048]{1,0:T(8,128)(2,1)} %param.19) | copy-start | bytes 6291460
  (4 other events, 4.2 us)
Sparse Core Ops, SparseCore 0:
  9.6 35.5 all-gather.2
  105.4 152.8 all-reduce.7
  259.9 34.6 all-gather.4
  343.8 152.9 all-reduce.9
  600.0 61.0 reduce-scatter.11
  665.2 60.9 reduce-scatter.9
  728.8 153.1 all-reduce.11
  886.2 67.3 reduce-scatter.13
  957.7 66.5 reduce-scatter.7
  1027.8 148.5 reduce-scatter.19
  1180.4 147.9 reduce-scatter.17
  1331.9 147.9 reduce-scatter.15
where the time goes:
time: 1500 us; the launch traced here: 1490 us
  waiting for transfers between devices  1070 us (71%)
  matrix products  262 us (17%)
  other arithmetic  110 us (7%)
  blocking collectives  16.8 us (1%)
  between operations  16.5 us (1%)
    psum x1, waiting for transfers between devices, body(): lax.psum(ffn_part.astype(jnp.bfloat16), 'tensor').astype(jnp.float32)  154 us
    psum x1, waiting for transfers between devices, body(): lax.psum(jnp.dot(attn_low, w_out, preferred_element_type=jnp.float32), 't...  152 us
    reduce_scatter x1, waiting for transfers between devices, body(): lax.psum_scatter(grad_up.astype(jnp.bfloat16), 'dp', scatter_dimension=0,...  149 us
    reduce_scatter x1, waiting for transfers between devices, body(): lax.psum_scatter(grad_gate.astype(jnp.bfloat16), 'dp', scatter_dimension=...  149 us
    psum x1, waiting for transfers between devices, body(): d_normed_two = lax.psum(d_norm_part, 'tensor')  139 us
    reduce_scatter x1, waiting for transfers between devices, body(): lax.psum_scatter(grad_down.astype(jnp.bfloat16), 'dp', scatter_dimension=...  127 us
    reduce_scatter x1, waiting for transfers between devices, body(): lax.psum_scatter(grad_wquery.astype(jnp.bfloat16), 'dp', scatter_dimensio...  68.9 us
    reduce_scatter x1, waiting for transfers between devices, body(): lax.psum_scatter(grad_wout.astype(jnp.bfloat16), 'dp', scatter_dimension=...  63.9 us
  transfers between devices with their start and end apart: 12, of which 10 were waited for; matrix products, arithmetic and copies ran while one was open for 11% of the time, Pallas kernels for 0%

commit v1 on v0

v1 whole, which is shorter than its diff:
```python
import functools

import jax
import jax.numpy as jnp
from jax import lax
from jax.experimental import pallas as pl
from jax.experimental.pallas import tpu as pltpu
from jax.sharding import PartitionSpec as P

HEAD_SIZE = 64


EPSILON = 1e-05
MULTIPLIER = 0.015625
RESIDUAL_SCALE = 0.22
THETA_BASE = 10000.0
MASK_VALUE = -1e30
LOW = jnp.bfloat16
WIDE = jnp.float32
LANES = 128
TILE = 256
NN = (((1,), (0,)), ((), ()))
NT = (((1,), (1,)), ((), ()))
TN = (((0,), (0,)), ((), ()))


def dot(a, b, dims=NN):
    return lax.dot_general(a, b, dims, preferred_element_type=WIDE)


def after(value, *others):
    return lax.optimization_barrier((value, *others))[0]


def positions_of(seg_ids):
    length = seg_ids.shape[-1]
    index = jnp.broadcast_to(jnp.arange(length, dtype=jnp.int32), seg_ids.shape)
    before = jnp.concatenate([seg_ids[:, :1] - 1, seg_ids[:, :-1]], axis=1)
    starts = jnp.where(seg_ids != before, index, jnp.zeros_like(index))
    return index - lax.cummax(starts, axis=1)


def rope_tables(positions):
    half = HEAD_SIZE // 2
    freq = THETA_BASE ** (-2.0 * jnp.arange(half, dtype=jnp.float32) / HEAD_SIZE)
    angle = positions.astype(jnp.float32)[:, None] * freq[None, :]
    cosine, sine = jnp.cos(angle), jnp.sin(angle)
    repeats = LANES // HEAD_SIZE
    return (
        jnp.concatenate([cosine, cosine] * repeats, axis=1),
        jnp.concatenate([-sine, sine] * repeats, axis=1),
    )


def lane_index(shape):
    return lax.broadcasted_iota(jnp.int32, shape, len(shape) - 1)


def turn(u, cosine, sine):
    quarter = HEAD_SIZE // 2
    first = lane_index(u.shape) % HEAD_SIZE < quarter
    other = jnp.where(
        first, pltpu.roll(u, u.shape[1] - quarter, 1), pltpu.roll(u, quarter, 1)
    )
    return u * cosine + other * sine


def project_kernel(turned, n_ref, w_ref, cos_ref, sin_ref, out_ref):
    cosine, sine = cos_ref[...], sin_ref[...]
    out = dot(n_ref[...], w_ref[...])
    for j in range(out.shape[1] // LANES):
        part = out[:, j * LANES : (j + 1) * LANES]
        if j * LANES < turned:
            part = turn(part, cosine, sine)
        out_ref[:, j * LANES : (j + 1) * LANES] = part.astype(LOW)


def project(n, weight, cosine, sine, turned):
    rows, width = n.shape
    columns = weight.shape[1]
    moving = lambda i: (i, 0)
    return pl.pallas_call(
        functools.partial(project_kernel, turned),
        grid=(rows // TILE,),
        in_specs=[
            pl.BlockSpec((TILE, width), moving),
            pl.BlockSpec((width, columns), lambda i: (0, 0)),
            pl.BlockSpec((TILE, LANES), moving),
            pl.BlockSpec((TILE, LANES), moving),
        ],
        out_specs=pl.BlockSpec((TILE, columns), moving),
        out_shape=jax.ShapeDtypeStruct((rows, columns), LOW),
        cost_estimate=pl.CostEstimate(
            flops=2 * rows * width * columns,
            bytes_accessed=2 * (rows * width + width * columns + rows * columns),
            transcendentals=0,
        ),
        name="project",
    )(n, weight, cosine, sine)


def doubled(pair, half):
    swapped = pltpu.roll(pair.astype(WIDE), HEAD_SIZE, 1).astype(pair.dtype)
    low = lane_index(pair.shape) < HEAD_SIZE
    return jnp.where(low == (half == 0), pair, swapped)


def attend_kernel(per_kv, q_ref, k_ref, v_ref, segq_ref, segk_ref, o_ref, lse_ref):
    half = (pl.program_id(1) // per_kv) % 2
    length = k_ref.shape[0]
    k, v = doubled(k_ref[...], half), doubled(v_ref[...], half)
    low = lane_index((TILE, LANES)) < HEAD_SIZE
    q_at = lax.broadcasted_iota(jnp.int32, (TILE, TILE), 0)
    k_at = lax.broadcasted_iota(jnp.int32, (TILE, TILE), 1)
    for i in range(length // TILE):
        rows = slice(i * TILE, (i + 1) * TILE)
        reach = (i + 1) * TILE
        q = q_ref[rows, :]
        same = segq_ref[rows, :] == segk_ref[:, :reach]
        last = same[:, i * TILE :] & (k_at <= q_at)
        allowed = jnp.concatenate([same[:, : i * TILE], last], axis=1) if i else last
        outs = []
        for head in range(2):
            mine = jnp.where(low == (head == 0), q, jnp.zeros_like(q))
            raw = dot(mine, k[:reach], NT)
            scores = jnp.where(allowed, MULTIPLIER * raw, MASK_VALUE)
            top = jnp.max(scores, axis=1, keepdims=True)
            e = jnp.exp(scores - top)
            total = jnp.sum(e, axis=1, keepdims=True)
            p = (e * (1.0 / total)).astype(LOW)
            outs.append(dot(p, v[:reach]))
            lse = top + jnp.log(total)
            lse_ref[0, head : head + 1, rows] = jnp.transpose(
                jnp.broadcast_to(lse, (TILE, LANES))
            )[:1]
        o_ref[rows, :] = jnp.where(low, outs[0], outs[1]).astype(LOW)


def attend(qkv, q_width, kv_width, seg_col, seg_row, seqs):
    rows = qkv.shape[0]
    length = rows // seqs
    pairs, kv_pairs = q_width // LANES, kv_width // LANES
    per_kv = pairs // kv_pairs // 2
    return pl.pallas_call(
        functools.partial(attend_kernel, per_kv),
        grid=(seqs, pairs),
        in_specs=[
            pl.BlockSpec((length, LANES), lambda s, h: (s, h)),
            pl.BlockSpec((length, LANES), lambda s, h: (s, pairs + h // (2 * per_kv))),
            pl.BlockSpec((length, LANES), lambda s, h: (s, pairs + kv_pairs + h // (2 * per_kv))),
            pl.BlockSpec((length, 1), lambda s, h: (s, 0)),
            pl.BlockSpec((None, 1, length), lambda s, h: (s, 0, 0)),
        ],
        out_specs=[
            pl.BlockSpec((length, LANES), lambda s, h: (s, h)),
            pl.BlockSpec((1, 2, length), lambda s, h: (h, 0, s)),
        ],
        out_shape=[
            jax.ShapeDtypeStruct((rows, q_width), LOW),
            jax.ShapeDtypeStruct((pairs, 2, rows), WIDE),
        ],
        cost_estimate=pl.CostEstimate(
            flops=4 * rows * length * q_width,
            bytes_accessed=6 * rows * q_width,
            transcendentals=rows * length * pairs * 2,
        ),
        name="attend",
    )(qkv, qkv, qkv, seg_col, seg_row)


def attend_back_kernel(
    per_kv,
    q_ref,
    k_ref,
    v_ref,
    g_ref,
    lse_ref,
    segc_ref,
    segr_ref,
    cos_ref,
    sin_ref,
    dq_ref,
    dk_ref,
    dv_ref,
    dk_acc,
    dv_acc,
    p_buf,
    dp_buf,
):
    pair = pl.program_id(1)
    slot = (pair // per_kv) % 2
    length = k_ref.shape[0]
    k, v = doubled(k_ref[...], slot), doubled(v_ref[...], slot)
    low = lane_index((TILE, LANES)) < HEAD_SIZE
    k_at = lax.broadcasted_iota(jnp.int32, (TILE, TILE), 0)
    q_at = lax.broadcasted_iota(jnp.int32, (TILE, TILE), 1)

    @pl.when(pair % per_kv == 0)
    def _():
        dk_acc[slot] = jnp.zeros_like(dk_acc[slot])
        dv_acc[slot] = jnp.zeros_like(dv_acc[slot])

    for i in range(length // TILE):
        rows = slice(i * TILE, (i + 1) * TILE)
        q, g = q_ref[rows, :], g_ref[rows, :]
        dq = []
        for head in range(2):
            chosen = low == (head == 0)
            qh = jnp.where(chosen, q, jnp.zeros_like(q))
            gh = jnp.where(chosen, g, jnp.zeros_like(g))
            lse = lse_ref[0, head : head + 1, rows]
            inner = jnp.zeros((1, TILE), WIDE)
            for j in range(i + 1):
                keys = slice(j * TILE, (j + 1) * TILE)
                allowed = segc_ref[keys, :] == segr_ref[:, rows]
                if i == j:
                    allowed = allowed & (k_at <= q_at)
                raw = dot(k[keys], qh, NT)
                p = jnp.exp(jnp.where(allowed, MULTIPLIER * raw, MASK_VALUE) - lse)
                dp = dot(v[keys], gh, NT)
                inner = inner + jnp.sum(p * dp, axis=0, keepdims=True)
                p_buf[keys, :] = p
                dp_buf[keys, :] = dp
            total = jnp.zeros((TILE, LANES), WIDE)
            for j in range(i + 1):
                keys = slice(j * TILE, (j + 1) * TILE)
                p = p_buf[keys, :]
                ds = (p * (dp_buf[keys, :] - inner)).astype(LOW)
                dv_acc[slot, keys, :] += dot(p.astype(LOW), gh)
                dk_acc[slot, keys, :] += dot(ds, qh)
                total = total + dot(ds, k[keys], TN)
            dq.append(total)
        dq_ref[rows, :] = turn(
            MULTIPLIER * jnp.where(low, dq[0], dq[1]), cos_ref[rows, :], -sin_ref[rows, :]
        ).astype(LOW)

    @pl.when(pair % (2 * per_kv) == 2 * per_kv - 1)
    def _():
        low_all = lane_index((length, LANES)) < HEAD_SIZE

        def folded(acc):
            a, b = acc[0], acc[1]
            a = a + pltpu.roll(a, HEAD_SIZE, 1)
            b = b + pltpu.roll(b, HEAD_SIZE, 1)
            return jnp.where(low_all, a, b)

        dk_ref[...] = turn(MULTIPLIER * folded(dk_acc), cos_ref[...], -sin_ref[...]).astype(LOW)
        dv_ref[...] = folded(dv_acc).astype(LOW)


def attend_back(qkv, q_width, kv_width, g, lse, seg_col, seg_row, cosine, sine, seqs):
    rows = qkv.shape[0]
    length = rows // seqs
    pairs, kv_pairs = q_width // LANES, kv_width // LANES
    per_kv = pairs // kv_pairs // 2
    by_pair = lambda s, h: (s, h)
    by_kv = lambda s, h: (s, h // (2 * per_kv))
    by_seq = lambda s, h: (s, 0)
    return pl.pallas_call(
        functools.partial(attend_back_kernel, per_kv),
        grid=(seqs, pairs),
        in_specs=[
            pl.BlockSpec((length, LANES), by_pair),
            pl.BlockSpec((length, LANES), lambda s, h: (s, pairs + h // (2 * per_kv))),
            pl.BlockSpec((length, LANES), lambda s, h: (s, pairs + kv_pairs + h // (2 * per_kv))),
            pl.BlockSpec((length, LANES), by_pair),
            pl.BlockSpec((1, 2, length), lambda s, h: (h, 0, s)),
            pl.BlockSpec((length, 1), by_seq),
            pl.BlockSpec((None, 1, length), lambda s, h: (s, 0, 0)),
            pl.BlockSpec((length, LANES), by_seq),
            pl.BlockSpec((length, LANES), by_seq),
        ],
        out_specs=[
            pl.BlockSpec((length, LANES), by_pair),
            pl.BlockSpec((length, LANES), by_kv),
            pl.BlockSpec((length, LANES), by_kv),
        ],
        out_shape=[
            jax.ShapeDtypeStruct((rows, q_width), LOW),
            jax.ShapeDtypeStruct((rows, kv_width), LOW),
            jax.ShapeDtypeStruct((rows, kv_width), LOW),
        ],
        scratch_shapes=[
            pltpu.VMEM((2, length, LANES), WIDE),
            pltpu.VMEM((2, length, LANES), WIDE),
            pltpu.VMEM((length, TILE), WIDE),
            pltpu.VMEM((length, TILE), WIDE),
        ],
        cost_estimate=pl.CostEstimate(
            flops=10 * rows * length * q_width,
            bytes_accessed=10 * rows * q_width,
            transcendentals=rows * length * pairs * 2,
        ),
        name="attend_back",
    )(qkv, qkv, qkv, g, lse, seg_col, seg_row, cosine, sine)


def mix_kernel(n_ref, wg_ref, wu_ref, dm_ref, *refs):
    m_ref, dg_ref, du_ref = refs[-3:]
    n = n_ref[...]
    g = dot(n, wg_ref[...])
    u = dot(n, wu_ref[...])
    dm = dm_ref[...]
    s = jax.nn.sigmoid(g)
    active = g * s
    m_ref[...] = (active * u).astype(LOW)
    dg_ref[...] = (dm * u * s * (1.0 + g * (1.0 - s))).astype(LOW)
    du_ref[...] = (dm * active).astype(LOW)


def mix(n, wg, wu, dm, at, held=()):
    rows, width = n.shape
    units = wg.shape[1]
    moving = lambda i: (0, i)
    spec = pl.BlockSpec((rows, TILE), lambda i: (at, i))
    return pl.pallas_call(
        mix_kernel,
        grid=(units // TILE,),
        in_specs=[
            pl.BlockSpec((rows, width), lambda i: (0, 0)),
            pl.BlockSpec((width, TILE), moving),
            pl.BlockSpec((width, TILE), moving),
            spec,
        ]
        + [pl.BlockSpec(memory_space=pl.ANY)] * len(held),
        out_specs=[spec] * 3,
        out_shape=[jax.ShapeDtypeStruct(dm.shape, LOW)] * 3,
        input_output_aliases={4 + i: i for i in range(len(held))},
        cost_estimate=pl.CostEstimate(
            flops=4 * rows * width * units,
            bytes_accessed=4 * width * units + 2 * rows * width + 10 * rows * units,
            transcendentals=rows * units,
        ),
        name="mix",
    )(n, wg, wu, dm, *held)


def unmix_kernel(dg_ref, du_ref, wg_ref, wu_ref, *out_refs):
    total = dot(dg_ref[...], wg_ref[...], NT) + dot(du_ref[...], wu_ref[...], NT)
    share = out_refs[0].shape[0]
    for i, ref in enumerate(out_refs):
        ref[...] = total[i * share : (i + 1) * share].astype(LOW)


def unmix(dg, du, wg, wu, at, share, pieces):
    units, width = dg.shape[1], wg.shape[0]
    rows = share * pieces
    held = pl.BlockSpec((rows, units), lambda i: (at, 0))
    moving = pl.BlockSpec((TILE, units), lambda i: (i, 0))
    return pl.pallas_call(
        unmix_kernel,
        grid=(width // TILE,),
        in_specs=[held, held, moving, moving],
        out_specs=[pl.BlockSpec((share, TILE), lambda i: (0, i))] * pieces,
        out_shape=[jax.ShapeDtypeStruct((share, width), LOW)] * pieces,
        cost_estimate=pl.CostEstimate(
            flops=4 * rows * width * units,
            bytes_accessed=4 * width * units + 4 * rows * units + 2 * rows * width,
            transcendentals=0,
        ),
        name="unmix",
    )(dg, du, wg, wu)


def swap(array, axis, mask):
    size = lax.axis_size(axis)
    return lax.ppermute(array, axis, [(i, i ^ mask) for i in range(size)])


def powers(size):
    return [1 << i for i in range(size.bit_length() - 1)]


def spread_masks(size):
    masks, bit = [1], 2
    while bit < size:
        masks.append(bit)
        if 2 * bit < size:
            masks.append(3 * bit)
        bit *= 4
    return masks


def gather_shares(own):
    shares = {0: own}
    for mask in reversed(powers(lax.axis_size("tensor"))):
        shares.update({r ^ mask: swap(a, "tensor", mask) for r, a in shares.items()})
    return [shares[r] for r in range(len(shares))]


def sum_shares(parts):
    parts = dict(enumerate(parts))
    for mask in powers(lax.axis_size("tensor")):
        sent = {r: a for r, a in parts.items() if r & mask}
        parts = {r: a for r, a in parts.items() if not r & mask}
        for r, a in reversed(sent.items()):
            got = swap(a.astype(LOW), "tensor", mask).astype(WIDE)
            parts[r ^ mask] = parts[r ^ mask].astype(WIDE) + got
    return parts[0]


def in_order(shares, rank):
    share = shares[0].shape[0]
    whole = jnp.zeros((share * len(shares),) + shares[0].shape[1:], shares[0].dtype)
    for r, a in enumerate(shares):
        whole = lax.dynamic_update_slice_in_dim(whole, a, (rank ^ r) * share, 0)
    return whole


def out_of_order(whole, rank):
    count = lax.axis_size("tensor")
    share = whole.shape[0] // count
    return [lax.dynamic_slice_in_dim(whole, (rank ^ r) * share, share, 0) for r in range(count)]


def block_order(masks):
    order = [0]
    for mask in reversed(masks):
        order = [mask ^ b for b in order] + order
    return order


def permute_columns(array, masks, place):
    count = 1 << len(masks)
    width = array.shape[1] // count
    return jnp.concatenate(
        [
            lax.dynamic_slice_in_dim(array, (place ^ b) * width, width, 1)
            for b in block_order(masks)
        ],
        axis=1,
    )


class Reduction:
    def __init__(self, term, masks, width, axis):
        self.term, self.masks, self.width, self.axis = term, list(masks), width, axis
        self.count = 1 << len(masks)
        self.low, self.size, self.got = 0, self.count // 2, []
        self.sent = None

    def total(self, low, high):
        value = self.term(low, high)
        for first, array in self.got:
            piece = lax.slice_in_dim(
                array, (low - first) * self.width, (high - first) * self.width, axis=self.axis
            )
            value = value + piece.astype(WIDE)
        return value

    def step(self):
        self.sent = self.total(self.low, self.low + self.size).astype(LOW)
        self.low += self.size
        self.size //= 2
        self.got.append((self.low, swap(self.sent, "dp", self.masks.pop(0))))
        return self

    def finish(self):
        while self.masks:
            self.step()
        return self.total(self.low, self.count)


def reduce_rows(left, right, masks):
    width = left.shape[1] // (1 << len(masks))
    term = lambda low, high: dot(left[:, low * width : high * width], right, TN)
    return Reduction(term, masks, width, 0)


def reduce_cols(left, right, masks):
    width = right.shape[1] // (1 << len(masks))
    term = lambda low, high: dot(left, right[:, low * width : high * width], TN)
    return Reduction(term, masks, width, 1)


def rotate(masks, by):
    by %= len(masks)
    return masks[by:] + masks[:by]


def rows_of(shares):
    return jnp.concatenate(shares, axis=0)


def inverse_rms(value_rows):
    return lax.rsqrt(jnp.mean(value_rows * value_rows, axis=-1, keepdims=True) + EPSILON)


def norm_back(d_normed, value_rows, inverse, gain):
    scaled = d_normed * gain
    return inverse * scaled - value_rows * inverse**3 * jnp.mean(
        scaled * value_rows, axis=-1, keepdims=True
    )


def body(
    layer_in,
    cotangent,
    segments,
    gain_attn,
    w_query,
    key_weight,
    value_weight,
    w_out,
    gain_ffn,
    w_gate,
    w_up,
    w_down,
):
    share, width = layer_in.shape
    count = lax.axis_size("tensor")
    half = count // 2
    rank = lax.axis_index("tensor")
    place = lax.axis_index("dp")
    masks = spread_masks(lax.axis_size("dp"))
    order_a = order_b = masks
    order_c = masks[1:2] + masks[:1] + masks[2:]
    seqs = segments.shape[0]
    q_width, kv_width = w_query.shape[1], key_weight.shape[1]

    gain_one = gain_attn.astype(WIDE)
    gain_two = gain_ffn.astype(WIDE)
    x = layer_in.astype(WIDE)
    inverse_one = inverse_rms(x)
    n1_shares = gather_shares((x * inverse_one * gain_one).astype(LOW))
    d_out = cotangent.astype(WIDE)
    branch_own = after((RESIDUAL_SCALE * d_out).astype(LOW), n1_shares[half])
    branch_shares = gather_shares(branch_own)

    w_qkv = jnp.concatenate([w_query, key_weight, value_weight], axis=1)
    cosine, sine = rope_tables(positions_of(segments).reshape(-1))
    seg_col, seg_row = segments.reshape(-1, 1), segments[:, None, :]
    cos_parts, sin_parts = out_of_order(cosine, rank), out_of_order(sine, rank)
    turned = q_width + kv_width
    qkv_shares = []
    for low in (0, half):
        part = slice(low, low + half)
        out = project(
            rows_of(n1_shares[part]), w_qkv, rows_of(cos_parts[part]), rows_of(sin_parts[part]), turned
        )
        qkv_shares += [out[i * share : (i + 1) * share] for i in range(half)]
    qkv = in_order(qkv_shares, rank)
    attended, lse = attend(qkv, q_width, kv_width, seg_col, seg_row, seqs)
    attn_shares = out_of_order(attended, rank)
    attn_parts = [dot(a, w_out).astype(LOW) for a in attn_shares]
    attn_total = sum_shares(attn_parts)

    d_branch = after(rows_of(branch_shares), *attn_parts)
    d_mixed = dot(d_branch, w_down, NT)
    hidden = x + RESIDUAL_SCALE * attn_total
    inverse_two = inverse_rms(hidden)
    n2_shares = gather_shares((hidden * inverse_two * gain_two).astype(LOW))
    held = mix(rows_of(n2_shares[:half]), w_gate, w_up, d_mixed, 0)
    mixed, d_gate, d_upper = mix(rows_of(n2_shares[half:]), w_gate, w_up, d_mixed, 1, held)

    n2 = rows_of(n2_shares)
    grad_down = reduce_cols(mixed, permute_columns(d_branch, order_a, place), order_a).step()
    grad_gate = reduce_rows(permute_columns(n2, order_b, place), d_gate, order_b).step()
    grad_up = reduce_rows(permute_columns(n2, order_c, place), d_upper, order_c).step()
    d_gate_late = after(d_gate, grad_down.sent, grad_gate.sent, grad_up.sent)
    far = unmix(d_gate_late, d_upper, w_gate, w_up, 1, share, half)
    near = unmix(after(d_gate_late, *far), d_upper, w_gate, w_up, 0, share, half)
    d_normed = sum_shares(list(near) + list(far))
    gain_two_part = jnp.sum(d_normed * hidden * inverse_two, axis=0)
    d_hidden = d_out + norm_back(d_normed, hidden, inverse_two, gain_two)
    da_shares = gather_shares((RESIDUAL_SCALE * d_hidden).astype(LOW))

    ffn_part = dot(after(mixed, *near), w_down).astype(LOW)
    ffn_part = after(ffn_part, da_shares[half])
    ffn_total = sum_shares([ffn_part[r * share : (r + 1) * share] for r in range(count)])
    out_rows = (hidden + RESIDUAL_SCALE * ffn_total).astype(LOW)

    d_attn = in_order([dot(a, w_out, NT).astype(LOW) for a in da_shares], rank)
    d_query, d_keys, d_values = attend_back(
        qkv, q_width, kv_width, d_attn, lse, seg_col, seg_row, cosine, sine, seqs
    )
    grad_wout = reduce_cols(
        rows_of(attn_shares), permute_columns(rows_of(da_shares), order_a, place), order_a
    ).step()
    n1 = rows_of(n1_shares)
    d_qkv_shares = [
        jnp.concatenate(parts, axis=1)
        for parts in zip(*(out_of_order(a, rank) for a in (d_query, d_keys, d_values)))
    ]
    d_qkv = rows_of(d_qkv_shares)
    grad_q = reduce_rows(permute_columns(n1, order_b, place), d_qkv[:, :q_width], order_b).step()
    grad_kv = reduce_rows(permute_columns(n1, order_c, place), d_qkv[:, q_width:], order_c).step()
    d_qkv_late = [after(a, grad_q.sent, grad_kv.sent) for a in d_qkv_shares]
    d_norm_parts = [dot(a, w_qkv, NT).astype(LOW) for a in d_qkv_late]
    d_normed_one = sum_shares(d_norm_parts)
    grad_rows = (d_hidden + norm_back(d_normed_one, x, inverse_one, gain_one)).astype(LOW)

    gain_one_part = sum(
        jnp.sum(d.astype(WIDE) * n.astype(WIDE), axis=0)
        for d, n in zip(d_norm_parts, [after(n, *d_norm_parts) for n in n1_shares])
    )
    gains = jnp.stack([gain_one_part / gain_one, gain_two_part])
    block = width // lax.axis_size("dp")
    gains = permute_columns(gains, masks, place)
    for mask in powers(count):
        gains = gains + swap(gains, "tensor", mask)
    gains = Reduction(
        lambda low, high: gains[:, low * block : high * block], masks, block, 1
    ).finish()
    grad_kv = grad_kv.finish()
    return (
        out_rows,
        grad_rows,
        gains[0],
        grad_q.finish(),
        grad_kv[:, :kv_width],
        grad_kv[:, kv_width:],
        grad_wout.finish(),
        gains[1],
        grad_gate.finish(),
        grad_up.finish(),
        grad_down.finish(),
    )


def solution(mesh):
    return jax.shard_map(
        body,
        mesh=mesh,
        in_specs=(
            P(("dp", "tensor"), None),
            P(("dp", "tensor"), None),
            P("dp", None),
            P(),
            P(None, "tensor"),
            P(None, "tensor"),
            P(None, "tensor"),
            P("tensor", None),
            P(),
            P(None, "tensor"),
            P(None, "tensor"),
            P("tensor", None),
        ),
        out_specs=(
            P(("dp", "tensor"), None),
            P(("dp", "tensor"), None),
            P("dp"),
            P("dp", "tensor"),
            P("dp", "tensor"),
            P("dp", "tensor"),
            P("tensor", "dp"),
            P("dp"),
            P("dp", "tensor"),
            P("dp", "tensor"),
            P("tensor", "dp"),
        ),
        check_vma=False,
    )
```

time: 1500 us -> 736 us (0.49)
  waiting for transfers between devices: 1070 us -> 345 us
  matrix products: 262 us -> 122 us
  Pallas kernels: 0 us -> 123 us
  other arithmetic: 110 us -> 67.1 us
  starting transfers between devices: 1.13 us -> 33.6 us
  local copies, waits for them, and re-layouts: 10.6 us -> 31.9 us
  blocking collectives: 16.8 us -> 0 us
    reduce_scatter x7 -> x0, waiting for transfers between devices: 597 us -> none  [the longest x1 149 us: body(): lax.psum_scatter(grad_up.astype(jnp.bfloat16), 'dp', scatter_dimension=0,...]
    psum x3 -> x0, waiting for transfers between devices: 446 us -> none  [the longest x1 154 us: body(): lax.psum(ffn_part.astype(jnp.bfloat16), 'tensor').astype(jnp.float32)]
    ppermute x0 -> x47, waiting for transfers between devices: none -> 345 us  [swap(): return lax.ppermute(array, axis, [(i, i ^ mask) for i in range(size)])]
    dot_general x27 -> x38, matrix products: 262 us -> 122 us  [dot(): return lax.dot_general(a, b, dims, preferred_element_type=WIDE)]
    pallas_call x0 -> x8, Pallas kernels: none -> 123 us  [the longest x2 34.8 us: mix(): pl.pallas_call(mix_kernel, grid=(units // TILE,), in_specs=[pl.BlockSpec(...]
    convert_element_type x15 -> x12, other arithmetic: 61 us -> 17.6 us  [the longest x2 4.51 us: sum_shares(): got = swap(a.astype(LOW), 'tensor', mask).astype(WIDE)]
    ppermute x0 -> x47, starting transfers between devices: none -> 33.6 us  [swap(): return lax.ppermute(array, axis, [(i, i ^ mask) for i in range(size)])]
    concatenate x2 -> x20, other arithmetic: 0.12 us -> 31.9 us  [the longest x13 28.3 us: rows_of(): return jnp.concatenate(shares, axis=0)]
  transfers between devices with their start and end apart: 12 -> 47, of which waited for: 10 -> 20; matrix products, arithmetic and copies ran while one was open for 11% -> 24% of each run, Pallas kernels for 0% -> 12%
where the time goes in v1:
time: 736 us; the launch traced here: 725 us
  waiting for transfers between devices  345 us (47%)
  Pallas kernels  123 us (17%)
  matrix products  122 us (17%)
  other arithmetic  67.1 us (9%)
  starting transfers between devices  33.6 us (5%)
  local copies, waits for them, and re-layouts  31.9 us (4%)
    ppermute x47, waiting for transfers between devices, swap(): return lax.ppermute(array, axis, [(i, i ^ mask) for i in range(size)])  345 us
    dot_general x38, matrix products, dot(): return lax.dot_general(a, b, dims, preferred_element_type=WIDE)  122 us
    pallas_call x2, Pallas kernels, mix(): pl.pallas_call(mix_kernel, grid=(units // TILE,), in_specs=[pl.BlockSpec(...  34.8 us
    ppermute x47, starting transfers between devices, swap(): return lax.ppermute(array, axis, [(i, i ^ mask) for i in range(size)])  33.6 us
    pallas_call x2, Pallas kernels, unmix(): pl.pallas_call(unmix_kernel, grid=(width // TILE,), in_specs=[held, held,...  30 us
    concatenate x13, other arithmetic, rows_of(): return jnp.concatenate(shares, axis=0)  28.3 us
    pallas_call x1, Pallas kernels, attend_back(): pl.pallas_call(functools.partial(attend_back_kernel, per_kv), grid=(seqs,...  26.8 us
    pallas_call x1, Pallas kernels, attend(): pl.pallas_call(functools.partial(attend_kernel, per_kv), grid=(seqs, pair...  20 us
  transfers between devices with their start and end apart: 47, of which 20 were waited for; matrix products, arithmetic and copies ran while one was open for 24% of the time, Pallas kernels for 12%

profile of v1, /device:TPU:16, one launch (start us, length us, event | category | flops | bytes accessed | tf_op | source)
XLA Modules:
  0.0 724.9 jit_solution(687542052796434812)
XLA Ops:
  8.8 3.1 fusion.139
  22.2 8.7 %collective-permute-done.1 = bf16[256,2048]{1,0:T(8,128)(2,1)} collective-permute-done((bf16[256,2048]{1,0:T(8,128)(2,1)S(1)}, bf16[256,2048]{1,0:T(8,128)(2,1)}, u32[]{:S(2)}, u32[]{:S(2)}) %collective-permute-start.1) | collective-permute-done | bytes 1048608 | tf_op jit(solution)/shard_map/ppermute | solution.py:367
  37.7 5.5 project.2
  45.7 3.1 pad_maximum_fusion.5.n_ref
  48.8 5.5 project.3
  57.8 20.0 %attend.1 = (bf16[1024,512]{1,0:T(8,128)(2,1)}, f32[4,2,1024]{2,1,0:T(2,128)}) custom-call(bf16[1024,768]{1,0:T(8,128)(2,1)} %slice_dynamic-update-slice_fusion.q_ref.k_ref.v_ref, bf16[1024,768]{1,0:T(8,128)(2,1)} %slice_dynamic-update-slice_fusion.q_ref.k_ref.v_ref, bf16[1024,768]{1,0:T(8,128)(2,1)} %slice_dynamic-update-slice_fusion.q_ref.k_ref.v_ref, ...), custom_call_target="tpu_custom_call" | custom-call | flops 2147483648 | bytes 3145728 | tf_op jit(solution)/shard_map/attend/pallas_call | solution.py:144
  90.5 19.6 %collective-permute-done.5 = bf16[256,2048]{1,0:T(8,128)(2,1)} collective-permute-done((bf16[256,2048]{1,0:T(8,128)(2,1)}, bf16[256,2048]{1,0:T(8,128)(2,1)}, u32[]{:S(2)}, u32[]{:S(2)}) %collective-permute-start.5) | collective-permute-done | bytes 1048608 | tf_op jit(solution)/shard_map/ppermute | solution.py:367
  114.6 11.0 %fusion.182.dm_ref = f32[1024,2048]{1,0:T(8,128)} fusion(bf16[1024,2048]{1,0:T(8,128)(2,1)S(1)} %pad_maximum_fusion, bf16[2048,2048]{1,0:T(8,128)(2,1)S(1)} %bitcast.88), kind=kOutput, calls=%fused_computation.338 | convolution fusion | flops 8589934592 | bytes 20971520 | tf_op jit(solution)/shard_map/dot_general | solution.py:28
  125.7 14.1 %collective-permute-done.6 = bf16[256,2048]{1,0:T(8,128)(2,1)} collective-permute-done((bf16[256,2048]{1,0:T(8,128)(2,1)S(1)}, bf16[256,2048]{1,0:T(8,128)(2,1)}, u32[]{:S(2)}, u32[]{:S(2)}) %collective-permute-start.6) | collective-permute-done | bytes 1048608 | tf_op jit(solution)/shard_map/ppermute | solution.py:367
  142.2 17.2 %mix.2 = (bf16[1024,2048]{1,0:T(8,128)(2,1)}, bf16[1024,2048]{1,0:T(8,128)(2,1)}, bf16[1024,2048]{1,0:T(8,128)(2,1)}) custom-call(bf16[512,2048]{1,0:T(8,128)(2,1)} %pad_maximum_fusion.7.n_ref, bf16[2048,2048]{1,0:T(8,128)(2,1)} %wg_ref.7, bf16[2048,2048]{1,0:T(8,128)(2,1)} %wu_ref.7, f32[1024,2048]{1,0:T(8,128)} %fusion.182.dm_ref), custom_call_target="tpu_custom_call" | custom-call | flops 8589934592 | bytes 29360128 | tf_op jit(solution)/shard_map/mix/pallas_call | solution.py:316
  164.8 3.1 pad_maximum_fusion.6.n_ref
  167.9 17.6 %mix.3 = (bf16[1024,2048]{1,0:T(8,128)(2,1)}, bf16[1024,2048]{1,0:T(8,128)(2,1)}, bf16[1024,2048]{1,0:T(8,128)(2,1)}) custom-call(bf16[512,2048]{1,0:T(8,128)(2,1)} %pad_maximum_fusion.6.n_ref, bf16[2048,2048]{1,0:T(8,128)(2,1)} %wg_ref.7, bf16[2048,2048]{1,0:T(8,128)(2,1)} %wu_ref.7, ...), custom_call_target="tpu_custom_call", output_to_operand_aliasing={{0}: (4, {}), {1}: (5, {}), {2}: (6, {})} | custom-call | flops 8589934592 | bytes 29360128 | tf_op jit(solution)/shard_map/mix/pallas_call | solution.py:316
  185.5 9.6 %convolution_convert_fusion.1 = bf16[1024,2048]{1,0:T(8,128)(2,1)} fusion(bf16[1024,2048]{1,0:T(8,128)(2,1)} %get-tuple-element.48.du_ref, bf16[1024,256]{1,0:T(8,128)(2,1)} %get-tuple-element.98, bf16[1024,256]{1,0:T(8,128)(2,1)} %get-tuple-element.97, bf16[1024,256]{1,0:T(8,128)(2,1)} %get-tuple-element.101, bf16[1024,256]{1,0:T(8,128)(2,1)} %get-tuple-element.102), kind=kOutput, calls=%fused_computation.13 | convolution fusion | flops 4305453056 | bytes 10485760 | tf_op jit(solution)/shard_map/dot_general | solution.py:28
  195.2 6.7 convolution_convert_fusion.2
  201.9 6.6 convolution_convert_fusion.3
  208.5 14.9 %unmix.2 = (bf16[256,2048]{1,0:T(8,128)(2,1)}, bf16[256,2048]{1,0:T(8,128)(2,1)}) custom-call(bf16[1024,2048]{1,0:T(8,128)(2,1)} %get-tuple-element.52.dg_ref, bf16[1024,2048]{1,0:T(8,128)(2,1)} %get-tuple-element.48.du_ref, bf16[2048,2048]{1,0:T(8,128)(2,1)} %wg_ref.7, bf16[2048,2048]{1,0:T(8,128)(2,1)} %wu_ref.7), custom_call_target="tpu_custom_call" | custom-call | flops 8589934592 | bytes 23068672 | tf_op jit(solution)/shard_map/unmix/pallas_call | solution.py:350
  224.0 15.0 %unmix.3 = (bf16[256,2048]{1,0:T(8,128)(2,1)}, bf16[256,2048]{1,0:T(8,128)(2,1)}) custom-call(bf16[1024,2048]{1,0:T(8,128)(2,1)} %get-tuple-element.52.dg_ref, bf16[1024,2048]{1,0:T(8,128)(2,1)} %get-tuple-element.48.du_ref, bf16[2048,2048]{1,0:T(8,128)(2,1)} %wg_ref.7, bf16[2048,2048]{1,0:T(8,128)(2,1)} %wu_ref.7), custom_call_target="tpu_custom_call" | custom-call | flops 8589934592 | bytes 23068672 | tf_op jit(solution)/shard_map/unmix/pallas_call | solution.py:350
  239.0 2.9 add_convert_fusion.5
  251.9 15.9 %collective-permute-done.14 = bf16[256,2048]{1,0:T(8,128)(2,1)} collective-permute-done((bf16[256,2048]{1,0:T(8,128)(2,1)}, bf16[256,2048]{1,0:T(8,128)(2,1)}, u32[]{:S(2)}, u32[]{:S(2)}) %collective-permute-start.14) | collective-permute-done | bytes 1048608 | tf_op jit(solution)/shard_map/ppermute | solution.py:367
  270.3 4.2 multiply_convert_fusion
  275.0 9.1 %convolution_convert_fusion = bf16[1024,2048]{1,0:T(8,128)(2,1)S(1)} fusion(bf16[1024,2048]{1,0:T(8,128)(2,1)S(1)} %copy-done.17, bf16[2048,2048]{1,0:T(8,128)(2,1)S(1)} %bitcast.90), kind=kOutput, calls=%fused_computation.12 | convolution fusion | flops 8592031744 | bytes 16777216 | tf_op jit(solution)/shard_map/dot_general | solution.py:28
  286.7 12.6 %collective-permute-done.15 = bf16[256,2048]{1,0:T(8,128)(2,1)S(1)} collective-permute-done((bf16[256,2048]{1,0:T(8,128)(2,1)S(1)}, bf16[256,2048]{1,0:T(8,128)(2,1)S(1)}, u32[]{:S(2)}, u32[]{:S(2)}) %collective-permute-start.15) | collective-permute-done | bytes 1048608 | tf_op jit(solution)/shard_map/ppermute | solution.py:367
  306.6 26.8 %attend_back.1 = (bf16[1024,512]{1,0:T(8,128)(2,1)}, bf16[1024,128]{1,0:T(8,128)(2,1)}, bf16[1024,128]{1,0:T(8,128)(2,1)}) custom-call(bf16[1024,768]{1,0:T(8,128)(2,1)} %slice_dynamic-update-slice_fusion.q_ref.k_ref.v_ref, bf16[1024,768]{1,0:T(8,128)(2,1)} %slice_dynamic-update-slice_fusion.q_ref.k_ref.v_ref, ...), custom_call_target="tpu_custom_call" | custom-call | flops 5368709120 | bytes 5242880 | tf_op jit(solution)/shard_map/attend_back/pallas_call | solution.py:259
  334.9 6.4 maximum_maximum_fusion
  344.9 2.9 convolution_convert_fusion.8
  347.8 2.9 convolution_convert_fusion.10
  350.8 3.0 convolution_convert_fusion.11
  354.9 2.9 convolution_convert_fusion.9
  369.6 5.5 add_convert_fusion
  375.1 3.6 collective-permute-done.32
  380.9 6.0 add_convert_fusion.1
  386.9 72.3 %collective-permute-done.33 = bf16[512,256]{1,0:T(8,128)(2,1)S(1)} collective-permute-done((bf16[512,256]{1,0:T(8,128)(2,1)S(1)}, bf16[512,256]{1,0:T(8,128)(2,1)S(1)}, u32[]{:S(2)}, u32[]{:S(2)}) %collective-permute-start.33) | collective-permute-done | bytes 262176 | tf_op jit(solution)/shard_map/ppermute | solution.py:367
  461.6 5.3 add_convert_fusion.2
  474.9 8.8 %collective-permute-done.18 = bf16[256,2048]{1,0:T(8,128)(2,1)} collective-permute-done((bf16[256,2048]{1,0:T(8,128)(2,1)S(1)}, bf16[256,2048]{1,0:T(8,128)(2,1)}, u32[]{:S(2)}, u32[]{:S(2)}) %collective-permute-start.18) | collective-permute-done | bytes 1048608 | tf_op jit(solution)/shard_map/ppermute | solution.py:367
  485.2 3.3 add_convert_fusion.3
  488.5 6.8 collective-permute-done.35
  501.3 32.9 %collective-permute-done.30 = bf16[512,512]{1,0:T(8,128)(2,1)S(1)} collective-permute-done((bf16[512,512]{1,0:T(8,128)(2,1)}, bf16[512,512]{1,0:T(8,128)(2,1)S(1)}, u32[]{:S(2)}, u32[]{:S(2)}) %collective-permute-start.30) | collective-permute-done | bytes 524320 | tf_op jit(solution)/shard_map/ppermute | solution.py:367
  536.2 8.7 %collective-permute-done.36 = bf16[512,512]{1,0:T(8,128)(2,1)S(1)} collective-permute-done((bf16[512,512]{1,0:T(8,128)(2,1)S(1)}, bf16[512,512]{1,0:T(8,128)(2,1)S(1)}, u32[]{:S(2)}, u32[]{:S(2)}) %collective-permute-start.36) | collective-permute-done | bytes 524320 | tf_op jit(solution)/shard_map/ppermute | solution.py:367
  546.7 17.2 %collective-permute-done.31 = bf16[256,512]{1,0:T(8,128)(2,1)S(1)} collective-permute-done((bf16[256,512]{1,0:T(8,128)(2,1)S(1)}, bf16[256,512]{1,0:T(8,128)(2,1)S(1)}, u32[]{:S(2)}, u32[]{:S(2)}) %collective-permute-start.31) | collective-permute-done | bytes 262176 | tf_op jit(solution)/shard_map/ppermute | solution.py:367
  566.7 4.4 collective-permute-done.37
  580.7 3.4 fusion.9
  584.5 3.0 collective-permute-start.27
  592.0 50.4 %collective-permute-done.27 = bf16[2,512]{1,0:T(2,128)(2,1)S(1)} collective-permute-done((bf16[2,512]{1,0:T(2,128)(2,1)S(1)}, bf16[2,512]{1,0:T(2,128)(2,1)S(1)}, u32[]{:S(2)}, u32[]{:S(2)}) %collective-permute-start.27) | collective-permute-done | bytes 2080 | tf_op jit(solution)/shard_map/ppermute | solution.py:367
  647.2 53.1 %collective-permute-done.28 = bf16[2,256]{1,0:T(2,128)(2,1)S(1)} collective-permute-done((bf16[2,256]{1,0:T(2,128)(2,1)S(1)}, bf16[2,256]{1,0:T(2,128)(2,1)S(1)}, u32[]{:S(2)}, u32[]{:S(2)}) %collective-permute-start.28) | collective-permute-done | bytes 1056 | tf_op jit(solution)/shard_map/ppermute | solution.py:367
  700.9 4.0 fusion.4
  704.9 4.8 fusion.7
  709.8 10.8 %collective-permute-done.40 = bf16[256,2048]{1,0:T(8,128)(2,1)S(1)} collective-permute-done((bf16[256,2048]{1,0:T(8,128)(2,1)S(1)}, bf16[256,2048]{1,0:T(8,128)(2,1)S(1)}, u32[]{:S(2)}, u32[]{:S(2)}) %collective-permute-start.40) | collective-permute-done | bytes 1048608 | tf_op jit(solution)/shard_map/ppermute | solution.py:367
  720.6 4.0 fusion.1
  (358 shorter events, 142.9 us)
Async XLA Ops:
  5.2 29.8 %collective-permute-start = (bf16[256,2048]{1,0:T(8,128)(2,1)S(1)}, bf16[256,2048]{1,0:T(8,128)(2,1)}, u32[]{:S(2)}, u32[]{:S(2)}) collective-permute-start(bf16[256,2048]{1,0:T(8,128)(2,1)S(1)} %fusion.20), channel_id=1, source_target_pairs={{0,1},{1,0},{2,3},{3,2},{4,5},{5,4},{6,7},{7,6},{8,9},{9,8},{10,11... | collective-permute-start | bytes 3145736 | tf_op jit(solution)/shard_map/ppermute | solution.py:367
  5.2 25.7 %collective-permute-start.1 = (bf16[256,2048]{1,0:T(8,128)(2,1)S(1)}, bf16[256,2048]{1,0:T(8,128)(2,1)}, u32[]{:S(2)}, u32[]{:S(2)}) collective-permute-start(bf16[256,2048]{1,0:T(8,128)(2,1)S(1)} %fusion.20), channel_id=1, source_target_pairs={{0,2},{1,3},{2,0},{3,1},{4,6},{5,7},{6,4},{7,5},{8,10},{9,11},{10,... | collective-permute-start | bytes 3145736 | tf_op jit(solution)/shard_map/ppermute | solution.py:367
  30.9 14.8 %collective-permute-start.2 = (bf16[256,2048]{1,0:T(8,128)(2,1)}, bf16[256,2048]{1,0:T(8,128)(2,1)}, u32[]{:S(2)}, u32[]{:S(2)}) collective-permute-start(bf16[256,2048]{1,0:T(8,128)(2,1)} %collective-permute-done.1), channel_id=1, source_target_pairs={{0,1},{1,0},{2,3},{3,2},{4,5},{5,4},{6,7},{7,6},{8,9},{9,8},{10,11... | collective-permute-start | bytes 3145736 | tf_op jit(solution)/shard_map/ppermute | solution.py:367
  33.4 47.0 %collective-permute-start.9 = (bf16[256,2048]{1,0:T(8,128)(2,1)}, bf16[256,2048]{1,0:T(8,128)(2,1)}, u32[]{:S(2)}, u32[]{:S(2)}) collective-permute-start(bf16[256,2048]{1,0:T(8,128)(2,1)} %fusion.12), channel_id=1, source_target_pairs={{0,2},{1,3},{2,0},{3,1},{4,6},{5,7},{6,4},{7,5},{8,10},{9,11},{10,... | collective-permute-start | bytes 3145736 | tf_op jit(solution)/shard_map/ppermute | solution.py:367
  79.9 2.8 collective-permute-start.4
  80.2 5.5 collective-permute-start.8
  80.5 5.5 collective-permute-start.10
  82.4 8.1 %collective-permute-start.3 = (bf16[256,2048]{1,0:T(8,128)(2,1)}, bf16[256,2048]{1,0:T(8,128)(2,1)}, u32[]{:S(2)}, u32[]{:S(2)}) collective-permute-start(bf16[256,2048]{1,0:T(8,128)(2,1)} %convolution_convert_fusion.6), channel_id=1, source_target_pairs={{0,1},{1,0},{2,3},{3,2},{4,5},{5,4},{6,7},{7,6},{8,9},{9,8},{10,11... | collective-permute-start | bytes 3145736 | tf_op jit(solution)/shard_map/ppermute | solution.py:367
  84.4 25.6 %collective-permute-start.5 = (bf16[256,2048]{1,0:T(8,128)(2,1)}, bf16[256,2048]{1,0:T(8,128)(2,1)}, u32[]{:S(2)}, u32[]{:S(2)}) collective-permute-start(bf16[256,2048]{1,0:T(8,128)(2,1)} %add_convert_fusion.6), channel_id=1, source_target_pairs={{0,2},{1,3},{2,0},{3,1},{4,6},{5,7},{6,4},{7,5},{8,10},{9,11},{10,... | collective-permute-start | bytes 3145736 | tf_op jit(solution)/shard_map/ppermute | solution.py:367
  114.0 25.8 %collective-permute-start.11 = (bf16[256,2048]{1,0:T(8,128)(2,1)S(1)}, bf16[256,2048]{1,0:T(8,128)(2,1)S(1)}, u32[]{:S(2)}, u32[]{:S(2)}) collective-permute-start(bf16[256,2048]{1,0:T(8,128)(2,1)S(1)} %multiply_convert_fusion.1), channel_id=1, source_target_pairs={{0,1},{1,0},{2,3},{3,2},{4,5},{5,4},{6,7},{7,6},{8,9},{9,8},{10,11... | collective-permute-start | bytes 3145736 | tf_op jit(solution)/shard_map/ppermute | solution.py:367
  114.1 25.7 %collective-permute-start.6 = (bf16[256,2048]{1,0:T(8,128)(2,1)S(1)}, bf16[256,2048]{1,0:T(8,128)(2,1)}, u32[]{:S(2)}, u32[]{:S(2)}) collective-permute-start(bf16[256,2048]{1,0:T(8,128)(2,1)S(1)} %multiply_convert_fusion.1), channel_id=1, source_target_pairs={{0,2},{1,3},{2,0},{3,1},{4,6},{5,7},{6,4},{7,5},{8,10},{9,11},{10,... | collective-permute-start | bytes 3145736 | tf_op jit(solution)/shard_map/ppermute | solution.py:367
  139.8 19.7 %collective-permute-start.7 = (bf16[256,2048]{1,0:T(8,128)(2,1)}, bf16[256,2048]{1,0:T(8,128)(2,1)}, u32[]{:S(2)}, u32[]{:S(2)}) collective-permute-start(bf16[256,2048]{1,0:T(8,128)(2,1)} %collective-permute-done.6), channel_id=1, source_target_pairs={{0,1},{1,0},{2,3},{3,2},{4,5},{5,4},{6,7},{7,6},{8,9},{9,8},{10,11... | collective-permute-start | bytes 3145736 | tf_op jit(solution)/shard_map/ppermute | solution.py:367
  223.5 15.5 %collective-permute-start.13 = (bf16[256,2048]{1,0:T(8,128)(2,1)}, bf16[256,2048]{1,0:T(8,128)(2,1)}, u32[]{:S(2)}, u32[]{:S(2)}) collective-permute-start(bf16[256,2048]{1,0:T(8,128)(2,1)} %get-tuple-element.51), channel_id=1, source_target_pairs={{0,1},{1,0},{2,3},{3,2},{4,5},{5,4},{6,7},{7,6},{8,9},{9,8},{10,11... | collective-permute-start | bytes 3145736 | tf_op jit(solution)/shard_map/ppermute | solution.py:367
  239.0 12.9 %collective-permute-start.12 = (bf16[256,2048]{1,0:T(8,128)(2,1)}, bf16[256,2048]{1,0:T(8,128)(2,1)}, u32[]{:S(2)}, u32[]{:S(2)}) collective-permute-start(bf16[256,2048]{1,0:T(8,128)(2,1)} %get-tuple-element.54), channel_id=1, source_target_pairs={{0,1},{1,0},{2,3},{3,2},{4,5},{5,4},{6,7},{7,6},{8,9},{9,8},{10,11... | collective-permute-start | bytes 3145736 | tf_op jit(solution)/shard_map/ppermute | solution.py:367
  241.9 25.9 %collective-permute-start.14 = (bf16[256,2048]{1,0:T(8,128)(2,1)}, bf16[256,2048]{1,0:T(8,128)(2,1)}, u32[]{:S(2)}, u32[]{:S(2)}) collective-permute-start(bf16[256,2048]{1,0:T(8,128)(2,1)} %add_convert_fusion.5), channel_id=1, source_target_pairs={{0,2},{1,3},{2,0},{3,1},{4,6},{5,7},{6,4},{7,5},{8,10},{9,11},{10,... | collective-permute-start | bytes 3145736 | tf_op jit(solution)/shard_map/ppermute | solution.py:367
  248.3 119.7 %collective-permute-start.44 = (bf16[2048,1024]{1,0:T(8,128)(2,1)}, bf16[2048,1024]{1,0:T(8,128)(2,1)}, u32[]{:S(2)}, u32[]{:S(2)}) collective-permute-start(bf16[2048,1024]{1,0:T(8,128)(2,1)} %convolution_convert_fusion.3), channel_id=1, source_target_pairs={{0,4},{4,0},{8,12},{12,8},{16,20},{20,16},{24,28},{28,24},{1,5},{5... | collective-permute-start | bytes 12582920 | tf_op jit(solution)/shard_map/ppermute | solution.py:367
  249.8 129.5 %collective-permute-start.41 = (bf16[1024,2048]{1,0:T(8,128)(2,1)}, bf16[1024,2048]{1,0:T(8,128)(2,1)}, u32[]{:S(2)}, u32[]{:S(2)}) collective-permute-start(bf16[1024,2048]{1,0:T(8,128)(2,1)} %convolution_convert_fusion.1), channel_id=1, source_target_pairs={{0,8},{4,12},{8,0},{12,4},{16,24},{20,28},{24,16},{28,20},{1,9},{5... | collective-permute-start | bytes 12582920 | tf_op jit(solution)/shard_map/ppermute | solution.py:367
  251.4 209.7 %collective-permute-start.38 = (bf16[1024,2048]{1,0:T(8,128)(2,1)}, bf16[1024,2048]{1,0:T(8,128)(2,1)}, u32[]{:S(2)}, u32[]{:S(2)}) collective-permute-start(bf16[1024,2048]{1,0:T(8,128)(2,1)} %convolution_convert_fusion.2), channel_id=1, source_target_pairs={{0,4},{4,0},{8,12},{12,8},{16,20},{20,16},{24,28},{28,24},{1,5},{5... | collective-permute-start | bytes 12582920 | tf_op jit(solution)/shard_map/ppermute | solution.py:367
  274.5 24.8 %collective-permute-start.15 = (bf16[256,2048]{1,0:T(8,128)(2,1)S(1)}, bf16[256,2048]{1,0:T(8,128)(2,1)S(1)}, u32[]{:S(2)}, u32[]{:S(2)}) collective-permute-start(bf16[256,2048]{1,0:T(8,128)(2,1)S(1)} %get-tuple-element.73), channel_id=1, source_target_pairs={{0,2},{1,3},{2,0},{3,1},{4,6},{5,7},{6,4},{7,5},{8,10},{9,11},{10,... | collective-permute-start | bytes 3145736 | tf_op jit(solution)/shard_map/ppermute | solution.py:367
  275.0 25.8 %collective-permute-start.19 = (bf16[256,2048]{1,0:T(8,128)(2,1)S(1)}, bf16[256,2048]{1,0:T(8,128)(2,1)S(1)}, u32[]{:S(2)}, u32[]{:S(2)}) collective-permute-start(bf16[256,2048]{1,0:T(8,128)(2,1)S(1)} %get-tuple-element.73), channel_id=1, source_target_pairs={{0,1},{1,0},{2,3},{3,2},{4,5},{5,4},{6,7},{7,6},{8,9},{9,8},{10,11... | collective-permute-start | bytes 3145736 | tf_op jit(solution)/shard_map/ppermute | solution.py:367
  299.2 4.9 collective-permute-start.20
  300.8 64.0 %collective-permute-start.17 = (bf16[256,2048]{1,0:T(8,128)(2,1)}, bf16[256,2048]{1,0:T(8,128)(2,1)}, u32[]{:S(2)}, u32[]{:S(2)}) collective-permute-start(bf16[256,2048]{1,0:T(8,128)(2,1)} %get-tuple-element.96), channel_id=1, source_target_pairs={{0,1},{1,0},{2,3},{3,2},{4,5},{5,4},{6,7},{7,6},{8,9},{9,8},{10,11... | collective-permute-start | bytes 3145736 | tf_op jit(solution)/shard_map/ppermute | solution.py:367
  304.1 170.1 %collective-permute-start.16 = (bf16[256,2048]{1,0:T(8,128)(2,1)}, bf16[256,2048]{1,0:T(8,128)(2,1)}, u32[]{:S(2)}, u32[]{:S(2)}) collective-permute-start(bf16[256,2048]{1,0:T(8,128)(2,1)} %get-tuple-element.95), channel_id=1, source_target_pairs={{0,1},{1,0},{2,3},{3,2},{4,5},{5,4},{6,7},{7,6},{8,9},{9,8},{10,11... | collective-permute-start | bytes 3145736 | tf_op jit(solution)/shard_map/ppermute | solution.py:367
  364.8 13.9 %collective-permute-start.32 = (bf16[1024,256]{1,0:T(8,128)(2,1)S(1)}, bf16[1024,256]{1,0:T(8,128)(2,1)S(1)}, u32[]{:S(2)}, u32[]{:S(2)}) collective-permute-start(bf16[1024,256]{1,0:T(8,128)(2,1)S(1)} %fusion.65), channel_id=1, source_target_pairs={{0,8},{4,12},{8,0},{12,4},{16,24},{20,28},{24,16},{28,20},{1,9},{5... | collective-permute-start | bytes 1572872 | tf_op jit(solution)/shard_map/ppermute | solution.py:367
  368.0 103.5 %collective-permute-start.29 = (bf16[1024,512]{1,0:T(8,128)(2,1)}, bf16[1024,512]{1,0:T(8,128)(2,1)}, u32[]{:S(2)}, u32[]{:S(2)}) collective-permute-start(bf16[1024,512]{1,0:T(8,128)(2,1)} %fusion.62), channel_id=1, source_target_pairs={{0,4},{4,0},{8,12},{12,8},{16,20},{20,16},{24,28},{28,24},{1,5},{5... | collective-permute-start | bytes 3145736 | tf_op jit(solution)/shard_map/ppermute | solution.py:367
  378.7 119.0 %collective-permute-start.22 = (bf16[256,2048]{1,0:T(8,128)(2,1)S(1)}, bf16[256,2048]{1,0:T(8,128)(2,1)}, u32[]{:S(2)}, u32[]{:S(2)}) collective-permute-start(bf16[256,2048]{1,0:T(8,128)(2,1)S(1)} %convolution_convert_fusion.8), channel_id=1, source_target_pairs={{0,1},{1,0},{2,3},{3,2},{4,5},{5,4},{6,7},{7,6},{8,9},{9,8},{10,11... | collective-permute-start | bytes 3145736 | tf_op jit(solution)/shard_map/ppermute | solution.py:367
  379.2 82.3 %copy-start.2 = (bf16[1024,2048]{1,0:T(8,128)(2,1)S(1)}, bf16[1024,2048]{1,0:T(8,128)(2,1)}, u32[]{:S(2)}) copy-start(bf16[1024,2048]{1,0:T(8,128)(2,1)} %get-tuple-element.52.dg_ref) | copy-start | bytes 12582916
  379.3 79.9 %collective-permute-start.33 = (bf16[512,256]{1,0:T(8,128)(2,1)S(1)}, bf16[512,256]{1,0:T(8,128)(2,1)S(1)}, u32[]{:S(2)}, u32[]{:S(2)}) collective-permute-start(bf16[512,256]{1,0:T(8,128)(2,1)S(1)} %fusion.99), channel_id=1, source_target_pairs={{0,4},{4,0},{8,12},{12,8},{16,20},{20,16},{24,28},{28,24},{1,5},{5... | collective-permute-start | bytes 786440 | tf_op jit(solution)/shard_map/ppermute | solution.py:367
  459.1 24.6 %collective-permute-start.18 = (bf16[256,2048]{1,0:T(8,128)(2,1)S(1)}, bf16[256,2048]{1,0:T(8,128)(2,1)}, u32[]{:S(2)}, u32[]{:S(2)}) collective-permute-start(bf16[256,2048]{1,0:T(8,128)(2,1)S(1)} %add_convert_fusion.4), channel_id=1, source_target_pairs={{0,2},{1,3},{2,0},{3,1},{4,6},{5,7},{6,4},{7,5},{8,10},{9,11},{10,... | collective-permute-start | bytes 3145736 | tf_op jit(solution)/shard_map/ppermute | solution.py:367
  461.1 7.8 %collective-permute-start.34 = (bf16[256,256]{1,0:T(8,128)(2,1)S(1)}, bf16[256,256]{1,0:T(8,128)(2,1)S(1)}, u32[]{:S(2)}, u32[]{:S(2)}) collective-permute-start(bf16[256,256]{1,0:T(8,128)(2,1)S(1)} %fusion.83), channel_id=1, source_target_pairs={{0,24},{4,28},{8,16},{12,20},{16,8},{20,12},{24,0},{28,4},{1,25},{... | collective-permute-start | bytes 393224 | tf_op jit(solution)/shard_map/ppermute | solution.py:367
  468.9 26.4 %collective-permute-start.35 = (bf16[512,1024]{1,0:T(8,128)(2,1)}, bf16[512,1024]{1,0:T(8,128)(2,1)}, u32[]{:S(2)}, u32[]{:S(2)}) collective-permute-start(bf16[512,1024]{1,0:T(8,128)(2,1)} %fusion.59), channel_id=1, source_target_pairs={{0,4},{4,0},{8,12},{12,8},{16,20},{20,16},{24,28},{28,24},{1,5},{5... | collective-permute-start | bytes 3145736 | tf_op jit(solution)/shard_map/ppermute | solution.py:367
  471.5 101.8 %collective-permute-start.21 = (bf16[256,2048]{1,0:T(8,128)(2,1)S(1)}, bf16[256,2048]{1,0:T(8,128)(2,1)S(1)}, u32[]{:S(2)}, u32[]{:S(2)}) collective-permute-start(bf16[256,2048]{1,0:T(8,128)(2,1)S(1)} %convolution_convert_fusion.10), channel_id=1, source_target_pairs={{0,1},{1,0},{2,3},{3,2},{4,5},{5,4},{6,7},{7,6},{8,9},{9,8},{10,11... | collective-permute-start | bytes 3145736 | tf_op jit(solution)/shard_map/ppermute | solution.py:367
  474.3 106.5 %collective-permute-start.45 = (bf16[2048,512]{1,0:T(8,128)(2,1)}, bf16[2048,512]{1,0:T(8,128)(2,1)}, u32[]{:S(2)}, u32[]{:S(2)}) collective-permute-start(bf16[2048,512]{1,0:T(8,128)(2,1)} %add_convert_fusion), channel_id=1, source_target_pairs={{0,8},{4,12},{8,0},{12,4},{16,24},{20,28},{24,16},{28,20},{1,9},{5... | collective-permute-start | bytes 6291464 | tf_op jit(solution)/shard_map/ppermute | solution.py:367
  483.7 103.8 %collective-permute-start.42 = (bf16[512,2048]{1,0:T(8,128)(2,1)}, bf16[512,2048]{1,0:T(8,128)(2,1)S(1)}, u32[]{:S(2)}, u32[]{:S(2)}) collective-permute-start(bf16[512,2048]{1,0:T(8,128)(2,1)} %add_convert_fusion.1), channel_id=1, source_target_pairs={{0,4},{4,0},{8,12},{12,8},{16,20},{20,16},{24,28},{28,24},{1,5},{5... | collective-permute-start | bytes 6291464 | tf_op jit(solution)/shard_map/ppermute | solution.py:367
  495.3 38.9 %collective-permute-start.30 = (bf16[512,512]{1,0:T(8,128)(2,1)}, bf16[512,512]{1,0:T(8,128)(2,1)S(1)}, u32[]{:S(2)}, u32[]{:S(2)}) collective-permute-start(bf16[512,512]{1,0:T(8,128)(2,1)} %fusion.89), channel_id=1, source_target_pairs={{0,8},{4,12},{8,0},{12,4},{16,24},{20,28},{24,16},{28,20},{1,9},{5... | collective-permute-start | bytes 1572872 | tf_op jit(solution)/shard_map/ppermute | solution.py:367
  497.7 47.1 %collective-permute-start.36 = (bf16[512,512]{1,0:T(8,128)(2,1)S(1)}, bf16[512,512]{1,0:T(8,128)(2,1)S(1)}, u32[]{:S(2)}, u32[]{:S(2)}) collective-permute-start(bf16[512,512]{1,0:T(8,128)(2,1)S(1)} %fusion.109), channel_id=1, source_target_pairs={{0,8},{4,12},{8,0},{12,4},{16,24},{20,28},{24,16},{28,20},{1,9},{5... | collective-permute-start | bytes 1572872 | tf_op jit(solution)/shard_map/ppermute | solution.py:367
  534.2 39.1 %collective-permute-start.23 = (bf16[256,2048]{1,0:T(8,128)(2,1)S(1)}, bf16[256,2048]{1,0:T(8,128)(2,1)S(1)}, u32[]{:S(2)}, u32[]{:S(2)}) collective-permute-start(bf16[256,2048]{1,0:T(8,128)(2,1)S(1)} %get-tuple-element.104), channel_id=1, source_target_pairs={{0,2},{1,3},{2,0},{3,1},{4,6},{5,7},{6,4},{7,5},{8,10},{9,11},{10,... | collective-permute-start | bytes 3145736 | tf_op jit(solution)/shard_map/ppermute | solution.py:367
  544.9 19.0 %collective-permute-start.31 = (bf16[256,512]{1,0:T(8,128)(2,1)S(1)}, bf16[256,512]{1,0:T(8,128)(2,1)S(1)}, u32[]{:S(2)}, u32[]{:S(2)}) collective-permute-start(bf16[256,512]{1,0:T(8,128)(2,1)S(1)} %fusion.75), channel_id=1, source_target_pairs={{0,24},{4,28},{8,16},{12,20},{16,8},{20,12},{24,0},{28,4},{1,25},{... | collective-permute-start | bytes 786440 | tf_op jit(solution)/shard_map/ppermute | solution.py:367
  563.9 7.2 collective-permute-start.37
  571.1 71.7 %collective-permute-start.39 = (bf16[512,2048]{1,0:T(8,128)(2,1)}, bf16[512,2048]{1,0:T(8,128)(2,1)S(1)}, u32[]{:S(2)}, u32[]{:S(2)}) collective-permute-start(bf16[512,2048]{1,0:T(8,128)(2,1)} %add_convert_fusion.2), channel_id=1, source_target_pairs={{0,8},{4,12},{8,0},{12,4},{16,24},{20,28},{24,16},{28,20},{1,9},{5... | collective-permute-start | bytes 6291464 | tf_op jit(solution)/shard_map/ppermute | solution.py:367
  575.1 1.2 collective-permute-start.24
  576.3 3.8 collective-permute-start.25
  580.2 4.4 collective-permute-start.26
  584.2 120.7 %collective-permute-start.46 = (bf16[2048,256]{1,0:T(8,128)(2,1)S(1)}, bf16[2048,256]{1,0:T(8,128)(2,1)S(1)}, u32[]{:S(2)}, u32[]{:S(2)}) collective-permute-start(bf16[2048,256]{1,0:T(8,128)(2,1)S(1)} %fusion.9), channel_id=1, source_target_pairs={{0,24},{4,28},{8,16},{12,20},{16,8},{20,12},{24,0},{28,4},{1,25},{... | collective-permute-start | bytes 3145736 | tf_op jit(solution)/shard_map/ppermute | solution.py:367
  584.5 57.9 %collective-permute-start.27 = (bf16[2,512]{1,0:T(2,128)(2,1)S(1)}, bf16[2,512]{1,0:T(2,128)(2,1)S(1)}, u32[]{:S(2)}, u32[]{:S(2)}) collective-permute-start(bf16[2,512]{1,0:T(2,128)(2,1)S(1)} %fusion.152), channel_id=1, source_target_pairs={{0,8},{4,12},{8,0},{12,4},{16,24},{20,28},{24,16},{28,20},{1,9},{5... | collective-permute-start | bytes 6152 | tf_op jit(solution)/shard_map/ppermute | solution.py:367
  590.2 110.7 %collective-permute-start.43 = (bf16[256,2048]{1,0:T(8,128)(2,1)S(1)}, bf16[256,2048]{1,0:T(8,128)(2,1)S(1)}, u32[]{:S(2)}, u32[]{:S(2)}) collective-permute-start(bf16[256,2048]{1,0:T(8,128)(2,1)S(1)} %fusion.10), channel_id=1, source_target_pairs={{0,24},{4,28},{8,16},{12,20},{16,8},{20,12},{24,0},{28,4},{1,25},{... | collective-permute-start | bytes 3145736 | tf_op jit(solution)/shard_map/ppermute | solution.py:367
  642.4 57.9 %collective-permute-start.28 = (bf16[2,256]{1,0:T(2,128)(2,1)S(1)}, bf16[2,256]{1,0:T(2,128)(2,1)S(1)}, u32[]{:S(2)}, u32[]{:S(2)}) collective-permute-start(bf16[2,256]{1,0:T(2,128)(2,1)S(1)} %fusion.164), channel_id=1, source_target_pairs={{0,24},{4,28},{8,16},{12,20},{16,8},{20,12},{24,0},{28,4},{1,25},{... | collective-permute-start | bytes 3080 | tf_op jit(solution)/shard_map/ppermute | solution.py:367
  645.4 75.2 %collective-permute-start.40 = (bf16[256,2048]{1,0:T(8,128)(2,1)S(1)}, bf16[256,2048]{1,0:T(8,128)(2,1)S(1)}, u32[]{:S(2)}, u32[]{:S(2)}) collective-permute-start(bf16[256,2048]{1,0:T(8,128)(2,1)S(1)} %fusion.11), channel_id=1, source_target_pairs={{0,24},{4,28},{8,16},{12,20},{16,8},{20,12},{24,0},{28,4},{1,25},{... | collective-permute-start | bytes 3145736 | tf_op jit(solution)/shard_map/ppermute | solution.py:367
  (87 other events, 1106.0 us)

commit v2 on v1

v2 whole, which is shorter than its diff:
```python
import functools

import jax
import jax.numpy as jnp
from jax import lax
from jax.experimental import pallas as pl
from jax.experimental.pallas import tpu as pltpu
from jax.sharding import PartitionSpec as P

HEAD_SIZE = 64


EPSILON = 1e-05
MULTIPLIER = 0.015625
RESIDUAL_SCALE = 0.22
THETA_BASE = 10000.0
MASK_VALUE = -1e30
LOW = jnp.bfloat16
WIDE = jnp.float32
LANES = 128
TILE = 256
NN = (((1,), (0,)), ((), ()))
NT = (((1,), (1,)), ((), ()))
TN = (((0,), (0,)), ((), ()))
COST = pl.CostEstimate(flops=1, bytes_accessed=1, transcendentals=0)


def dot(a, b, dims=NN):
    return lax.dot_general(a, b, dims, preferred_element_type=WIDE)


def after(value, *others):
    return lax.optimization_barrier((value, *others))[0]


class Lane:
    def __init__(self):
        self.last = ()

    def __call__(self, function, *operands):
        if self.last:
            operands = after(operands, *self.last)
        result = function(*operands)
        self.last = tuple(jax.tree.leaves(result))
        return result


def positions_of(seg_ids):
    length = seg_ids.shape[-1]
    index = jnp.broadcast_to(jnp.arange(length, dtype=jnp.int32), seg_ids.shape)
    before = jnp.concatenate([seg_ids[:, :1] - 1, seg_ids[:, :-1]], axis=1)
    starts = jnp.where(seg_ids != before, index, jnp.zeros_like(index))
    return index - lax.cummax(starts, axis=1)


def rope_tables(positions):
    half = HEAD_SIZE // 2
    freq = THETA_BASE ** (-2.0 * jnp.arange(half, dtype=jnp.float32) / HEAD_SIZE)
    angle = positions.astype(jnp.float32)[:, None] * freq[None, :]
    cosine, sine = jnp.cos(angle), jnp.sin(angle)
    repeats = LANES // HEAD_SIZE
    return (
        jnp.concatenate([cosine, cosine] * repeats, axis=1),
        jnp.concatenate([-sine, sine] * repeats, axis=1),
    )


def lane_index(shape):
    return lax.broadcasted_iota(jnp.int32, shape, len(shape) - 1)


def turn(u, cosine, sine):
    quarter = HEAD_SIZE // 2
    first = lane_index(u.shape) % HEAD_SIZE < quarter
    other = jnp.where(
        first, pltpu.roll(u, u.shape[1] - quarter, 1), pltpu.roll(u, quarter, 1)
    )
    return u * cosine + other * sine


def load_shares(share_refs, held, sems):
    copies, first = [], 0
    for i, ref in enumerate(share_refs):
        copies.append(pltpu.make_async_copy(ref, held.at[pl.ds(first, ref.shape[0])], sems.at[i]))
        first += ref.shape[0]
    for copy in copies:
        copy.start()
    for copy in copies:
        copy.wait()


def rows_in(shares):
    return sum(a.shape[0] for a in shares)


def project_kernel(count, turned, dims, order_ref, *refs):
    share_refs, w_ref, tables = refs[:count], refs[count], refs[count + 1 : count + 3]
    out_ref, held, sems = refs[-3:]
    share = out_ref.shape[0]

    @pl.when(pl.program_id(0) == 0)
    def _():
        load_shares(share_refs, held, sems)

    mine = held[pl.ds(pl.multiple_of(pl.program_id(0) * share, share), share), :]
    out = dot(mine, w_ref[...], dims)
    for j in range(out.shape[1] // LANES):
        part = out[:, j * LANES : (j + 1) * LANES]
        if j * LANES < turned:
            part = turn(part, tables[0][...], tables[1][...])
        out_ref[:, j * LANES : (j + 1) * LANES] = part.astype(LOW)


def project(shares, order, weight, rows, dims, turned=0, tables=(), given=()):
    count, (share, width) = len(shares), shares[0].shape
    columns = weight.shape[1] if dims is NN else weight.shape[0]
    moving = lambda i, order: (order[i], 0)
    return pl.pallas_call(
        functools.partial(project_kernel, count, turned, dims),
        grid_spec=pltpu.PrefetchScalarGridSpec(
            num_scalar_prefetch=1,
            grid=(count,),
            in_specs=[pl.BlockSpec(memory_space=pl.ANY)] * count
            + [pl.BlockSpec(weight.shape, lambda i, order: (0, 0))]
            + [pl.BlockSpec((share, LANES), moving)] * len(tables)
            + [pl.BlockSpec(memory_space=pl.ANY)] * len(given),
            out_specs=pl.BlockSpec((share, columns), moving),
            scratch_shapes=[
                pltpu.VMEM((count * share, width), LOW),
                pltpu.SemaphoreType.DMA((count,)),
            ],
        ),
        out_shape=jax.ShapeDtypeStruct((rows, columns), LOW),
        input_output_aliases={count + 2 + len(tables): 0} if given else {},
        cost_estimate=COST,
        name="project",
    )(order, *shares, weight, *tables, *given)


def pieces_kernel(dims, order_ref, a_ref, w_ref, *out_refs):
    w = w_ref[...]
    for i, ref in enumerate(out_refs):
        share = ref.shape[0]
        mine = a_ref[pl.ds(pl.multiple_of(order_ref[i] * share, share), share), :]
        ref[...] = dot(mine, w, dims).astype(LOW)


def pieces(a, weight, order, count, transposed):
    rows, depth = a.shape
    share = rows // count
    width = weight.shape[0] if transposed else weight.shape[1]
    moving = (
        pl.BlockSpec((TILE, depth), lambda i, order: (i, 0))
        if transposed
        else pl.BlockSpec((depth, TILE), lambda i, order: (0, i))
    )
    return pl.pallas_call(
        functools.partial(pieces_kernel, NT if transposed else NN),
        grid_spec=pltpu.PrefetchScalarGridSpec(
            num_scalar_prefetch=1,
            grid=(width // TILE,),
            in_specs=[pl.BlockSpec((rows, depth), lambda i, order: (0, 0)), moving],
            out_specs=[pl.BlockSpec((share, TILE), lambda i, order: (0, i))] * count,
        ),
        out_shape=[jax.ShapeDtypeStruct((share, width), LOW)] * count,
        cost_estimate=COST,
        name="pieces",
    )(order, a, weight)


def doubled(pair, half):
    swapped = pltpu.roll(pair.astype(WIDE), HEAD_SIZE, 1).astype(pair.dtype)
    low = lane_index(pair.shape) < HEAD_SIZE
    return jnp.where(low == (half == 0), pair, swapped)


def attend_kernel(per_kv, q_ref, k_ref, v_ref, segq_ref, segk_ref, o_ref, lse_ref):
    half = (pl.program_id(1) // per_kv) % 2
    length = k_ref.shape[0]
    k, v = doubled(k_ref[...], half), doubled(v_ref[...], half)
    low = lane_index((TILE, LANES)) < HEAD_SIZE
    q_at = lax.broadcasted_iota(jnp.int32, (TILE, TILE), 0)
    k_at = lax.broadcasted_iota(jnp.int32, (TILE, TILE), 1)
    for i in range(length // TILE):
        rows = slice(i * TILE, (i + 1) * TILE)
        reach = (i + 1) * TILE
        q = q_ref[rows, :]
        same = segq_ref[rows, :] == segk_ref[:, :reach]
        last = same[:, i * TILE :] & (k_at <= q_at)
        allowed = jnp.concatenate([same[:, : i * TILE], last], axis=1) if i else last
        outs = []
        for head in range(2):
            mine = jnp.where(low == (head == 0), q, jnp.zeros_like(q))
            raw = dot(mine, k[:reach], NT)
            scores = jnp.where(allowed, MULTIPLIER * raw, MASK_VALUE)
            top = jnp.max(scores, axis=1, keepdims=True)
            e = jnp.exp(scores - top)
            total = jnp.sum(e, axis=1, keepdims=True)
            p = (e * (1.0 / total)).astype(LOW)
            outs.append(dot(p, v[:reach]))
            lse = top + jnp.log(total)
            lse_ref[0, head : head + 1, rows] = jnp.transpose(
                jnp.broadcast_to(lse, (TILE, LANES))
            )[:1]
        o_ref[rows, :] = jnp.where(low, outs[0], outs[1]).astype(LOW)


def attend(qkv, q_width, kv_width, seg_col, seg_row, seqs):
    rows = qkv.shape[0]
    length = rows // seqs
    pairs, kv_pairs = q_width // LANES, kv_width // LANES
    per_kv = pairs // kv_pairs // 2
    return pl.pallas_call(
        functools.partial(attend_kernel, per_kv),
        grid=(seqs, pairs),
        in_specs=[
            pl.BlockSpec((length, LANES), lambda s, h: (s, h)),
            pl.BlockSpec((length, LANES), lambda s, h: (s, pairs + h // (2 * per_kv))),
            pl.BlockSpec((length, LANES), lambda s, h: (s, pairs + kv_pairs + h // (2 * per_kv))),
            pl.BlockSpec((length, 1), lambda s, h: (s, 0)),
            pl.BlockSpec((None, 1, length), lambda s, h: (s, 0, 0)),
        ],
        out_specs=[
            pl.BlockSpec((length, LANES), lambda s, h: (s, h)),
            pl.BlockSpec((1, 2, length), lambda s, h: (h, 0, s)),
        ],
        out_shape=[
            jax.ShapeDtypeStruct((rows, q_width), LOW),
            jax.ShapeDtypeStruct((pairs, 2, rows), WIDE),
        ],
        cost_estimate=COST,
        name="attend",
    )(qkv, qkv, qkv, seg_col, seg_row)


def attend_back_kernel(
    per_kv,
    q_ref,
    k_ref,
    v_ref,
    g_ref,
    lse_ref,
    segc_ref,
    segr_ref,
    cos_ref,
    sin_ref,
    out_ref,
    dk_acc,
    dv_acc,
    p_buf,
    dp_buf,
):
    pair, pairs = pl.program_id(1), pl.num_programs(1)
    slot = (pair // per_kv) % 2
    length = k_ref.shape[0]
    k, v = doubled(k_ref[...], slot), doubled(v_ref[...], slot)
    low = lane_index((TILE, LANES)) < HEAD_SIZE
    k_at = lax.broadcasted_iota(jnp.int32, (TILE, TILE), 0)
    q_at = lax.broadcasted_iota(jnp.int32, (TILE, TILE), 1)

    @pl.when(pair % per_kv == 0)
    def _():
        dk_acc[slot] = jnp.zeros_like(dk_acc[slot])
        dv_acc[slot] = jnp.zeros_like(dv_acc[slot])

    for i in range(length // TILE):
        rows = slice(i * TILE, (i + 1) * TILE)
        q, g = q_ref[rows, :], g_ref[rows, :]
        dq = []
        for head in range(2):
            chosen = low == (head == 0)
            qh = jnp.where(chosen, q, jnp.zeros_like(q))
            gh = jnp.where(chosen, g, jnp.zeros_like(g))
            lse = lse_ref[0, head : head + 1, rows]
            inner = jnp.zeros((1, TILE), WIDE)
            for j in range(i + 1):
                keys = slice(j * TILE, (j + 1) * TILE)
                allowed = segc_ref[keys, :] == segr_ref[:, rows]
                if i == j:
                    allowed = allowed & (k_at <= q_at)
                raw = dot(k[keys], qh, NT)
                p = jnp.exp(jnp.where(allowed, MULTIPLIER * raw, MASK_VALUE) - lse)
                dp = dot(v[keys], gh, NT)
                inner = inner + jnp.sum(p * dp, axis=0, keepdims=True)
                p_buf[keys, :] = p
                dp_buf[keys, :] = dp
            total = jnp.zeros((TILE, LANES), WIDE)
            for j in range(i + 1):
                keys = slice(j * TILE, (j + 1) * TILE)
                p = p_buf[keys, :]
                ds = (p * (dp_buf[keys, :] - inner)).astype(LOW)
                dv_acc[slot, keys, :] += dot(p.astype(LOW), gh)
                dk_acc[slot, keys, :] += dot(ds, qh)
                total = total + dot(ds, k[keys], TN)
            dq.append(total)
        out_ref[rows, pl.ds(pl.multiple_of(pair * LANES, LANES), LANES)] = turn(
            MULTIPLIER * jnp.where(low, dq[0], dq[1]), cos_ref[rows, :], -sin_ref[rows, :]
        ).astype(LOW)

    @pl.when(pair % (2 * per_kv) == 2 * per_kv - 1)
    def _():
        low_all = lane_index((length, LANES)) < HEAD_SIZE

        def folded(acc):
            a, b = acc[0], acc[1]
            a = a + pltpu.roll(a, HEAD_SIZE, 1)
            b = b + pltpu.roll(b, HEAD_SIZE, 1)
            return jnp.where(low_all, a, b)

        kv_pair = pair // (2 * per_kv)
        key_at = pl.multiple_of((pairs + kv_pair) * LANES, LANES)
        value_at = pl.multiple_of((pairs + pairs // (2 * per_kv) + kv_pair) * LANES, LANES)
        out_ref[:, pl.ds(key_at, LANES)] = turn(
            MULTIPLIER * folded(dk_acc), cos_ref[...], -sin_ref[...]
        ).astype(LOW)
        out_ref[:, pl.ds(value_at, LANES)] = folded(dv_acc).astype(LOW)


def attend_back(qkv, q_width, kv_width, g, lse, seg_col, seg_row, cosine, sine, seqs):
    rows = qkv.shape[0]
    length = rows // seqs
    pairs, kv_pairs = q_width // LANES, kv_width // LANES
    per_kv = pairs // kv_pairs // 2
    by_pair = lambda s, h: (s, h)
    by_seq = lambda s, h: (s, 0)
    return pl.pallas_call(
        functools.partial(attend_back_kernel, per_kv),
        grid=(seqs, pairs),
        in_specs=[
            pl.BlockSpec((length, LANES), by_pair),
            pl.BlockSpec((length, LANES), lambda s, h: (s, pairs + h // (2 * per_kv))),
            pl.BlockSpec((length, LANES), lambda s, h: (s, pairs + kv_pairs + h // (2 * per_kv))),
            pl.BlockSpec((length, LANES), by_pair),
            pl.BlockSpec((1, 2, length), lambda s, h: (h, 0, s)),
            pl.BlockSpec((length, 1), by_seq),
            pl.BlockSpec((None, 1, length), lambda s, h: (s, 0, 0)),
            pl.BlockSpec((length, LANES), by_seq),
            pl.BlockSpec((length, LANES), by_seq),
        ],
        out_specs=pl.BlockSpec((length, qkv.shape[1]), by_seq),
        out_shape=jax.ShapeDtypeStruct(qkv.shape, LOW),
        scratch_shapes=[
            pltpu.VMEM((2, length, LANES), WIDE),
            pltpu.VMEM((2, length, LANES), WIDE),
            pltpu.VMEM((length, TILE), WIDE),
            pltpu.VMEM((length, TILE), WIDE),
        ],
        cost_estimate=COST,
        name="attend_back",
    )(qkv, qkv, qkv, g, lse, seg_col, seg_row, cosine, sine)


def branch_kernel(count, at_ref, *refs):
    w_ref, out_ref, held, sems = refs[count:]

    @pl.when(pl.program_id(0) == 0)
    def _():
        load_shares(refs[:count], held, sems)

    out_ref[...] = dot(held[...], w_ref[...], NT)


def branch(shares, w_down, at):
    count, width, rows = len(shares), shares[0].shape[1], rows_in(shares)
    units = w_down.shape[0] // 2
    tiles = units // TILE
    return pl.pallas_call(
        functools.partial(branch_kernel, count),
        grid_spec=pltpu.PrefetchScalarGridSpec(
            num_scalar_prefetch=1,
            grid=(tiles,),
            in_specs=[pl.BlockSpec(memory_space=pl.ANY)] * count
            + [pl.BlockSpec((TILE, width), lambda i, at: (at[0] * tiles + i, 0))],
            out_specs=pl.BlockSpec((rows, TILE), lambda i, at: (0, i)),
            scratch_shapes=[
                pltpu.VMEM((rows, width), LOW),
                pltpu.SemaphoreType.DMA((count,)),
            ],
        ),
        out_shape=jax.ShapeDtypeStruct((rows, units), WIDE),
        cost_estimate=COST,
        name="branch",
    )(at, *shares, w_down)


def mix_kernel(count, at_ref, *refs):
    share_refs, (wg_ref, wu_ref, dm_ref) = refs[:count], refs[count : count + 3]
    m_ref, dg_ref, du_ref, held, sems = refs[-5:]

    @pl.when(pl.program_id(0) == 0)
    def _():
        load_shares(share_refs, held, sems)

    n = held[...]
    g = dot(n, wg_ref[...])
    u = dot(n, wu_ref[...])
    dm = dm_ref[...]
    s = jax.nn.sigmoid(g)
    active = g * s
    m_ref[...] = (active * u).astype(LOW)
    dg_ref[...] = (dm * u * s * (1.0 + g * (1.0 - s))).astype(LOW)
    du_ref[...] = (dm * active).astype(LOW)


def mix(shares, wg, wu, dm, at, block, given=()):
    count, width, rows = len(shares), shares[0].shape[1], rows_in(shares)
    tiles = dm.shape[1] // TILE
    weight = pl.BlockSpec((width, TILE), lambda i, at: (0, at[0] * tiles + i))
    spec = pl.BlockSpec((rows, TILE), lambda i, at: (block, i))
    return pl.pallas_call(
        functools.partial(mix_kernel, count),
        grid_spec=pltpu.PrefetchScalarGridSpec(
            num_scalar_prefetch=1,
            grid=(tiles,),
            in_specs=[pl.BlockSpec(memory_space=pl.ANY)] * count
            + [weight, weight, spec]
            + [pl.BlockSpec(memory_space=pl.ANY)] * len(given),
            out_specs=[spec] * 3,
            scratch_shapes=[
                pltpu.VMEM((rows, width), LOW),
                pltpu.SemaphoreType.DMA((count,)),
            ],
        ),
        out_shape=[jax.ShapeDtypeStruct(dm.shape, LOW)] * 3,
        input_output_aliases={count + 4 + i: i for i in range(len(given))},
        cost_estimate=COST,
        name="mix",
    )(at, *shares, wg, wu, dm, *given)


def unmix_kernel(at_ref, dg_ref, du_ref, wg_ref, wu_ref, *out_refs):
    total = dot(dg_ref[...], wg_ref[...], NT) + dot(du_ref[...], wu_ref[...], NT)
    share = out_refs[0].shape[0]
    for i, ref in enumerate(out_refs):
        ref[...] = total[i * share : (i + 1) * share].astype(LOW)


def unmix(dg, du, wg, wu, at, block, share, pieces):
    units, width = dg.shape[1], wg.shape[0]
    rows = share * pieces
    given = pl.BlockSpec((rows, units), lambda i, at: (block, 0))
    moving = pl.BlockSpec((TILE, units), lambda i, at: (i, at[0]))
    return pl.pallas_call(
        unmix_kernel,
        grid_spec=pltpu.PrefetchScalarGridSpec(
            num_scalar_prefetch=1,
            grid=(width // TILE,),
            in_specs=[given, given, moving, moving],
            out_specs=[pl.BlockSpec((share, TILE), lambda i, at: (0, i))] * pieces,
        ),
        out_shape=[jax.ShapeDtypeStruct((share, width), LOW)] * pieces,
        cost_estimate=COST,
        name="unmix",
    )(at, dg, du, wg, wu)


def down_kernel(at_ref, m_ref, w_ref, *out_refs):
    total = dot(m_ref[...], w_ref[...])
    share = out_refs[0].shape[0]
    for i, ref in enumerate(out_refs):
        ref[...] = total[i * share : (i + 1) * share].astype(LOW)


def down(m, w_down, at, share):
    rows, units = m.shape
    width = w_down.shape[1]
    pieces = rows // share
    return pl.pallas_call(
        down_kernel,
        grid_spec=pltpu.PrefetchScalarGridSpec(
            num_scalar_prefetch=1,
            grid=(width // TILE,),
            in_specs=[
                pl.BlockSpec((rows, units), lambda i, at: (0, 0)),
                pl.BlockSpec((units, TILE), lambda i, at: (at[0], i)),
            ],
            out_specs=[pl.BlockSpec((share, TILE), lambda i, at: (0, i))] * pieces,
        ),
        out_shape=[jax.ShapeDtypeStruct((share, width), LOW)] * pieces,
        cost_estimate=COST,
        name="down",
    )(at, m, w_down)


def spread_kernel(count, columns_ref, rows_ref, *refs):
    out_ref = refs[-1]
    share = refs[0].shape[0]
    for i in range(count):
        out_ref[pl.ds(pl.multiple_of(rows_ref[i] * share, share), share), :] = refs[i][...]


def spread(shares, rows, block, masks, place, given=None, order=None):
    count, (share, width) = len(shares), shares[0].shape
    blocks = jnp.array(block_order(masks), jnp.int32) ^ place
    order = jnp.arange(count, dtype=jnp.int32) if order is None else order
    columns = width // (1 << len(masks))
    if columns % LANES:
        whole = jnp.zeros((rows, width), LOW) if given is None else given
        for i, a in enumerate(shares):
            piece = permute_columns(a, masks, place)
            first = (block * count + order[i]) * share
            whole = lax.dynamic_update_slice_in_dim(whole, piece, first, 0)
        return whole
    extra = [] if given is None else [given]
    return pl.pallas_call(
        functools.partial(spread_kernel, count),
        grid_spec=pltpu.PrefetchScalarGridSpec(
            num_scalar_prefetch=2,
            grid=(width // columns,),
            in_specs=[pl.BlockSpec((share, columns), lambda i, blocks, order: (0, blocks[i]))] * count
            + [pl.BlockSpec(memory_space=pl.ANY)] * len(extra),
            out_specs=pl.BlockSpec((count * share, columns), lambda i, blocks, order: (block, i)),
        ),
        out_shape=jax.ShapeDtypeStruct((rows, width), LOW),
        input_output_aliases={count + 2: 0} if extra else {},
        cost_estimate=COST,
        name="spread",
    )(blocks, order, *shares, *extra)


def product_rows(left, right, given, low, size, width, kind):
    tokens, across = right.shape
    tile = min(TILE, size * width)
    tiles = size * width // tile

    def kernel(left_ref, right_ref, *refs):
        value = dot(left_ref[...], right_ref[...], TN)
        for ref in refs[:-1]:
            value = value + ref[...].astype(WIDE)
        refs[-1][...] = value.astype(kind)

    def at(first):
        start = (low - first) * width // tile
        return lambda i: (start + i, 0)

    start = low * width // tile
    return pl.pallas_call(
        kernel,
        grid=(tiles,),
        in_specs=[
            pl.BlockSpec((tokens, tile), lambda i: (0, start + i)),
            pl.BlockSpec((tokens, across), lambda i: (0, 0)),
        ]
        + [pl.BlockSpec((tile, across), at(first)) for first, _ in given],
        out_specs=pl.BlockSpec((tile, across), lambda i: (i, 0)),
        out_shape=jax.ShapeDtypeStruct((size * width, across), kind),
        cost_estimate=COST,
        name="product_rows",
    )(left, right, *(array for _, array in given))


def product_cols(left, right, given, low, size, width, kind):
    tokens, down_to = left.shape
    across = size * width
    tile = min(TILE, down_to)

    def kernel(left_ref, right_ref, *refs):
        value = dot(left_ref[...], right_ref[...], TN)
        for ref in refs[:-1]:
            value = value + ref[...].astype(WIDE)
        refs[-1][...] = value.astype(kind)

    def at(first):
        start = (low - first) // size
        return lambda i: (i, start)

    return pl.pallas_call(
        kernel,
        grid=(down_to // tile,),
        in_specs=[
            pl.BlockSpec((tokens, tile), lambda i: (0, i)),
            pl.BlockSpec((tokens, across), lambda i: (0, low // size)),
        ]
        + [pl.BlockSpec((tile, across), at(first)) for first, _ in given],
        out_specs=pl.BlockSpec((tile, across), lambda i: (i, 0)),
        out_shape=jax.ShapeDtypeStruct((down_to, across), kind),
        cost_estimate=COST,
        name="product_cols",
    )(left, right, *(array for _, array in given))


def half_kernel(axis, at_ref, own_ref, other_ref, out_ref):
    size = own_ref.shape[axis]
    for ref, half in ((own_ref, at_ref[0]), (other_ref, 1 - at_ref[0])):
        where = pl.ds(pl.multiple_of(half * size, size), size)
        if axis == 0:
            out_ref[where, :] = ref[...].astype(WIDE)
        else:
            out_ref[:, where] = ref[...].astype(WIDE)


def halves(own, other, at, axis):
    shape = list(own.shape)
    shape[axis] *= 2
    return pl.pallas_call(
        functools.partial(half_kernel, axis),
        grid_spec=pltpu.PrefetchScalarGridSpec(
            num_scalar_prefetch=1,
            grid=(1,),
            in_specs=[pl.BlockSpec(own.shape, lambda i, at: (0, 0))] * 2,
            out_specs=pl.BlockSpec(tuple(shape), lambda i, at: (0, 0)),
        ),
        out_shape=jax.ShapeDtypeStruct(tuple(shape), WIDE),
        cost_estimate=COST,
        name="halves",
    )(at, own, other)


def whole(function, shapes, *arrays):
    def kernel(*refs):
        results = function(*(ref[...] for ref in refs[: len(arrays)]))
        for ref, value in zip(refs[len(arrays) :], results):
            ref[...] = value.astype(ref.dtype)

    return pl.pallas_call(
        kernel,
        out_shape=[jax.ShapeDtypeStruct(shape, kind) for shape, kind in shapes],
        in_specs=[pl.BlockSpec(memory_space=pltpu.VMEM)] * len(arrays),
        out_specs=[pl.BlockSpec(memory_space=pltpu.VMEM)] * len(shapes),
        cost_estimate=COST,
        name="whole",
    )(*arrays)


def norm_back_kernel(count, d_ref, value_ref, inverse_ref, gain_ref, *refs):
    term_refs, (dx_ref, low_ref, gain_out_ref) = refs[:count], refs[count:]
    d_normed = term_refs[0][...].astype(WIDE)
    for ref in term_refs[1:]:
        d_normed = d_normed + ref[...].astype(WIDE)
    values, inverse = value_ref[...].astype(WIDE), inverse_ref[...]
    scaled = d_normed * gain_ref[...].astype(WIDE)
    mean = jnp.mean(scaled * values, axis=-1, keepdims=True)
    dx = d_ref[...].astype(WIDE) + inverse * scaled - values * (inverse * inverse * inverse * mean)
    dx_ref[...] = dx.astype(dx_ref.dtype)
    low_ref[...] = (RESIDUAL_SCALE * dx).astype(LOW)

    @pl.when(pl.program_id(0) == 0)
    def _():
        gain_out_ref[...] = jnp.zeros_like(gain_out_ref)

    gain_out_ref[...] += jnp.sum(d_normed * values * inverse, axis=0, keepdims=True)


def norm_back(d_rows, values, inverse, gain, terms, kind, tile=64):
    rows, width = values.shape
    spec = pl.BlockSpec((tile, width), lambda i: (i, 0))
    fixed = pl.BlockSpec((1, width), lambda i: (0, 0))
    return pl.pallas_call(
        functools.partial(norm_back_kernel, len(terms)),
        grid=(rows // tile,),
        in_specs=[spec, spec, pl.BlockSpec((tile, 1), lambda i: (i, 0)), fixed] + [spec] * len(terms),
        out_specs=[spec, spec, fixed],
        out_shape=[
            jax.ShapeDtypeStruct((rows, width), kind),
            jax.ShapeDtypeStruct((rows, width), LOW),
            jax.ShapeDtypeStruct((1, width), WIDE),
        ],
        cost_estimate=COST,
        name="norm_back",
    )(d_rows, values, inverse, gain.reshape(1, -1), *terms)


def sum_all_kernel(steps, part_ref, out_ref, sent, got, send_sems, got_sems):
    partners = []
    for axis, mask in steps:
        mine = lax.axis_index(axis)
        partners.append({axis: mine + mask * (1 - 2 * (mine // mask % 2))})
    barrier = pltpu.get_barrier_semaphore()
    for partner in partners:
        pl.semaphore_signal(barrier, inc=1, device_id=partner, device_id_type=pl.DeviceIdType.MESH)
    pl.semaphore_wait(barrier, len(partners))
    total = part_ref[...]
    for i, partner in enumerate(partners):
        sent[i] = total
        copy = pltpu.make_async_remote_copy(
            src_ref=sent.at[i],
            dst_ref=got.at[i],
            send_sem=send_sems.at[i],
            recv_sem=got_sems.at[i],
            device_id=partner,
            device_id_type=pl.DeviceIdType.MESH,
        )
        copy.start()
        copy.wait()
        total = total + got[i]
    out_ref[...] = total


def sum_all(part, steps):
    count = len(steps)
    return pl.pallas_call(
        functools.partial(sum_all_kernel, steps),
        out_shape=jax.ShapeDtypeStruct(part.shape, part.dtype),
        in_specs=[pl.BlockSpec(memory_space=pltpu.VMEM)],
        out_specs=pl.BlockSpec(memory_space=pltpu.VMEM),
        scratch_shapes=[
            pltpu.VMEM((count, *part.shape), part.dtype),
            pltpu.VMEM((count, *part.shape), part.dtype),
            pltpu.SemaphoreType.DMA((count,)),
            pltpu.SemaphoreType.DMA((count,)),
        ],
        compiler_params=pltpu.CompilerParams(collective_id=0, has_side_effects=True),
        cost_estimate=COST,
        name="sum_all",
    )(part)


NEAR, FAR, PAIR = 1, 2, 2


def swap(array, axis, mask):
    size = lax.axis_size(axis)
    return lax.ppermute(array, axis, [(i, i ^ mask) for i in range(size)])


def powers(size):
    return [1 << i for i in range(size.bit_length() - 1)]


def swap_both(array):
    count = lax.axis_size("tensor")
    size = lax.axis_size("dp") * count
    mask = PAIR * count + FAR
    return lax.ppermute(array, ("dp", "tensor"), [(i, i ^ mask) for i in range(size)])


def cut(array):
    half = array.shape[0] // 2
    return array[:half], array[half:]


def added(*arrays):
    total = arrays[0].astype(WIDE)
    for a in arrays[1:]:
        total = total + a.astype(WIDE)
    return total


def add_low(*arrays):
    return whole(lambda *a: (added(*a),), [(arrays[0].shape, LOW)], *arrays)[0]


def joined(mine, got):
    rows, width = mine.shape
    return whole(lambda a, b: cut(added(a, b)), [((rows // 2, width), LOW)] * 2, mine, got)


class GroupSum:
    def near(self, *chips):
        return [swap(chip[1], "tensor", NEAR) for chip in chips]

    def start_both(self, lane, both):
        (got,) = self.near(both)
        low, high = lane(joined, both[0], got)
        self.low, self.high = swap(low, "tensor", FAR), swap(high, "dp", PAIR)

    def start_far_pair(self, lane, own, far, pair):
        got_own, got_far, got_pair = self.near(own, far, pair)

        def relay(own, got_own, far, got_far, high, pair, got_pair, low):
            far, pair = added(far, got_far), added(pair, got_pair)
            rows = low.shape[0]
            far = jnp.concatenate([far[:rows], far[rows:] + high.astype(WIDE)], axis=0)
            pair = jnp.concatenate([pair[:rows] + low.astype(WIDE), pair[rows:]], axis=0)
            return added(own, got_own), far, pair

        self.own, far, pair = lane(
            functools.partial(whole, relay, [(own[0].shape, kind) for kind in (WIDE, LOW, LOW)]),
            own[0],
            got_own,
            far[0],
            got_far,
            self.high,
            pair[0],
            got_pair,
            self.low,
        )
        self.far, self.pair = swap(far, "tensor", FAR), swap(pair, "dp", PAIR)

    def terms(self):
        return self.own, self.far, self.pair


def block_order(masks):
    order = [0]
    for mask in reversed(masks):
        order = [mask ^ b for b in order] + order
    return order


def permute_columns(array, masks, place):
    count = 1 << len(masks)
    width = array.shape[1] // count
    return jnp.concatenate(
        [
            lax.dynamic_slice_in_dim(array, (place ^ b) * width, width, 1)
            for b in block_order(masks)
        ],
        axis=1,
    )


class Reduction:
    def __init__(self, left, right, masks, axis):
        self.left, self.right, self.masks, self.axis = left, right, list(masks), axis
        self.count = 1 << len(masks)
        self.width = (right if axis else left).shape[1] // self.count
        self.low, self.size, self.got = 0, self.count // 2, []

    def total(self, lane, low, high):
        firsts = [first for first, _ in self.got]
        width, axis = self.width, self.axis
        kind = WIDE if high == self.count else LOW

        def compute(left, right, *arrays):
            if (high - low) * width % LANES == 0:
                product = product_cols if axis else product_rows
                return product(left, right, list(zip(firsts, arrays)), low, high - low, width, kind)
            part = slice(low * width, high * width)
            value = dot(left, right[:, part], TN) if axis else dot(left[:, part], right, TN)
            for first, array in zip(firsts, arrays):
                piece = lax.slice_in_dim(
                    array, (low - first) * width, (high - first) * width, axis=axis
                )
                value = value + piece.astype(WIDE)
            return value.astype(kind)

        return lane(compute, self.left, self.right, *(array for _, array in self.got))

    def step(self, lane):
        sent = self.total(lane, self.low, self.low + self.size)
        self.low += self.size
        self.size //= 2
        self.got.append((self.low, swap(sent, "dp", self.masks.pop(0))))
        return self

    def finish(self, lane):
        while self.masks:
            self.step(lane)
        return self.total(lane, self.low, self.count)

    def step_half(self, lane):
        while len(self.masks) > 1:
            self.step(lane)
        sent = self.total(lane, self.low, self.low + self.size)
        self.low += self.size
        self.other = swap(sent, "dp", self.masks.pop(0))
        return self

    def finish_half(self, lane, at):
        own = self.total(lane, self.low, self.count)
        return lane(lambda a, b, at: halves(a, b, at, 1 - self.axis), own, self.other, at)


def rows_of(shares):
    return jnp.concatenate(shares, axis=0)


def inverse_rms(value_rows):
    return lax.rsqrt(jnp.mean(value_rows * value_rows, axis=-1, keepdims=True) + EPSILON)


def body(
    layer_in,
    cotangent,
    segments,
    gain_attn,
    w_query,
    key_weight,
    value_weight,
    w_out,
    gain_ffn,
    w_gate,
    w_up,
    w_down,
):
    share, width = layer_in.shape
    count = lax.axis_size("tensor")
    rank = lax.axis_index("tensor")
    place = lax.axis_index("dp")
    masks = powers(lax.axis_size("dp"))
    group_masks = [m for m in masks if m != PAIR] + [PAIR]
    at = place // PAIR % 2
    at_array = at.reshape(1).astype(jnp.int32)
    order = jnp.arange(count, dtype=jnp.int32) ^ rank
    seqs = segments.shape[0]
    q_width, kv_width = w_query.shape[1], key_weight.shape[1]
    rows = count * share
    lane = Lane()


    def first_norm(layer_in, gain):
        x = layer_in.astype(WIDE)
        inverse = inverse_rms(x)
        return (x * inverse * gain.astype(WIDE)).astype(LOW), inverse

    n1_own, inverse_one = lane(first_norm, layer_in, gain_attn)
    n1_far, n1_near = swap(n1_own, "tensor", FAR), swap(n1_own, "tensor", NEAR)

    def prepare(segments, w_query, key_weight, value_weight, cotangent):
        tables = rope_tables(positions_of(segments).reshape(-1))
        w_qkv = jnp.concatenate([w_query, key_weight, value_weight], axis=1)
        seg_col, seg_row = segments.reshape(-1, 1), segments[:, None, :]
        branch_own = (RESIDUAL_SCALE * cotangent.astype(WIDE)).astype(LOW)
        return tables, w_qkv, seg_col, seg_row, branch_own

    tables, w_qkv, seg_col, seg_row, branch_own = lane(
        prepare, segments, w_query, key_weight, value_weight, cotangent
    )
    turned = q_width + kv_width
    qkv = lane(
        lambda a, b, order, w, c, s: project([a, b], order, w, rows, NN, turned, (c, s)),
        n1_own,
        n1_near,
        order[:2],
        w_qkv,
        *tables,
    )
    n1_other = swap(n1_far, "tensor", NEAR)
    branch_own = after(branch_own, n1_far)
    branch_chips = [
        branch_own,
        swap_both(branch_own),
        swap(branch_own, "tensor", FAR),
        swap(branch_own, "dp", PAIR),
    ]
    qkv = lane(
        lambda a, b, order, w, c, s, q: project([a, b], order, w, rows, NN, turned, (c, s), (q,)),
        n1_far,
        n1_other,
        order[2:],
        w_qkv,
        *tables,
        qkv,
    )
    attended, lse = lane(
        lambda q, c, r: attend(q, q_width, kv_width, c, r, seqs), qkv, seg_col, seg_row
    )
    parts = lane(lambda a, w, o: pieces(a, w, o, count, False), attended, w_out, order)
    got_near, got_other = swap(parts[1], "tensor", NEAR), swap(parts[3], "tensor", NEAR)
    sent = lane(lambda a, b: added(a, b).astype(LOW), parts[2], got_other)
    got_far = swap(sent, "tensor", FAR)

    branch_shares = [b for a in branch_chips for b in (a, swap(a, "tensor", NEAR))]
    d_mixed = lane(lambda a, w, at: branch(a, w, at), branch_shares, w_down, at_array)
    branch_spread = lane(lambda a: spread(a, 2 * rows, 0, group_masks, place), branch_shares)

    def second_norm(layer_in, mine, near, far, gain):
        hidden = layer_in.astype(WIDE) + RESIDUAL_SCALE * added(mine, near, far)
        inverse = inverse_rms(hidden)
        return hidden, inverse, (hidden * inverse * gain.astype(WIDE)).astype(LOW)

    hidden, inverse_two, n2_own = lane(
        second_norm, layer_in, parts[0], got_near, got_far, gain_ffn
    )
    n2_far, n2_pair = swap(n2_own, "tensor", FAR), swap(n2_own, "dp", PAIR)
    n2_own = [n2_own, swap(n2_own, "tensor", NEAR)]
    blend = lambda block: lambda a, g, u, d, at, *m: mix(a, g, u, d, at, block, m)
    scatter = lambda block: lambda a, *n: spread(a, 2 * rows, block, group_masks, place, *n)
    mixed = lane(blend(0), n2_own, w_gate, w_up, d_mixed, at_array)
    n2 = lane(scatter(0), n2_own)
    n2_far, n2_pair = after((n2_far, n2_pair), n2)
    n2_both = [swap(cut(n2_pair)[0], "tensor", FAR), swap(cut(n2_far)[1], "dp", PAIR)]
    n2_four = [n2_far, swap(n2_far, "tensor", NEAR), n2_pair, swap(n2_pair, "tensor", NEAR)]
    mixed = lane(blend(1), n2_four, w_gate, w_up, d_mixed, at_array, *mixed)
    n2 = lane(scatter(1), n2_four, n2)
    n2_both = n2_both + [swap(a, "tensor", NEAR) for a in n2_both]
    mixed, d_gate, d_upper = lane(blend(1), n2_both, w_gate, w_up, d_mixed, at_array, *mixed)

    grad_down = Reduction(mixed, branch_spread, group_masks, 1).step(lane)
    back = lambda block, pieces: lambda dg, du, wg, wu, at: unmix(
        dg, du, wg, wu, at, block, share, pieces
    )
    ffn = (d_gate, d_upper, w_gate, w_up, at_array)
    d_normed = GroupSum()
    dn_both = lane(back(1, 2), *ffn)
    dn_four = lane(back(1, 4), *ffn)
    d_normed.start_both(lane, dn_both)
    dn_own = lane(back(0, 2), *ffn)
    n2 = lane(
        lambda a, n: spread(a, 2 * rows, 1, group_masks, place, n), n2_both, n2
    )
    d_normed.start_far_pair(lane, dn_own, dn_four[:2], dn_four[2:])
    grad_gate = Reduction(n2, d_gate, group_masks, 0).step(lane)
    grad_down.step(lane)
    grad_up = Reduction(n2, d_upper, group_masks, 0).step(lane)
    ffn_parts = lane(lambda m, w, at: down(m, w, at, share), mixed, w_down, at_array)
    d_hidden, da_own, gain_two_part = lane(
        lambda c, h, i, g, *t: norm_back(c, h, i, g, t, WIDE),
        cotangent,
        hidden,
        inverse_two,
        gain_ffn,
        *d_normed.terms(),
    )
    da_far, da_near = swap(da_own, "tensor", FAR), swap(da_own, "tensor", NEAR)
    n1_shares = [n1_own, n1_near, n1_far, n1_other]
    natural = lambda a, o: spread(a, rows, 0, masks, place, None, o)
    n1 = lane(natural, n1_shares, order)
    grad_gate.step(lane)
    grad_down.step_half(lane)
    out_total = GroupSum()
    out_total.start_both(lane, ffn_parts[2:4])
    d_attn = lane(
        lambda a, b, o, w: project([a, b], o, w, rows, NT), da_own, da_near, order[:2], w_out
    )
    da_other = swap(after(da_far, d_attn), "tensor", NEAR)
    d_attn = lane(
        lambda a, b, o, w, d: project([a, b], o, w, rows, NT, given=(d,)),
        da_far,
        da_other,
        order[2:],
        w_out,
        d_attn,
    )
    out_total.start_far_pair(lane, ffn_parts[:2], ffn_parts[4:6], ffn_parts[6:8])

    d_qkv = lane(
        lambda q, g, l, c, r, a, b: attend_back(q, q_width, kv_width, g, l, c, r, a, b, seqs),
        qkv,
        d_attn,
        lse,
        seg_col,
        seg_row,
        *tables,
    )
    grad_gate.step_half(lane)
    out_rows = lane(
        lambda hidden, *terms: whole(
            lambda hidden, *terms: (hidden + RESIDUAL_SCALE * added(*terms),),
            [(hidden.shape, LOW)],
            hidden,
            *terms,
        )[0],
        hidden,
        *out_total.terms(),
    )
    parts = lane(lambda a, w, o: pieces(a, w, o, count, True), d_qkv, w_qkv, order)
    got_near, got_other = swap(parts[1], "tensor", NEAR), swap(parts[3], "tensor", NEAR)
    grad_qkv = Reduction(n1, d_qkv, masks, 0).step(lane)
    kept, sent = lane(
        lambda *a: whole(
            lambda a, b, c, d: (added(a, b), added(c, d)),
            [(a[0].shape, WIDE), (a[0].shape, LOW)],
            *a,
        ),
        parts[0],
        got_near,
        parts[2],
        got_other,
    )
    got_far = swap(sent, "tensor", FAR)
    grad_up.step(lane)
    grad_down = grad_down.finish_half(lane, at_array)
    da = lane(natural, [da_own, da_near, da_far, da_other], order)
    grad_wout = Reduction(attended, da, masks, 1).step(lane)
    grad_rows, _, gain_one_part = lane(
        lambda c, h, i, g, *t: norm_back(c, h, i, g, t, LOW),
        d_hidden,
        layer_in,
        inverse_one,
        gain_attn,
        kept,
        got_far,
    )
    grad_gate = grad_gate.finish_half(lane, at_array)
    grad_qkv.step(lane)
    grad_up.step_half(lane)
    grad_wout.step(lane)
    grad_qkv.step(lane)
    grad_up = grad_up.finish_half(lane, at_array)
    grad_wout.step(lane)
    grad_qkv = grad_qkv.finish(lane)
    grad_wout = grad_wout.finish(lane)
    steps = [("tensor", m) for m in powers(count)] + [("dp", m) for m in masks]
    gains = lane(
        lambda a, b: sum_all(jnp.concatenate([a, b], axis=0), steps), gain_one_part, gain_two_part
    )
    block = width // lax.axis_size("dp")
    gains = lax.dynamic_slice_in_dim(gains, place * block, block, 1)
    return (
        out_rows,
        grad_rows,
        gains[0],
        grad_qkv[:, :q_width],
        grad_qkv[:, q_width : q_width + kv_width],
        grad_qkv[:, q_width + kv_width :],
        grad_wout,
        gains[1],
        grad_gate,
        grad_up,
        grad_down,
    )


def solution(mesh):
    return jax.shard_map(
        body,
        mesh=mesh,
        in_specs=(
            P(("dp", "tensor"), None),
            P(("dp", "tensor"), None),
            P("dp", None),
            P(),
            P(None, "tensor"),
            P(None, "tensor"),
            P(None, "tensor"),
            P("tensor", None),
            P(),
            P(None, "tensor"),
            P(None, "tensor"),
            P("tensor", None),
        ),
        out_specs=(
            P(("dp", "tensor"), None),
            P(("dp", "tensor"), None),
            P("dp"),
            P("dp", "tensor"),
            P("dp", "tensor"),
            P("dp", "tensor"),
            P("tensor", "dp"),
            P("dp"),
            P("dp", "tensor"),
            P("dp", "tensor"),
            P("tensor", "dp"),
        ),
        check_vma=False,
    )
```

time: 736 us -> 605 us (0.82)
  Pallas kernels: 123 us -> 404 us
  waiting for transfers between devices: 345 us -> 84.4 us
  matrix products: 122 us -> 0 us
  other arithmetic: 67.1 us -> 17.5 us
  starting transfers between devices: 33.6 us -> 53.3 us
    pallas_call x6 -> x52, Pallas kernels: 75.8 us -> 357 us  [the longest x12 65.2 us: product_rows(): pl.pallas_call(kernel, grid=(tiles,), in_specs=[pl.BlockSpec((tokens, til...]
    ppermute x47 -> x58, waiting for transfers between devices: 345 us -> 83.9 us  [swap(): return lax.ppermute(array, axis, [(i, i ^ mask) for i in range(size)])]
    dot_general x38 -> x0, matrix products: 122 us -> none  [dot(): return lax.dot_general(a, b, dims, preferred_element_type=WIDE)]
    concatenate x19 -> x1, other arithmetic: 30.6 us -> 0.61 us  [body(): jnp.concatenate([a, b], axis=0)]
    ppermute x47 -> x58, starting transfers between devices: 33.6 us -> 52.8 us  [swap(): return lax.ppermute(array, axis, [(i, i ^ mask) for i in range(size)])]
    convert_element_type x12 -> x6, other arithmetic: 17.6 us -> 7.38 us  [the longest x2 3.19 us: first_norm(): return ((x * inverse * gain.astype(WIDE)).astype(LOW), inverse)]
    dynamic_slice x9 -> x0, local copies, waits for them, and re-layouts: 9.7 us -> none  [the longest x4 6.99 us: permute_columns(): lax.dynamic_slice_in_dim(array, (place ^ b) * width, width, 1)]
    reduce_sum x5 -> x0, other arithmetic: 8.86 us -> none  [the longest x4 6.37 us: body(): jnp.sum(d.astype(WIDE) * n.astype(WIDE), axis=0)]
  transfers between devices with their start and end apart: 47 -> 59, of which waited for: 20 -> 22; matrix products, arithmetic and copies ran while one was open for 24% -> 4% of each run, Pallas kernels for 12% -> 60%
where the time goes in v2:
time: 605 us; the launch traced here: 594 us
  Pallas kernels  404 us (67%)
  waiting for transfers between devices  84.4 us (14%)
  starting transfers between devices  53.3 us (9%)
  local copies, waits for them, and re-layouts  33.2 us (5%)
  other arithmetic  17.5 us (3%)
    ppermute x58, waiting for transfers between devices, swap(): return lax.ppermute(array, axis, [(i, i ^ mask) for i in range(size)])  83.9 us
    pallas_call x12, Pallas kernels, product_rows(): pl.pallas_call(kernel, grid=(tiles,), in_specs=[pl.BlockSpec((tokens, til...  65.2 us
    ppermute x58, starting transfers between devices, swap(): return lax.ppermute(array, axis, [(i, i ^ mask) for i in range(size)])  52.8 us
    pallas_call x6, Pallas kernels, spread(): pl.pallas_call(functools.partial(spread_kernel, count), grid_spec=pltpu.P...  45.5 us
    pallas_call x8, Pallas kernels, product_cols(): pl.pallas_call(kernel, grid=(down_to // tile,), in_specs=[pl.BlockSpec((t...  38.8 us
    pallas_call x3, Pallas kernels, mix(): pl.pallas_call(functools.partial(mix_kernel, count), grid_spec=pltpu.Pref...  37.4 us
    pallas_call x3, Pallas kernels, unmix(): pl.pallas_call(unmix_kernel, grid_spec=pltpu.PrefetchScalarGridSpec(num_s...  34.5 us
    pallas_call x4, Pallas kernels, project(): pl.pallas_call(functools.partial(project_kernel, count, turned, dims), gr...  27.2 us
  transfers between devices with their start and end apart: 59, of which 22 were waited for; matrix products, arithmetic and copies ran while one was open for 4% of the time, Pallas kernels for 60%

profile of v2, /device:TPU:16, one launch (start us, length us, event | category | flops | bytes accessed | tf_op | source)
XLA Modules:
  0.0 594.2 jit_solution(17993634654943886170)
XLA Ops:
  13.2 18.0 %collective-permute-done.refs_0_.refs_2_ = bf16[256,2048]{1,0:T(8,128)(2,1)} collective-permute-done((bf16[256,2048]{1,0:T(8,128)(2,1)}, bf16[256,2048]{1,0:T(8,128)(2,1)}, u32[]{:S(2)}, u32[]{:S(2)}) %collective-permute-start) | collective-permute-done | bytes 1048608 | tf_op jit(solution)/shard_map/ppermute | solution.py:713
  38.3 7.7 %project.4.refs_5_ = bf16[1024,768]{1,0:T(8,128)(2,1)} custom-call(s32[2]{0:T(128)} %get-tuple-element.513.order_ref, bf16[256,2048]{1,0:T(8,128)(2,1)} %fusion.2.refs_0_, bf16[256,2048]{1,0:T(8,128)(2,1)} %collective-permute-done.2.refs_1_, bf16[2048,768]{1,0:T(8,128)(2,1)} %copy-done, f32[1024,128]{1,0:T(8,128)} %get-tuple-element.539.refs_3_.cos_ref, ...), custom_call_target="tpu_custom_call" | custom-call | flops 1 | bytes 1 | tf_op jit(solution)/shard_map/project/pallas_call | solution.py:118
  45.9 7.5 %project.5.q_ref.k_ref.v_ref = bf16[1024,768]{1,0:T(8,128)(2,1)} custom-call(s32[2]{0:T(128)} %get-tuple-element.518.order_ref, bf16[256,2048]{1,0:T(8,128)(2,1)} %collective-permute-done.refs_0_.refs_2_, bf16[256,2048]{1,0:T(8,128)(2,1)} %collective-permute-done.1.refs_1_.refs_3_, bf16[2048,768]{1,0:T(8,128)(2,1)} %copy-done, ...), custom_call_target="tpu_custom_call", output_to_operand_aliasing={{}: (6, {})} | custom-call | flops 1 | bytes 1 | tf_op jit(solution)/shard_map/project/pallas_call | solution.py:118
  54.4 20.1 %attend.1 = (bf16[1024,512]{1,0:T(8,128)(2,1)}, f32[4,2,1024]{2,1,0:T(2,128)}) custom-call(bf16[1024,768]{1,0:T(8,128)(2,1)} %project.5.q_ref.k_ref.v_ref, bf16[1024,768]{1,0:T(8,128)(2,1)} %project.5.q_ref.k_ref.v_ref, bf16[1024,768]{1,0:T(8,128)(2,1)} %project.5.q_ref.k_ref.v_ref, s32[1024,1]{1,0:T(8,128)} %copy.44.segq_ref, s32[1,1,1024]{2,1,0:T(1,128)} %bitcast.19), custom_call_target="tpu_custom_call" | custom-call | flops 1 | bytes 1 | tf_op jit(solution)/shard_map/attend/pallas_call | solution.py:213
  74.5 8.3 %pieces.2 = (bf16[256,2048]{1,0:T(8,128)(2,1)}, bf16[256,2048]{1,0:T(8,128)(2,1)}, bf16[256,2048]{1,0:T(8,128)(2,1)}, bf16[256,2048]{1,0:T(8,128)(2,1)}) custom-call(s32[4]{0:T(128)} %copy-done.36, bf16[1024,512]{1,0:T(8,128)(2,1)} %get-tuple-element.626.a_ref.left_ref, bf16[512,2048]{1,0:T(8,128)(2,1)} %refs_2_.2), custom_call_target="tpu_custom_call" | custom-call | flops 1 | bytes 1 | tf_op jit(solution)/shard_map/pieces/pallas_call | solution.py:157
  94.1 15.8 %branch.1.refs_4_.refs_6_ = f32[2048,1024]{1,0:T(8,128)} custom-call(s32[1]{0:T(128)} %bitcast.7.at_ref, bf16[256,2048]{1,0:T(8,128)(2,1)} %multiply_convert_fusion.1.refs_0_, bf16[256,2048]{1,0:T(8,128)(2,1)} %copy-done.11, bf16[256,2048]{1,0:T(8,128)(2,1)} %collective-permute-done.7.refs_2_, bf16[256,2048]{1,0:T(8,128)(2,1)} %collective-permute-done.8.refs_3_, ...), custom_call_target="tpu_custom_call" | custom-call | flops 1 | bytes 1 | tf_op jit(solution)/shard_map/branch/pallas_call | solution.py:367
  110.6 9.9 %spread.6.right_ref = bf16[2048,2048]{1,0:T(8,128)(2,1)} custom-call(s32[8]{0:T(128)} %broadcast_xor_fusion.1.columns_ref, s32[8]{0:T(128)} %iota.32.rows_ref, bf16[256,2048]{1,0:T(8,128)(2,1)} %multiply_convert_fusion.1.refs_0_, bf16[256,2048]{1,0:T(8,128)(2,1)} %copy-done.11, bf16[256,2048]{1,0:T(8,128)(2,1)} %collective-permute-done.7.refs_2_, ...), custom_call_target="tpu_custom_call" | custom-call | flops 1 | bytes 1 | tf_op jit(solution)/shard_map/spread/pallas_call | solution.py:505
  127.7 10.7 %mix.3 = (bf16[2048,1024]{1,0:T(8,128)(2,1)}, bf16[2048,1024]{1,0:T(8,128)(2,1)}, bf16[2048,1024]{1,0:T(8,128)(2,1)}) custom-call(s32[1]{0:T(128)} %bitcast.7.at_ref, bf16[256,2048]{1,0:T(8,128)(2,1)} %copy-done.5, bf16[256,2048]{1,0:T(8,128)(2,1)} %copy-done.17, bf16[2048,2048]{1,0:T(8,128)(2,1)} %wg_ref.2, bf16[2048,2048]{1,0:T(8,128)(2,1)} %wu_ref.2, ...), custom_call_target="tpu_custom_call" | custom-call | flops 1 | bytes 1 | tf_op jit(solution)/shard_map/mix/pallas_call | solution.py:410
  138.9 6.9 %spread.7.refs_4_ = bf16[2048,2048]{1,0:T(8,128)(2,1)} custom-call(s32[8]{0:T(128)} %broadcast_xor_fusion.1.columns_ref, s32[2]{0:T(128)} %iota.33.rows_ref, bf16[256,2048]{1,0:T(8,128)(2,1)} %copy-done.5, bf16[256,2048]{1,0:T(8,128)(2,1)} %copy-done.17), custom_call_target="tpu_custom_call" | custom-call | flops 1 | bytes 1 | tf_op jit(solution)/shard_map/spread/pallas_call | solution.py:505
  155.3 10.6 %collective-permute-done.16.refs_0_ = bf16[128,2048]{1,0:T(8,128)(2,1)S(1)} collective-permute-done((bf16[128,2048]{1,0:T(8,128)(2,1)S(1)}, bf16[128,2048]{1,0:T(8,128)(2,1)S(1)}, u32[]{:S(2)}, u32[]{:S(2)}) %collective-permute-start.16) | collective-permute-done | bytes 524320 | tf_op jit(solution)/shard_map/ppermute | solution.py:713
  169.2 16.0 %mix.4 = (bf16[2048,1024]{1,0:T(8,128)(2,1)}, bf16[2048,1024]{1,0:T(8,128)(2,1)}, bf16[2048,1024]{1,0:T(8,128)(2,1)}) custom-call(s32[1]{0:T(128)} %bitcast.7.at_ref, bf16[256,2048]{1,0:T(8,128)(2,1)} %collective-permute-done.13.refs_0_, bf16[256,2048]{1,0:T(8,128)(2,1)} %copy-done.18, ...), custom_call_target="tpu_custom_call", output_to_operand_aliasing={{0}: (8, {}), {1}: (9, {}), {2}: (10, {})} | custom-call | flops 1 | bytes 1 | tf_op jit(solution)/shard_map/mix/pallas_call | solution.py:410
  185.8 7.4 %spread.8.refs_4_ = bf16[2048,2048]{1,0:T(8,128)(2,1)} custom-call(s32[8]{0:T(128)} %broadcast_xor_fusion.1.columns_ref, s32[4]{0:T(128)} %iota.34.rows_ref, bf16[256,2048]{1,0:T(8,128)(2,1)} %collective-permute-done.13.refs_0_, bf16[256,2048]{1,0:T(8,128)(2,1)} %copy-done.18, ...), custom_call_target="tpu_custom_call", output_to_operand_aliasing={{}: (6, {})} | custom-call | flops 1 | bytes 1 | tf_op jit(solution)/shard_map/spread/pallas_call | solution.py:505
  193.2 10.7 %mix.5 = (bf16[2048,1024]{1,0:T(8,128)(2,1)}, bf16[2048,1024]{1,0:T(8,128)(2,1)}, bf16[2048,1024]{1,0:T(8,128)(2,1)}) custom-call(s32[1]{0:T(128)} %bitcast.7.at_ref, bf16[128,2048]{1,0:T(8,128)(2,1)} %copy-done.22, bf16[128,2048]{1,0:T(8,128)(2,1)} %copy-done.23, ...), custom_call_target="tpu_custom_call", output_to_operand_aliasing={{0}: (8, {}), {1}: (9, {}), {2}: (10, {})} | custom-call | flops 1 | bytes 1 | tf_op jit(solution)/shard_map/mix/pallas_call | solution.py:410
  203.9 8.6 %product_cols.8 = bf16[1024,1024]{1,0:T(8,128)(2,1)} custom-call(bf16[2048,1024]{1,0:T(8,128)(2,1)} %get-tuple-element.567.left_ref.m_ref, bf16[2048,2048]{1,0:T(8,128)(2,1)} %spread.6.right_ref), custom_call_target="tpu_custom_call" | custom-call | flops 1 | bytes 1 | tf_op jit(solution)/shard_map/product_cols/pallas_call | solution.py:567
  212.6 10.3 %unmix.3 = (bf16[256,2048]{1,0:T(8,128)(2,1)}, bf16[256,2048]{1,0:T(8,128)(2,1)}) custom-call(s32[1]{0:T(128)} %bitcast.7.at_ref, bf16[2048,1024]{1,0:T(8,128)(2,1)} %get-tuple-element.590.dg_ref.right_ref, bf16[2048,1024]{1,0:T(8,128)(2,1)} %get-tuple-element.611.du_ref.right_ref, bf16[2048,2048]{1,0:T(8,128)(2,1)} %wg_ref.2, bf16[2048,2048]{1,0:T(8,128)(2,1)} %wu_ref.2), custom_call_target="tpu_custom_call" | custom-call | flops 1 | bytes 1 | tf_op jit(solution)/shard_map/unmix/pallas_call | solution.py:443
  223.4 13.9 %unmix.4 = (bf16[256,2048]{1,0:T(8,128)(2,1)}, bf16[256,2048]{1,0:T(8,128)(2,1)}, bf16[256,2048]{1,0:T(8,128)(2,1)}, bf16[256,2048]{1,0:T(8,128)(2,1)}) custom-call(s32[1]{0:T(128)} %bitcast.7.at_ref, bf16[2048,1024]{1,0:T(8,128)(2,1)} %get-tuple-element.590.dg_ref.right_ref, bf16[2048,1024]{1,0:T(8,128)(2,1)} %get-tuple-element.611.du_ref.right_ref, ...), custom_call_target="tpu_custom_call" | custom-call | flops 1 | bytes 1 | tf_op jit(solution)/shard_map/unmix/pallas_call | solution.py:443
  241.6 10.3 %unmix.5 = (bf16[256,2048]{1,0:T(8,128)(2,1)}, bf16[256,2048]{1,0:T(8,128)(2,1)}) custom-call(s32[1]{0:T(128)} %bitcast.7.at_ref, bf16[2048,1024]{1,0:T(8,128)(2,1)} %get-tuple-element.590.dg_ref.right_ref, bf16[2048,1024]{1,0:T(8,128)(2,1)} %get-tuple-element.611.du_ref.right_ref, bf16[2048,2048]{1,0:T(8,128)(2,1)} %wg_ref.2, bf16[2048,2048]{1,0:T(8,128)(2,1)} %wu_ref.2), custom_call_target="tpu_custom_call" | custom-call | flops 1 | bytes 1 | tf_op jit(solution)/shard_map/unmix/pallas_call | solution.py:443
  255.9 6.4 %spread.9.left_ref = bf16[2048,2048]{1,0:T(8,128)(2,1)} custom-call(s32[8]{0:T(128)} %broadcast_xor_fusion.1.columns_ref, s32[4]{0:T(128)} %iota.35.rows_ref, bf16[128,2048]{1,0:T(8,128)(2,1)} %copy-done.22, bf16[128,2048]{1,0:T(8,128)(2,1)} %copy-done.23, bf16[128,2048]{1,0:T(8,128)(2,1)} %collective-permute-done.18.refs_2_, ...), custom_call_target="tpu_custom_call", output_to_operand_aliasing={{}: (6, {})} | custom-call | flops 1 | bytes 1 | tf_op jit(solution)/shard_map/spread/pallas_call | solution.py:505
  262.3 4.3 collective-permute-done.26.refs_4_
  267.9 5.4 whole.7
  274.8 8.6 %product_rows.12 = bf16[1024,1024]{1,0:T(8,128)(2,1)} custom-call(bf16[2048,2048]{1,0:T(8,128)(2,1)} %spread.9.left_ref, bf16[2048,1024]{1,0:T(8,128)(2,1)} %get-tuple-element.590.dg_ref.right_ref), custom_call_target="tpu_custom_call" | custom-call | flops 1 | bytes 1 | tf_op jit(solution)/shard_map/product_rows/pallas_call | solution.py:537
  287.3 6.4 %product_cols.9 = bf16[1024,512]{1,0:T(8,128)(2,1)} custom-call(bf16[2048,1024]{1,0:T(8,128)(2,1)} %get-tuple-element.567.left_ref.m_ref, bf16[2048,2048]{1,0:T(8,128)(2,1)} %spread.6.right_ref, bf16[1024,1024]{1,0:T(8,128)(2,1)} %copy-done.2), custom_call_target="tpu_custom_call" | custom-call | flops 1 | bytes 1 | tf_op jit(solution)/shard_map/product_cols/pallas_call | solution.py:567
  293.7 8.7 %product_rows.13 = bf16[1024,1024]{1,0:T(8,128)(2,1)} custom-call(bf16[2048,2048]{1,0:T(8,128)(2,1)} %spread.9.left_ref, bf16[2048,1024]{1,0:T(8,128)(2,1)} %get-tuple-element.611.du_ref.right_ref), custom_call_target="tpu_custom_call" | custom-call | flops 1 | bytes 1 | tf_op jit(solution)/shard_map/product_rows/pallas_call | solution.py:537
  302.4 13.3 %down.1 = (bf16[256,2048]{1,0:T(8,128)(2,1)}, bf16[256,2048]{1,0:T(8,128)(2,1)}, bf16[256,2048]{1,0:T(8,128)(2,1)}, bf16[256,2048]{1,0:T(8,128)(2,1)}, bf16[256,...) custom-call(s32[1]{0:T(128)} %bitcast.7.at_ref, ...), custom_call_target="tpu_custom_call" | custom-call | flops 1 | bytes 1 | tf_op jit(solution)/shard_map/down/pallas_call | solution.py:468
  317.4 5.9 norm_back.2
  326.1 7.4 %spread.10.left_ref = bf16[1024,2048]{1,0:T(8,128)(2,1)} custom-call(s32[8]{0:T(128)} %broadcast_xor_fusion.columns_ref, s32[4]{0:T(128)} %copy-done.36, bf16[256,2048]{1,0:T(8,128)(2,1)} %fusion.2.refs_0_, bf16[256,2048]{1,0:T(8,128)(2,1)} %collective-permute-done.2.refs_1_, bf16[256,2048]{1,0:T(8,128)(2,1)} %collective-permute-done.refs_0_.refs_2_, ...), custom_call_target="tpu_custom_call" | custom-call | flops 1 | bytes 1 | tf_op jit(solution)/shard_map/spread/pallas_call | solution.py:505
  333.5 6.1 %product_rows.14 = bf16[512,1024]{1,0:T(8,128)(2,1)} custom-call(bf16[2048,2048]{1,0:T(8,128)(2,1)} %spread.9.left_ref, bf16[2048,1024]{1,0:T(8,128)(2,1)} %get-tuple-element.590.dg_ref.right_ref, bf16[1024,1024]{1,0:T(8,128)(2,1)} %collective-permute-done.33.refs_0_), custom_call_target="tpu_custom_call" | custom-call | flops 1 | bytes 1 | tf_op jit(solution)/shard_map/product_rows/pallas_call | solution.py:537
  340.6 5.3 product_cols.10
  349.6 6.0 %project.6.refs_3_ = bf16[1024,512]{1,0:T(8,128)(2,1)} custom-call(s32[2]{0:T(128)} %get-tuple-element.513.order_ref, bf16[256,2048]{1,0:T(8,128)(2,1)} %get-tuple-element.575.refs_0_, bf16[256,2048]{1,0:T(8,128)(2,1)} %copy-done.15, bf16[512,2048]{1,0:T(8,128)(2,1)} %refs_2_.2), custom_call_target="tpu_custom_call" | custom-call | flops 1 | bytes 1 | tf_op jit(solution)/shard_map/project/pallas_call | solution.py:118
  361.7 6.0 %project.7.g_ref = bf16[1024,512]{1,0:T(8,128)(2,1)} custom-call(s32[2]{0:T(128)} %get-tuple-element.518.order_ref, bf16[256,2048]{1,0:T(8,128)(2,1)} %copy-done.8, bf16[256,2048]{1,0:T(8,128)(2,1)} %copy-done.9, bf16[512,2048]{1,0:T(8,128)(2,1)} %refs_2_.2, bf16[1024,512]{1,0:T(8,128)(2,1)} %project.6.refs_3_), custom_call_target="tpu_custom_call", output_to_operand_aliasing={{}: (4, {})} | custom-call | flops 1 | bytes 1 | tf_op jit(solution)/shard_map/project/pallas_call | solution.py:118
  374.2 5.5 whole.9
  386.4 26.9 %attend_back.1.a_ref.right_ref = bf16[1024,768]{1,0:T(8,128)(2,1)} custom-call(bf16[1024,768]{1,0:T(8,128)(2,1)} %project.5.q_ref.k_ref.v_ref, bf16[1024,768]{1,0:T(8,128)(2,1)} %project.5.q_ref.k_ref.v_ref, bf16[1024,768]{1,0:T(8,128)(2,1)} %project.5.q_ref.k_ref.v_ref, bf16[1024,512]{1,0:T(8,128)(2,1)} %project.7.g_ref, ...), custom_call_target="tpu_custom_call" | custom-call | flops 1 | bytes 1 | tf_op jit(solution)/shard_map/attend_back/pallas_call | solution.py:326
  415.9 4.9 product_rows.15
  420.8 6.5 %collective-permute-done.43.refs_3_ = bf16[256,2048]{1,0:T(8,128)(2,1)} collective-permute-done((bf16[256,2048]{1,0:T(8,128)(2,1)}, bf16[256,2048]{1,0:T(8,128)(2,1)}, u32[]{:S(2)}, u32[]{:S(2)}) %collective-permute-start.43) | collective-permute-done | bytes 1048608 | tf_op jit(solution)/shard_map/ppermute | solution.py:713
  431.6 9.4 %pieces.3 = (bf16[256,2048]{1,0:T(8,128)(2,1)}, bf16[256,2048]{1,0:T(8,128)(2,1)}, bf16[256,2048]{1,0:T(8,128)(2,1)}, bf16[256,2048]{1,0:T(8,128)(2,1)}) custom-call(s32[4]{0:T(128)} %copy-done.36, bf16[1024,768]{1,0:T(8,128)(2,1)} %attend_back.1.a_ref.right_ref, bf16[2048,768]{1,0:T(8,128)(2,1)} %copy-done), custom_call_target="tpu_custom_call" | custom-call | flops 1 | bytes 1 | tf_op jit(solution)/shard_map/pieces/pallas_call | solution.py:157
  441.5 5.5 product_rows.16
  458.0 6.1 %product_rows.17 = bf16[512,1024]{1,0:T(8,128)(2,1)} custom-call(bf16[2048,2048]{1,0:T(8,128)(2,1)} %spread.9.left_ref, bf16[2048,1024]{1,0:T(8,128)(2,1)} %get-tuple-element.611.du_ref.right_ref, bf16[1024,1024]{1,0:T(8,128)(2,1)} %copy-done.3), custom_call_target="tpu_custom_call" | custom-call | flops 1 | bytes 1 | tf_op jit(solution)/shard_map/product_rows/pallas_call | solution.py:537
  464.5 5.5 product_cols.11.own_ref
  469.9 10.3 %collective-permute-done.49.other_ref = bf16[1024,256]{1,0:T(8,128)(2,1)} collective-permute-done((bf16[1024,256]{1,0:T(8,128)(2,1)}, bf16[1024,256]{1,0:T(8,128)(2,1)}, u32[]{:S(2)}, u32[]{:S(2)}) %collective-permute-start.49) | collective-permute-done | bytes 524320 | tf_op jit(solution)/shard_map/ppermute | solution.py:713
  483.1 7.5 %spread.11.right_ref = bf16[1024,2048]{1,0:T(8,128)(2,1)} custom-call(s32[8]{0:T(128)} %broadcast_xor_fusion.columns_ref, s32[4]{0:T(128)} %copy-done.36, bf16[256,2048]{1,0:T(8,128)(2,1)} %get-tuple-element.575.refs_0_, bf16[256,2048]{1,0:T(8,128)(2,1)} %copy-done.15, bf16[256,2048]{1,0:T(8,128)(2,1)} %copy-done.8, bf16[256,2048]{1,0:T(8,128)(2,1)} %copy-done.9), custom_call_target="tpu_custom_call" | custom-call | flops 1 | bytes 1 | tf_op jit(solution)/shard_map/spread/pallas_call | solution.py:505
  490.5 4.3 product_cols.12
  497.0 5.2 norm_back.3
  502.3 5.0 product_rows.18.own_ref
  517.3 4.9 product_rows.20
  528.4 10.5 %collective-permute-done.55.refs_1_ = bf16[512,768]{1,0:T(8,128)(2,1)S(1)} collective-permute-done((bf16[512,768]{1,0:T(8,128)(2,1)}, bf16[512,768]{1,0:T(8,128)(2,1)S(1)}, u32[]{:S(2)}, u32[]{:S(2)}) %collective-permute-start.55) | collective-permute-done | bytes 786464 | tf_op jit(solution)/shard_map/ppermute | solution.py:713
  542.9 4.5 collective-permute-start.58
  547.5 5.1 product_rows.22.own_ref
  575.2 17.4 %sum_all.1 = f32[2,2048]{1,0:T(2,128)} custom-call(f32[2,2048]{1,0:T(2,128)} %pad_maximum_fusion.2.part_ref), custom_call_target="tpu_custom_call" | custom-call | flops 1 | bytes 1 | tf_op jit(solution)/shard_map/sum_all/pallas_call | solution.py:691
  (258 shorter events, 164.6 us)
Async XLA Ops:
  5.4 32.9 %collective-permute-start.2 = (bf16[256,2048]{1,0:T(8,128)(2,1)}, bf16[256,2048]{1,0:T(8,128)(2,1)}, u32[]{:S(2)}, u32[]{:S(2)}) collective-permute-start(bf16[256,2048]{1,0:T(8,128)(2,1)} %fusion.2.refs_0_), channel_id=1, source_target_pairs={{0,1},{1,0},{2,3},{3,2},{4,5},{5,4},{6,7},{7,6},{8,9},{9,8},{10,11... | collective-permute-start | bytes 3145736 | tf_op jit(solution)/shard_map/ppermute | solution.py:713
  5.4 25.9 %collective-permute-start = (bf16[256,2048]{1,0:T(8,128)(2,1)}, bf16[256,2048]{1,0:T(8,128)(2,1)}, u32[]{:S(2)}, u32[]{:S(2)}) collective-permute-start(bf16[256,2048]{1,0:T(8,128)(2,1)} %fusion.2.refs_0_), channel_id=1, source_target_pairs={{0,2},{1,3},{2,0},{3,1},{4,6},{5,7},{6,4},{7,5},{8,10},{9,11},{10,... | collective-permute-start | bytes 3145736 | tf_op jit(solution)/shard_map/ppermute | solution.py:713
  31.3 14.7 %collective-permute-start.1 = (bf16[256,2048]{1,0:T(8,128)(2,1)}, bf16[256,2048]{1,0:T(8,128)(2,1)}, u32[]{:S(2)}, u32[]{:S(2)}) collective-permute-start(bf16[256,2048]{1,0:T(8,128)(2,1)} %collective-permute-done.refs_0_.refs_2_), channel_id=1, source_target_pairs={{0,1},{1,0},{2,3},{3,2},{4,5},{5,4},{6,7},{7,6},{8,9},{9,8},{10,11... | collective-permute-start | bytes 3145736 | tf_op jit(solution)/shard_map/ppermute | solution.py:713
  34.8 48.5 %collective-permute-start.9 = (bf16[256,2048]{1,0:T(8,128)(2,1)}, bf16[256,2048]{1,0:T(8,128)(2,1)}, u32[]{:S(2)}, u32[]{:S(2)}) collective-permute-start(bf16[256,2048]{1,0:T(8,128)(2,1)} %multiply_convert_fusion.1.refs_0_), channel_id=1, source_target_pairs={{0,2},{1,3},{2,0},{3,1},{4,6},{5,7},{6,4},{7,5},{8,10},{9,11},{10,... | collective-permute-start | bytes 3145736 | tf_op jit(solution)/shard_map/ppermute | solution.py:713
  36.3 47.1 %collective-permute-start.11 = (bf16[256,2048]{1,0:T(8,128)(2,1)}, bf16[256,2048]{1,0:T(8,128)(2,1)}, u32[]{:S(2)}, u32[]{:S(2)}) collective-permute-start(bf16[256,2048]{1,0:T(8,128)(2,1)} %multiply_convert_fusion.1.refs_0_), channel_id=1, source_target_pairs={{0,8},{4,12},{8,0},{12,4},{16,24},{20,28},{24,16},{28,20},{1,9},{5... | collective-permute-start | bytes 3145736 | tf_op jit(solution)/shard_map/ppermute | solution.py:713
  37.8 46.5 %collective-permute-start.7 = (bf16[256,2048]{1,0:T(8,128)(2,1)}, bf16[256,2048]{1,0:T(8,128)(2,1)}, u32[]{:S(2)}, u32[]{:S(2)}) collective-permute-start(bf16[256,2048]{1,0:T(8,128)(2,1)} %multiply_convert_fusion.1.refs_0_), channel_id=1, source_target_pairs={{0,10},{1,11},{2,8},{3,9},{4,14},{5,15},{6,12},{7,13},{8,2},{9,3},... | collective-permute-start | bytes 3145736 | tf_op jit(solution)/shard_map/ppermute | solution.py:724
  83.3 37.2 %collective-permute-start.3 = (bf16[256,2048]{1,0:T(8,128)(2,1)}, bf16[256,2048]{1,0:T(8,128)(2,1)}, u32[]{:S(2)}, u32[]{:S(2)}) collective-permute-start(bf16[256,2048]{1,0:T(8,128)(2,1)} %get-tuple-element.349), channel_id=1, source_target_pairs={{0,1},{1,0},{2,3},{3,2},{4,5},{5,4},{6,7},{7,6},{8,9},{9,8},{10,11... | collective-permute-start | bytes 3145736 | tf_op jit(solution)/shard_map/ppermute | solution.py:713
  88.7 31.8 %collective-permute-start.5 = (bf16[256,2048]{1,0:T(8,128)(2,1)}, bf16[256,2048]{1,0:T(8,128)(2,1)}, u32[]{:S(2)}, u32[]{:S(2)}) collective-permute-start(bf16[256,2048]{1,0:T(8,128)(2,1)} %add_convert_fusion), channel_id=1, source_target_pairs={{0,2},{1,3},{2,0},{3,1},{4,6},{5,7},{6,4},{7,5},{8,10},{9,11},{10,... | collective-permute-start | bytes 3145736 | tf_op jit(solution)/shard_map/ppermute | solution.py:713
  123.6 25.5 %collective-permute-start.13 = (bf16[256,2048]{1,0:T(8,128)(2,1)S(1)}, bf16[256,2048]{1,0:T(8,128)(2,1)}, u32[]{:S(2)}, u32[]{:S(2)}) collective-permute-start(bf16[256,2048]{1,0:T(8,128)(2,1)S(1)} %multiply_convert_fusion.refs_0_), channel_id=1, source_target_pairs={{0,2},{1,3},{2,0},{3,1},{4,6},{5,7},{6,4},{7,5},{8,10},{9,11},{10,... | collective-permute-start | bytes 3145736 | tf_op jit(solution)/shard_map/ppermute | solution.py:713
  125.1 25.2 %collective-permute-start.14 = (bf16[256,2048]{1,0:T(8,128)(2,1)S(1)}, bf16[256,2048]{1,0:T(8,128)(2,1)}, u32[]{:S(2)}, u32[]{:S(2)}) collective-permute-start(bf16[256,2048]{1,0:T(8,128)(2,1)S(1)} %multiply_convert_fusion.refs_0_), channel_id=1, source_target_pairs={{0,8},{4,12},{8,0},{12,4},{16,24},{20,28},{24,16},{28,20},{1,9},{5... | collective-permute-start | bytes 3145736 | tf_op jit(solution)/shard_map/ppermute | solution.py:713
  150.4 16.9 %collective-permute-start.20 = (bf16[256,2048]{1,0:T(8,128)(2,1)}, bf16[256,2048]{1,0:T(8,128)(2,1)S(1)}, u32[]{:S(2)}, u32[]{:S(2)}) collective-permute-start(bf16[256,2048]{1,0:T(8,128)(2,1)} %collective-permute-done.13.refs_0_), channel_id=1, source_target_pairs={{0,1},{1,0},{2,3},{3,2},{4,5},{5,4},{6,7},{7,6},{8,9},{9,8},{10,11... | collective-permute-start | bytes 3145736 | tf_op jit(solution)/shard_map/ppermute | solution.py:713
  150.4 16.9 %collective-permute-start.21 = (bf16[256,2048]{1,0:T(8,128)(2,1)}, bf16[256,2048]{1,0:T(8,128)(2,1)S(1)}, u32[]{:S(2)}, u32[]{:S(2)}) collective-permute-start(bf16[256,2048]{1,0:T(8,128)(2,1)} %collective-permute-done.14.refs_2_), channel_id=1, source_target_pairs={{0,1},{1,0},{2,3},{3,2},{4,5},{5,4},{6,7},{7,6},{8,9},{9,8},{10,11... | collective-permute-start | bytes 3145736 | tf_op jit(solution)/shard_map/ppermute | solution.py:713
  152.0 13.9 %collective-permute-start.16 = (bf16[128,2048]{1,0:T(8,128)(2,1)S(1)}, bf16[128,2048]{1,0:T(8,128)(2,1)S(1)}, u32[]{:S(2)}, u32[]{:S(2)}) collective-permute-start(bf16[128,2048]{1,0:T(8,128)(2,1)S(1)} %slice.47), channel_id=1, source_target_pairs={{0,2},{1,3},{2,0},{3,1},{4,6},{5,7},{6,4},{7,5},{8,10},{9,11},{10,... | collective-permute-start | bytes 1572872 | tf_op jit(solution)/shard_map/ppermute | solution.py:713
  153.6 13.6 %collective-permute-start.17 = (bf16[128,2048]{1,0:T(8,128)(2,1)S(1)}, bf16[128,2048]{1,0:T(8,128)(2,1)S(1)}, u32[]{:S(2)}, u32[]{:S(2)}) collective-permute-start(bf16[128,2048]{1,0:T(8,128)(2,1)S(1)} %slice.48), channel_id=1, source_target_pairs={{0,8},{4,12},{8,0},{12,4},{16,24},{20,28},{24,16},{28,20},{1,9},{5... | collective-permute-start | bytes 1572872 | tf_op jit(solution)/shard_map/ppermute | solution.py:713
  165.9 27.4 %collective-permute-start.18 = (bf16[128,2048]{1,0:T(8,128)(2,1)S(1)}, bf16[128,2048]{1,0:T(8,128)(2,1)}, u32[]{:S(2)}, u32[]{:S(2)}) collective-permute-start(bf16[128,2048]{1,0:T(8,128)(2,1)S(1)} %collective-permute-done.16.refs_0_), channel_id=1, source_target_pairs={{0,1},{1,0},{2,3},{3,2},{4,5},{5,4},{6,7},{7,6},{8,9},{9,8},{10,11... | collective-permute-start | bytes 1572872 | tf_op jit(solution)/shard_map/ppermute | solution.py:713
  167.3 26.0 %collective-permute-start.19 = (bf16[128,2048]{1,0:T(8,128)(2,1)S(1)}, bf16[128,2048]{1,0:T(8,128)(2,1)}, u32[]{:S(2)}, u32[]{:S(2)}) collective-permute-start(bf16[128,2048]{1,0:T(8,128)(2,1)S(1)} %collective-permute-done.17.refs_1_), channel_id=1, source_target_pairs={{0,1},{1,0},{2,3},{3,2},{4,5},{5,4},{6,7},{7,6},{8,9},{9,8},{10,11... | collective-permute-start | bytes 1572872 | tf_op jit(solution)/shard_map/ppermute | solution.py:713
  222.9 16.1 %collective-permute-start.22 = (bf16[256,2048]{1,0:T(8,128)(2,1)}, bf16[256,2048]{1,0:T(8,128)(2,1)}, u32[]{:S(2)}, u32[]{:S(2)}) collective-permute-start(bf16[256,2048]{1,0:T(8,128)(2,1)} %get-tuple-element.432), channel_id=1, source_target_pairs={{0,1},{1,0},{2,3},{3,2},{4,5},{5,4},{6,7},{7,6},{8,9},{9,8},{10,11... | collective-permute-start | bytes 3145736 | tf_op jit(solution)/shard_map/ppermute | solution.py:713
  237.2 16.6 %collective-permute-start.25 = (bf16[256,2048]{1,0:T(8,128)(2,1)}, bf16[256,2048]{1,0:T(8,128)(2,1)S(1)}, u32[]{:S(2)}, u32[]{:S(2)}) collective-permute-start(bf16[256,2048]{1,0:T(8,128)(2,1)} %get-tuple-element.439), channel_id=1, source_target_pairs={{0,1},{1,0},{2,3},{3,2},{4,5},{5,4},{6,7},{7,6},{8,9},{9,8},{10,11... | collective-permute-start | bytes 3145736 | tf_op jit(solution)/shard_map/ppermute | solution.py:713
  237.3 48.7 %collective-permute-start.23 = (bf16[1024,1024]{1,0:T(8,128)(2,1)}, bf16[1024,1024]{1,0:T(8,128)(2,1)S(1)}, u32[]{:S(2)}, u32[]{:S(2)}) collective-permute-start(bf16[1024,1024]{1,0:T(8,128)(2,1)} %product_cols.8), channel_id=1, source_target_pairs={{0,4},{4,0},{8,12},{12,8},{16,20},{20,16},{24,28},{28,24},{1,5},{5... | collective-permute-start | bytes 6291464 | tf_op jit(solution)/shard_map/ppermute | solution.py:713
  238.8 23.5 %collective-permute-start.27 = (bf16[256,2048]{1,0:T(8,128)(2,1)}, bf16[256,2048]{1,0:T(8,128)(2,1)}, u32[]{:S(2)}, u32[]{:S(2)}) collective-permute-start(bf16[256,2048]{1,0:T(8,128)(2,1)} %get-tuple-element.441), channel_id=1, source_target_pairs={{0,1},{1,0},{2,3},{3,2},{4,5},{5,4},{6,7},{7,6},{8,9},{9,8},{10,11... | collective-permute-start | bytes 3145736 | tf_op jit(solution)/shard_map/ppermute | solution.py:713
  251.9 16.0 %collective-permute-start.24 = (bf16[256,2048]{1,0:T(8,128)(2,1)}, bf16[256,2048]{1,0:T(8,128)(2,1)}, u32[]{:S(2)}, u32[]{:S(2)}) collective-permute-start(bf16[256,2048]{1,0:T(8,128)(2,1)} %get-tuple-element.452), channel_id=1, source_target_pairs={{0,1},{1,0},{2,3},{3,2},{4,5},{5,4},{6,7},{7,6},{8,9},{9,8},{10,11... | collective-permute-start | bytes 3145736 | tf_op jit(solution)/shard_map/ppermute | solution.py:713
  252.3 14.3 %collective-permute-start.26 = (bf16[128,2048]{1,0:T(8,128)(2,1)}, bf16[128,2048]{1,0:T(8,128)(2,1)}, u32[]{:S(2)}, u32[]{:S(2)}) collective-permute-start(bf16[128,2048]{1,0:T(8,128)(2,1)} %get-tuple-element.445), channel_id=1, source_target_pairs={{0,8},{4,12},{8,0},{12,4},{16,24},{20,28},{24,16},{28,20},{1,9},{5... | collective-permute-start | bytes 1572872 | tf_op jit(solution)/shard_map/ppermute | solution.py:713
  253.9 14.0 %collective-permute-start.28 = (bf16[128,2048]{1,0:T(8,128)(2,1)}, bf16[128,2048]{1,0:T(8,128)(2,1)}, u32[]{:S(2)}, u32[]{:S(2)}) collective-permute-start(bf16[128,2048]{1,0:T(8,128)(2,1)} %get-tuple-element.444), channel_id=1, source_target_pairs={{0,2},{1,3},{2,0},{3,1},{4,6},{5,7},{6,4},{7,5},{8,10},{9,11},{10,... | collective-permute-start | bytes 1572872 | tf_op jit(solution)/shard_map/ppermute | solution.py:713
  273.3 42.5 %collective-permute-start.34 = (bf16[256,2048]{1,0:T(8,128)(2,1)}, bf16[256,2048]{1,0:T(8,128)(2,1)S(1)}, u32[]{:S(2)}, u32[]{:S(2)}) collective-permute-start(bf16[256,2048]{1,0:T(8,128)(2,1)} %get-tuple-element.467), channel_id=1, source_target_pairs={{0,2},{1,3},{2,0},{3,1},{4,6},{5,7},{6,4},{7,5},{8,10},{9,11},{10,... | collective-permute-start | bytes 3145736 | tf_op jit(solution)/shard_map/ppermute | solution.py:713
  283.4 50.1 %collective-permute-start.33 = (bf16[1024,1024]{1,0:T(8,128)(2,1)}, bf16[1024,1024]{1,0:T(8,128)(2,1)}, u32[]{:S(2)}, u32[]{:S(2)}) collective-permute-start(bf16[1024,1024]{1,0:T(8,128)(2,1)} %product_rows.12), channel_id=1, source_target_pairs={{0,4},{4,0},{8,12},{12,8},{16,20},{20,16},{24,28},{28,24},{1,5},{5... | collective-permute-start | bytes 6291464 | tf_op jit(solution)/shard_map/ppermute | solution.py:713
  283.9 31.9 %collective-permute-start.35 = (bf16[256,2048]{1,0:T(8,128)(2,1)}, bf16[256,2048]{1,0:T(8,128)(2,1)}, u32[]{:S(2)}, u32[]{:S(2)}) collective-permute-start(bf16[256,2048]{1,0:T(8,128)(2,1)} %get-tuple-element.468), channel_id=1, source_target_pairs={{0,8},{4,12},{8,0},{12,4},{16,24},{20,28},{24,16},{28,20},{1,9},{5... | collective-permute-start | bytes 3145736 | tf_op jit(solution)/shard_map/ppermute | solution.py:713
  293.7 45.9 %collective-permute-start.32 = (bf16[1024,512]{1,0:T(8,128)(2,1)}, bf16[1024,512]{1,0:T(8,128)(2,1)S(1)}, u32[]{:S(2)}, u32[]{:S(2)}) collective-permute-start(bf16[1024,512]{1,0:T(8,128)(2,1)} %product_cols.9), channel_id=1, source_target_pairs={{0,16},{4,20},{8,24},{12,28},{16,0},{20,4},{24,8},{28,12},{1,17},{... | collective-permute-start | bytes 3145736 | tf_op jit(solution)/shard_map/ppermute | solution.py:713
  315.8 30.2 %collective-permute-start.31 = (bf16[256,2048]{1,0:T(8,128)(2,1)}, bf16[256,2048]{1,0:T(8,128)(2,1)}, u32[]{:S(2)}, u32[]{:S(2)}) collective-permute-start(bf16[256,2048]{1,0:T(8,128)(2,1)} %get-tuple-element.484), channel_id=1, source_target_pairs={{0,1},{1,0},{2,3},{3,2},{4,5},{5,4},{6,7},{7,6},{8,9},{9,8},{10,11... | collective-permute-start | bytes 3145736 | tf_op jit(solution)/shard_map/ppermute | solution.py:713
  323.3 25.3 %collective-permute-start.40 = (bf16[256,2048]{1,0:T(8,128)(2,1)}, bf16[256,2048]{1,0:T(8,128)(2,1)S(1)}, u32[]{:S(2)}, u32[]{:S(2)}) collective-permute-start(bf16[256,2048]{1,0:T(8,128)(2,1)} %get-tuple-element.575.refs_0_), channel_id=1, source_target_pairs={{0,1},{1,0},{2,3},{3,2},{4,5},{5,4},{6,7},{7,6},{8,9},{9,8},{10,11... | collective-permute-start | bytes 3145736 | tf_op jit(solution)/shard_map/ppermute | solution.py:713
  323.8 31.8 %collective-permute-start.39 = (bf16[256,2048]{1,0:T(8,128)(2,1)}, bf16[256,2048]{1,0:T(8,128)(2,1)S(1)}, u32[]{:S(2)}, u32[]{:S(2)}) collective-permute-start(bf16[256,2048]{1,0:T(8,128)(2,1)} %get-tuple-element.575.refs_0_), channel_id=1, source_target_pairs={{0,2},{1,3},{2,0},{3,1},{4,6},{5,7},{6,4},{7,5},{8,10},{9,11},{10,... | collective-permute-start | bytes 3145736 | tf_op jit(solution)/shard_map/ppermute | solution.py:713
  356.2 13.4 %collective-permute-start.30 = (bf16[256,2048]{1,0:T(8,128)(2,1)}, bf16[256,2048]{1,0:T(8,128)(2,1)}, u32[]{:S(2)}, u32[]{:S(2)}) collective-permute-start(bf16[256,2048]{1,0:T(8,128)(2,1)} %get-tuple-element.482), channel_id=1, source_target_pairs={{0,1},{1,0},{2,3},{3,2},{4,5},{5,4},{6,7},{7,6},{8,9},{9,8},{10,11... | collective-permute-start | bytes 3145736 | tf_op jit(solution)/shard_map/ppermute | solution.py:713
  356.3 13.3 %collective-permute-start.37 = (bf16[256,2048]{1,0:T(8,128)(2,1)}, bf16[256,2048]{1,0:T(8,128)(2,1)}, u32[]{:S(2)}, u32[]{:S(2)}) collective-permute-start(bf16[256,2048]{1,0:T(8,128)(2,1)} %get-tuple-element.486), channel_id=1, source_target_pairs={{0,1},{1,0},{2,3},{3,2},{4,5},{5,4},{6,7},{7,6},{8,9},{9,8},{10,11... | collective-permute-start | bytes 3145736 | tf_op jit(solution)/shard_map/ppermute | solution.py:713
  356.7 16.6 %collective-permute-start.36 = (bf16[128,2048]{1,0:T(8,128)(2,1)}, bf16[128,2048]{1,0:T(8,128)(2,1)}, u32[]{:S(2)}, u32[]{:S(2)}) collective-permute-start(bf16[128,2048]{1,0:T(8,128)(2,1)} %get-tuple-element.511), channel_id=1, source_target_pairs={{0,8},{4,12},{8,0},{12,4},{16,24},{20,28},{24,16},{28,20},{1,9},{5... | collective-permute-start | bytes 1572872 | tf_op jit(solution)/shard_map/ppermute | solution.py:713
  360.3 13.9 %collective-permute-start.38 = (bf16[128,2048]{1,0:T(8,128)(2,1)}, bf16[128,2048]{1,0:T(8,128)(2,1)}, u32[]{:S(2)}, u32[]{:S(2)}) collective-permute-start(bf16[128,2048]{1,0:T(8,128)(2,1)} %get-tuple-element.512), channel_id=1, source_target_pairs={{0,2},{1,3},{2,0},{3,1},{4,6},{5,7},{6,4},{7,5},{8,10},{9,11},{10,... | collective-permute-start | bytes 1572872 | tf_op jit(solution)/shard_map/ppermute | solution.py:713
  367.8 47.2 %collective-permute-start.44 = (bf16[512,1024]{1,0:T(8,128)(2,1)}, bf16[512,1024]{1,0:T(8,128)(2,1)S(1)}, u32[]{:S(2)}, u32[]{:S(2)}) collective-permute-start(bf16[512,1024]{1,0:T(8,128)(2,1)} %product_rows.14), channel_id=1, source_target_pairs={{0,16},{4,20},{8,24},{12,28},{16,0},{20,4},{24,8},{28,12},{1,17},{... | collective-permute-start | bytes 3145736 | tf_op jit(solution)/shard_map/ppermute | solution.py:713
  379.7 41.1 %collective-permute-start.42 = (bf16[256,2048]{1,0:T(8,128)(2,1)}, bf16[256,2048]{1,0:T(8,128)(2,1)}, u32[]{:S(2)}, u32[]{:S(2)}) collective-permute-start(bf16[256,2048]{1,0:T(8,128)(2,1)} %get-tuple-element.532), channel_id=1, source_target_pairs={{0,2},{1,3},{2,0},{3,1},{4,6},{5,7},{6,4},{7,5},{8,10},{9,11},{10,... | collective-permute-start | bytes 3145736 | tf_op jit(solution)/shard_map/ppermute | solution.py:713
  381.2 46.2 %collective-permute-start.43 = (bf16[256,2048]{1,0:T(8,128)(2,1)}, bf16[256,2048]{1,0:T(8,128)(2,1)}, u32[]{:S(2)}, u32[]{:S(2)}) collective-permute-start(bf16[256,2048]{1,0:T(8,128)(2,1)} %get-tuple-element.533), channel_id=1, source_target_pairs={{0,8},{4,12},{8,0},{12,4},{16,24},{20,28},{24,16},{28,20},{1,9},{5... | collective-permute-start | bytes 3145736 | tf_op jit(solution)/shard_map/ppermute | solution.py:713
  383.9 72.8 %collective-permute-start.48 = (bf16[1024,1024]{1,0:T(8,128)(2,1)}, bf16[1024,1024]{1,0:T(8,128)(2,1)S(1)}, u32[]{:S(2)}, u32[]{:S(2)}) collective-permute-start(bf16[1024,1024]{1,0:T(8,128)(2,1)} %product_rows.13), channel_id=1, source_target_pairs={{0,4},{4,0},{8,12},{12,8},{16,20},{20,16},{24,28},{28,24},{1,5},{5... | collective-permute-start | bytes 6291464 | tf_op jit(solution)/shard_map/ppermute | solution.py:713
  446.9 63.2 %collective-permute-start.52 = (bf16[1024,768]{1,0:T(8,128)(2,1)}, bf16[1024,768]{1,0:T(8,128)(2,1)}, u32[]{:S(2)}, u32[]{:S(2)}) collective-permute-start(bf16[1024,768]{1,0:T(8,128)(2,1)} %product_rows.16), channel_id=1, source_target_pairs={{0,4},{4,0},{8,12},{12,8},{16,20},{20,16},{24,28},{28,24},{1,5},{5... | collective-permute-start | bytes 4718600 | tf_op jit(solution)/shard_map/ppermute | solution.py:713
  453.5 42.0 %collective-permute-start.47 = (bf16[256,2048]{1,0:T(8,128)(2,1)}, bf16[256,2048]{1,0:T(8,128)(2,1)S(1)}, u32[]{:S(2)}, u32[]{:S(2)}) collective-permute-start(bf16[256,2048]{1,0:T(8,128)(2,1)} %get-tuple-element.563), channel_id=1, source_target_pairs={{0,2},{1,3},{2,0},{3,1},{4,6},{5,7},{6,4},{7,5},{8,10},{9,11},{10,... | collective-permute-start | bytes 3145736 | tf_op jit(solution)/shard_map/ppermute | solution.py:713
  454.1 26.1 %collective-permute-start.49 = (bf16[1024,256]{1,0:T(8,128)(2,1)}, bf16[1024,256]{1,0:T(8,128)(2,1)}, u32[]{:S(2)}, u32[]{:S(2)}) collective-permute-start(bf16[1024,256]{1,0:T(8,128)(2,1)} %product_cols.10), channel_id=1, source_target_pairs={{0,8},{4,12},{8,0},{12,4},{16,24},{20,28},{24,16},{28,20},{1,9},{5... | collective-permute-start | bytes 1572872 | tf_op jit(solution)/shard_map/ppermute | solution.py:713
  456.6 50.7 %collective-permute-start.53 = (bf16[256,1024]{1,0:T(8,128)(2,1)}, bf16[256,1024]{1,0:T(8,128)(2,1)}, u32[]{:S(2)}, u32[]{:S(2)}) collective-permute-start(bf16[256,1024]{1,0:T(8,128)(2,1)} %product_rows.15), channel_id=1, source_target_pairs={{0,8},{4,12},{8,0},{12,4},{16,24},{20,28},{24,16},{28,20},{1,9},{5... | collective-permute-start | bytes 1572872 | tf_op jit(solution)/shard_map/ppermute | solution.py:713
  464.1 52.3 %collective-permute-start.51 = (bf16[512,1024]{1,0:T(8,128)(2,1)}, bf16[512,1024]{1,0:T(8,128)(2,1)S(1)}, u32[]{:S(2)}, u32[]{:S(2)}) collective-permute-start(bf16[512,1024]{1,0:T(8,128)(2,1)} %product_rows.17), channel_id=1, source_target_pairs={{0,16},{4,20},{8,24},{12,28},{16,0},{20,4},{24,8},{28,12},{1,17},{... | collective-permute-start | bytes 3145736 | tf_op jit(solution)/shard_map/ppermute | solution.py:713
  494.8 27.4 %collective-permute-start.50 = (bf16[512,1024]{1,0:T(8,128)(2,1)}, bf16[512,1024]{1,0:T(8,128)(2,1)S(1)}, u32[]{:S(2)}, u32[]{:S(2)}) collective-permute-start(bf16[512,1024]{1,0:T(8,128)(2,1)} %product_cols.12), channel_id=1, source_target_pairs={{0,4},{4,0},{8,12},{12,8},{16,20},{20,16},{24,28},{28,24},{1,5},{5... | collective-permute-start | bytes 3145736 | tf_op jit(solution)/shard_map/ppermute | solution.py:713
  513.9 25.0 %collective-permute-start.55 = (bf16[512,768]{1,0:T(8,128)(2,1)}, bf16[512,768]{1,0:T(8,128)(2,1)S(1)}, u32[]{:S(2)}, u32[]{:S(2)}) collective-permute-start(bf16[512,768]{1,0:T(8,128)(2,1)} %product_rows.19), channel_id=1, source_target_pairs={{0,8},{4,12},{8,0},{12,4},{16,24},{20,28},{24,16},{28,20},{1,9},{5... | collective-permute-start | bytes 2359304 | tf_op jit(solution)/shard_map/ppermute | solution.py:713
  522.2 31.2 %collective-permute-start.56 = (bf16[256,1024]{1,0:T(8,128)(2,1)}, bf16[256,1024]{1,0:T(8,128)(2,1)S(1)}, u32[]{:S(2)}, u32[]{:S(2)}) collective-permute-start(bf16[256,1024]{1,0:T(8,128)(2,1)} %product_rows.20), channel_id=1, source_target_pairs={{0,8},{4,12},{8,0},{12,4},{16,24},{20,28},{24,16},{28,20},{1,9},{5... | collective-permute-start | bytes 1572872 | tf_op jit(solution)/shard_map/ppermute | solution.py:713
  526.3 32.7 %collective-permute-start.54 = (bf16[512,512]{1,0:T(8,128)(2,1)}, bf16[512,512]{1,0:T(8,128)(2,1)S(1)}, u32[]{:S(2)}, u32[]{:S(2)}) collective-permute-start(bf16[512,512]{1,0:T(8,128)(2,1)} %product_cols.13), channel_id=1, source_target_pairs={{0,8},{4,12},{8,0},{12,4},{16,24},{20,28},{24,16},{28,20},{1,9},{5... | collective-permute-start | bytes 1572872 | tf_op jit(solution)/shard_map/ppermute | solution.py:713
  542.9 19.9 %collective-permute-start.58 = (bf16[256,768]{1,0:T(8,128)(2,1)}, bf16[256,768]{1,0:T(8,128)(2,1)S(1)}, u32[]{:S(2)}, u32[]{:S(2)}) collective-permute-start(bf16[256,768]{1,0:T(8,128)(2,1)} %product_rows.21), channel_id=1, source_target_pairs={{0,16},{4,20},{8,24},{12,28},{16,0},{20,4},{24,8},{28,12},{1,17},{... | collective-permute-start | bytes 1179656 | tf_op jit(solution)/shard_map/ppermute | solution.py:713
  (56 other events, 310.2 us)

commit v3 on v2

--- a/solution.py
+++ b/solution.py
@@ -19,10 +19,24 @@
 WIDE = jnp.float32
 LANES = 128
 TILE = 256
+WIDE_TILE = 512
+
+NEAR, FAR, PAIR = 1, 2, 2
 NN = (((1,), (0,)), ((), ()))
 NT = (((1,), (1,)), ((), ()))
 TN = (((0,), (0,)), ((), ()))
 COST = pl.CostEstimate(flops=1, bytes_accessed=1, transcendentals=0)
+IDS = {
+    "sum_all": 0,
+    "near_in": 1,
+    "far_in": 2,
+    "near_back": 3,
+    "far_back": 4,
+    "out_pieces": 5,
+    "in_pieces": 6,
+    "unmix": 7,
+    "down": 8,
+}
 
 
 def dot(a, b, dims=NN):
@@ -93,17 +107,46 @@
     return sum(a.shape[0] for a in shares)
 
 
-def project_kernel(count, turned, dims, order_ref, *refs):
-    share_refs, w_ref, tables = refs[:count], refs[count], refs[count + 1 : count + 3]
-    out_ref, held, sems = refs[-3:]
-    share = out_ref.shape[0]
-
-    @pl.when(pl.program_id(0) == 0)
+def near_core():
+    mine = lax.axis_index("tensor")
+    return {"tensor": mine + NEAR * (1 - 2 * (mine // NEAR % 2))}
+
+
+def meet(partner):
+    barrier = pltpu.get_barrier_semaphore()
+    pl.semaphore_signal(barrier, inc=1, device_id=partner, device_id_type=pl.DeviceIdType.MESH)
+    pl.semaphore_wait(barrier, 1)
+
+
+def project_kernel(turned, dims, order_ref, share_ref, w_ref, *refs):
+    tables = refs[:2]
+    out_ref, other_ref, held, sems = refs[-4:]
+    i, partner = pl.program_id(0), near_core()
+    load = pltpu.make_async_copy(share_ref, held.at[0], sems.at[0])
+    send = pltpu.make_async_remote_copy(
+        src_ref=share_ref,
+        dst_ref=other_ref,
+        send_sem=sems.at[1],
+        recv_sem=sems.at[2],
+        device_id=partner,
+        device_id_type=pl.DeviceIdType.MESH,
+    )
+    load_other = pltpu.make_async_copy(other_ref, held.at[1], sems.at[3])
+
+    @pl.when(i == 0)
     def _():
-        load_shares(share_refs, held, sems)
-
-    mine = held[pl.ds(pl.multiple_of(pl.program_id(0) * share, share), share), :]
-    out = dot(mine, w_ref[...], dims)
+        load.start()
+        meet(partner)
+        send.start()
+        load.wait()
+
+    @pl.when(i == 1)
+    def _():
+        send.wait()
+        load_other.start()
+        load_other.wait()
+
+    out = dot(held[i], w_ref[...], dims)
     for j in range(out.shape[1] // LANES):
         part = out[:, j * LANES : (j + 1) * LANES]
         if j * LANES < turned:
@@ -111,61 +154,146 @@
         out_ref[:, j * LANES : (j + 1) * LANES] = part.astype(LOW)
 
 
-def project(shares, order, weight, rows, dims, turned=0, tables=(), given=()):
-    count, (share, width) = len(shares), shares[0].shape
+def project(own, order, weight, rows, dims, name, turned=0, tables=(), given=()):
+    share, width = own.shape
     columns = weight.shape[1] if dims is NN else weight.shape[0]
-    moving = lambda i, order: (order[i], 0)
+
+    def moving(i, *_):
+        mine = lax.axis_index("tensor")
+        if "far" in name:
+            mine = mine + FAR * (1 - 2 * (mine // FAR % 2))
+        return mine + NEAR * (1 - 2 * (mine // NEAR % 2)) * i, 0
+
     return pl.pallas_call(
-        functools.partial(project_kernel, count, turned, dims),
+        functools.partial(project_kernel, turned, dims),
         grid_spec=pltpu.PrefetchScalarGridSpec(
             num_scalar_prefetch=1,
-            grid=(count,),
-            in_specs=[pl.BlockSpec(memory_space=pl.ANY)] * count
+            grid=(2,),
+            in_specs=[pl.BlockSpec(memory_space=pl.ANY)]
             + [pl.BlockSpec(weight.shape, lambda i, order: (0, 0))]
             + [pl.BlockSpec((share, LANES), moving)] * len(tables)
             + [pl.BlockSpec(memory_space=pl.ANY)] * len(given),
-            out_specs=pl.BlockSpec((share, columns), moving),
+            out_specs=[pl.BlockSpec((share, columns), moving), pl.BlockSpec(memory_space=pl.ANY)],
             scratch_shapes=[
-                pltpu.VMEM((count * share, width), LOW),
-                pltpu.SemaphoreType.DMA((count,)),
+                pltpu.VMEM((2, share, width), LOW),
+                pltpu.SemaphoreType.DMA((4,)),
             ],
         ),
-        out_shape=jax.ShapeDtypeStruct((rows, columns), LOW),
-        input_output_aliases={count + 2 + len(tables): 0} if given else {},
+        out_shape=[
+            jax.ShapeDtypeStruct((rows, columns), LOW),
+            jax.ShapeDtypeStruct(own.shape, LOW),
+        ],
+        input_output_aliases={3 + len(tables): 0} if given else {},
+        compiler_params=pltpu.CompilerParams(collective_id=IDS[name], has_side_effects=True),
         cost_estimate=COST,
-        name="project",
-    )(order, *shares, weight, *tables, *given)
-
-
-def pieces_kernel(dims, order_ref, a_ref, w_ref, *out_refs):
-    w = w_ref[...]
-    for i, ref in enumerate(out_refs):
-        share = ref.shape[0]
-        mine = a_ref[pl.ds(pl.multiple_of(order_ref[i] * share, share), share), :]
-        ref[...] = dot(mine, w, dims).astype(LOW)
-
-
-def pieces(a, weight, order, count, transposed):
+        name=name,
+    )(order, own, weight, *tables, *given)
+
+
+def paired_kernel(compute, count, share, *refs):
+    half = count // 2
+    got_refs, sent, send_sems, got_sems = refs[-3 - half : -3], *refs[-3:]
+    mine_refs = refs[-3 - 2 * half : -3 - half]
+    i, steps, partner = pl.program_id(0), pl.num_programs(0), near_core()
+    tile = mine_refs[0].shape[1]
+
+    def copy(step, k):
+        columns = pl.ds(pl.multiple_of(step * tile, tile), tile)
+        return pltpu.make_async_remote_copy(
+            src_ref=sent.at[step % 2, k],
+            dst_ref=got_refs[k].at[:, columns],
+            send_sem=send_sems.at[step % 2, k],
+            recv_sem=got_sems.at[step, k],
+            device_id=partner,
+            device_id_type=pl.DeviceIdType.MESH,
+        )
+
+    @pl.when(i == 0)
+    def _():
+        meet(partner)
+
+    total = compute(refs[: -3 - 2 * half])
+    for k in range(half):
+        mine_refs[k][...] = total[2 * k * share : (2 * k + 1) * share].astype(LOW)
+
+    @pl.when(i >= 2)
+    def _():
+        for k in range(half):
+            copy(i - 2, k).wait_send()
+
+    for k in range(half):
+        sent[i % 2, k] = total[(2 * k + 1) * share : (2 * k + 2) * share].astype(LOW)
+
+    @pl.when(i >= 1)
+    def _():
+        for k in range(half):
+            copy(i - 1, k).start()
+
+    @pl.when(i == steps - 1)
+    def _():
+        for k in range(half):
+            copy(i, k).start()
+        for k in range(half):
+            copy(i - 1, k).wait_send()
+            copy(i, k).wait_send()
+
+        def arrived(step, carry):
+            for k in range(half):
+                copy(step, k).wait_recv()
+            return carry
+
+        lax.fori_loop(0, steps, arrived, 0)
+
+
+def paired(compute, name, count, share, width, tile, in_specs, prefetch, *operands):
+    half, steps = count // 2, width // tile
+    piece = jax.ShapeDtypeStruct((share, width), LOW)
+    results = pl.pallas_call(
+        functools.partial(paired_kernel, compute, count, share),
+        grid_spec=pltpu.PrefetchScalarGridSpec(
+            num_scalar_prefetch=1,
+            grid=(steps,),
+            in_specs=in_specs,
+            out_specs=[pl.BlockSpec((share, tile), lambda i, *_: (0, i))] * half
+            + [pl.BlockSpec(memory_space=pl.ANY)] * half,
+            scratch_shapes=[
+                pltpu.VMEM((2, half, share, tile), LOW),
+                pltpu.SemaphoreType.DMA((2, half)),
+                pltpu.SemaphoreType.DMA((steps, half)),
+            ],
+        ),
+        out_shape=[piece] * (2 * half),
+        compiler_params=pltpu.CompilerParams(collective_id=IDS[name], has_side_effects=True),
+        cost_estimate=COST,
+        name=name,
+    )(prefetch, *operands)
+    return list(zip(results[:half], results[half:]))
+
+
+def pieces(a, weight, order, count, dims, name):
     rows, depth = a.shape
     share = rows // count
-    width = weight.shape[0] if transposed else weight.shape[1]
+    width = weight.shape[1] if dims is NN else weight.shape[0]
+    tile = WIDE_TILE
     moving = (
-        pl.BlockSpec((TILE, depth), lambda i, order: (i, 0))
-        if transposed
-        else pl.BlockSpec((depth, TILE), lambda i, order: (0, i))
-    )
-    return pl.pallas_call(
-        functools.partial(pieces_kernel, NT if transposed else NN),
-        grid_spec=pltpu.PrefetchScalarGridSpec(
-            num_scalar_prefetch=1,
-            grid=(width // TILE,),
-            in_specs=[pl.BlockSpec((rows, depth), lambda i, order: (0, 0)), moving],
-            out_specs=[pl.BlockSpec((share, TILE), lambda i, order: (0, i))] * count,
-        ),
-        out_shape=[jax.ShapeDtypeStruct((share, width), LOW)] * count,
-        cost_estimate=COST,
-        name="pieces",
-    )(order, a, weight)
+        pl.BlockSpec((depth, tile), lambda i, *_: (0, i))
+        if dims is NN
+        else pl.BlockSpec((tile, depth), lambda i, *_: (i, 0))
+    )
+
+    def compute(refs):
+        _, a_ref, w_ref = refs
+        parts = []
+        for i in range(count):
+            block = lax.axis_index("tensor")
+            for mask in powers(count):
+                if i & mask:
+                    block = block + mask * (1 - 2 * (block // mask % 2))
+            parts.append(a_ref[pl.ds(pl.multiple_of(block * share, share), share), :])
+        return dot(jnp.concatenate(parts, axis=0), w_ref[...], dims)
+
+    given = pl.BlockSpec((rows, depth), lambda i, *_: (0, 0))
+    return paired(compute, name, count, share, width, tile, [given, moving], order, a, weight)
 
 
 def doubled(pair, half):
@@ -428,155 +556,152 @@
     )(at, *shares, wg, wu, dm, *given)
 
 
-def unmix_kernel(at_ref, dg_ref, du_ref, wg_ref, wu_ref, *out_refs):
-    total = dot(dg_ref[...], wg_ref[...], NT) + dot(du_ref[...], wu_ref[...], NT)
-    share = out_refs[0].shape[0]
-    for i, ref in enumerate(out_refs):
-        ref[...] = total[i * share : (i + 1) * share].astype(LOW)
-
-
-def unmix(dg, du, wg, wu, at, block, share, pieces):
-    units, width = dg.shape[1], wg.shape[0]
-    rows = share * pieces
-    given = pl.BlockSpec((rows, units), lambda i, at: (block, 0))
-    moving = pl.BlockSpec((TILE, units), lambda i, at: (i, at[0]))
-    return pl.pallas_call(
-        unmix_kernel,
-        grid_spec=pltpu.PrefetchScalarGridSpec(
-            num_scalar_prefetch=1,
-            grid=(width // TILE,),
-            in_specs=[given, given, moving, moving],
-            out_specs=[pl.BlockSpec((share, TILE), lambda i, at: (0, i))] * pieces,
-        ),
-        out_shape=[jax.ShapeDtypeStruct((share, width), LOW)] * pieces,
-        cost_estimate=COST,
-        name="unmix",
-    )(at, dg, du, wg, wu)
-
-
-def down_kernel(at_ref, m_ref, w_ref, *out_refs):
-    total = dot(m_ref[...], w_ref[...])
-    share = out_refs[0].shape[0]
-    for i, ref in enumerate(out_refs):
-        ref[...] = total[i * share : (i + 1) * share].astype(LOW)
+def unmix(dg, du, wg, wu, at, share):
+    (rows, units), width = dg.shape, wg.shape[0]
+    given = pl.BlockSpec((rows, units), lambda i, *_: (0, 0))
+    moving = pl.BlockSpec((WIDE_TILE, units), lambda i, *_: (i, lax.axis_index("dp") // PAIR % 2))
+
+    def compute(refs):
+        _, dg_ref, du_ref, wg_ref, wu_ref = refs
+        return dot(dg_ref[...], wg_ref[...], NT) + dot(du_ref[...], wu_ref[...], NT)
+
+    specs = [given, given, moving, moving]
+    return paired(compute, "unmix", rows // share, share, width, WIDE_TILE, specs, at, dg, du, wg, wu)
 
 
 def down(m, w_down, at, share):
     rows, units = m.shape
+    given = pl.BlockSpec((rows, units), lambda i, *_: (0, 0))
+    moving = pl.BlockSpec((units, WIDE_TILE), lambda i, *_: (lax.axis_index("dp") // PAIR % 2, i))
+
+    def compute(refs):
+        _, m_ref, w_ref = refs
+        return dot(m_ref[...], w_ref[...])
+
     width = w_down.shape[1]
-    pieces = rows // share
+    return paired(compute, "down", rows // share, share, width, WIDE_TILE, [given, moving], at, m, w_down)
+
+
+class Shares:
+    def __init__(self, shares, masks, place, order=None):
+        self.shares, self.rows = list(shares), rows_in(shares)
+        self.masks, self.place = masks, place
+        self.blocks = jnp.array(block_order(masks), jnp.int32) ^ place
+        sizes = [a.shape[0] for a in self.shares]
+        if order is None:
+            self.starts = jnp.array([sum(sizes[:i]) for i in range(len(sizes))], jnp.int32)
+        else:
+            self.starts = order * sizes[0]
+        self.shape = (self.rows, self.shares[0].shape[1])
+
+    def array(self):
+        whole = jnp.zeros(self.shape, LOW)
+        for i, a in enumerate(self.shares):
+            piece = permute_columns(a, self.masks, self.place)
+            whole = lax.dynamic_update_slice_in_dim(whole, piece, self.starts[i], 0)
+        return whole
+
+
+def block_copies(refs, starts_ref, blocks_ref, held, sems, low, width, j):
+    source = pl.ds(pl.multiple_of(blocks_ref[low + j] * width, width), width)
+    target = pl.ds(pl.multiple_of(j * width, width), width)
+    for i, ref in enumerate(refs):
+        first = pl.ds(pl.multiple_of(starts_ref[i], ref.shape[0]), ref.shape[0])
+        yield pltpu.make_async_copy(ref.at[:, source], held.at[first, target], sems.at[j, i])
+
+
+def product_rows(shares, starts, blocks, right, given, low, size, width, kind):
+    count = len(shares)
+    tokens, across = right.shape
+
+    def kernel(starts_ref, blocks_ref, *refs):
+        share_refs, right_ref, given_refs = refs[:count], refs[count], refs[count + 1 : -3]
+        out_ref, held, sems = refs[-3:]
+        i = pl.program_id(0)
+        copies = functools.partial(block_copies, share_refs, starts_ref, blocks_ref, held, sems, low, width)
+
+        @pl.when(i == 0)
+        def _():
+            for j in range(size):
+                for copy in copies(j):
+                    copy.start()
+
+        for copy in copies(i):
+            copy.wait()
+        value = dot(held[:, pl.ds(pl.multiple_of(i * width, width), width)], right_ref[...], TN)
+        for ref in given_refs:
+            value = value + ref[...].astype(WIDE)
+        out_ref[...] = value.astype(kind)
+
     return pl.pallas_call(
-        down_kernel,
-        grid_spec=pltpu.PrefetchScalarGridSpec(
-            num_scalar_prefetch=1,
-            grid=(width // TILE,),
-            in_specs=[
-                pl.BlockSpec((rows, units), lambda i, at: (0, 0)),
-                pl.BlockSpec((units, TILE), lambda i, at: (at[0], i)),
-            ],
-            out_specs=[pl.BlockSpec((share, TILE), lambda i, at: (0, i))] * pieces,
-        ),
-        out_shape=[jax.ShapeDtypeStruct((share, width), LOW)] * pieces,
-        cost_estimate=COST,
-        name="down",
-    )(at, m, w_down)
-
-
-def spread_kernel(count, columns_ref, rows_ref, *refs):
-    out_ref = refs[-1]
-    share = refs[0].shape[0]
-    for i in range(count):
-        out_ref[pl.ds(pl.multiple_of(rows_ref[i] * share, share), share), :] = refs[i][...]
-
-
-def spread(shares, rows, block, masks, place, given=None, order=None):
-    count, (share, width) = len(shares), shares[0].shape
-    blocks = jnp.array(block_order(masks), jnp.int32) ^ place
-    order = jnp.arange(count, dtype=jnp.int32) if order is None else order
-    columns = width // (1 << len(masks))
-    if columns % LANES:
-        whole = jnp.zeros((rows, width), LOW) if given is None else given
-        for i, a in enumerate(shares):
-            piece = permute_columns(a, masks, place)
-            first = (block * count + order[i]) * share
-            whole = lax.dynamic_update_slice_in_dim(whole, piece, first, 0)
-        return whole
-    extra = [] if given is None else [given]
-    return pl.pallas_call(
-        functools.partial(spread_kernel, count),
+        kernel,
         grid_spec=pltpu.PrefetchScalarGridSpec(
             num_scalar_prefetch=2,
-            grid=(width // columns,),
-            in_specs=[pl.BlockSpec((share, columns), lambda i, blocks, order: (0, blocks[i]))] * count
-            + [pl.BlockSpec(memory_space=pl.ANY)] * len(extra),
-            out_specs=pl.BlockSpec((count * share, columns), lambda i, blocks, order: (block, i)),
+            grid=(size,),
+            in_specs=[pl.BlockSpec(memory_space=pl.ANY)] * count
+            + [pl.BlockSpec((tokens, across), lambda i, *_: (0, 0))]
+            + [
+                pl.BlockSpec((width, across), lambda i, *_, start=low - first: (start + i, 0))
+                for first, _ in given
+            ],
+            out_specs=pl.BlockSpec((width, across), lambda i, *_: (i, 0)),
+            scratch_shapes=[
+                pltpu.VMEM((tokens, size * width), LOW),
+                pltpu.SemaphoreType.DMA((size, count)),
+            ],
         ),
-        out_shape=jax.ShapeDtypeStruct((rows, width), LOW),
-        input_output_aliases={count + 2: 0} if extra else {},
-        cost_estimate=COST,
-        name="spread",
-    )(blocks, order, *shares, *extra)
-
-
-def product_rows(left, right, given, low, size, width, kind):
-    tokens, across = right.shape
-    tile = min(TILE, size * width)
-    tiles = size * width // tile
-
-    def kernel(left_ref, right_ref, *refs):
-        value = dot(left_ref[...], right_ref[...], TN)
-        for ref in refs[:-1]:
-            value = value + ref[...].astype(WIDE)
-        refs[-1][...] = value.astype(kind)
-
-    def at(first):
-        start = (low - first) * width // tile
-        return lambda i: (start + i, 0)
-
-    start = low * width // tile
-    return pl.pallas_call(
-        kernel,
-        grid=(tiles,),
-        in_specs=[
-            pl.BlockSpec((tokens, tile), lambda i: (0, start + i)),
-            pl.BlockSpec((tokens, across), lambda i: (0, 0)),
-        ]
-        + [pl.BlockSpec((tile, across), at(first)) for first, _ in given],
-        out_specs=pl.BlockSpec((tile, across), lambda i: (i, 0)),
         out_shape=jax.ShapeDtypeStruct((size * width, across), kind),
         cost_estimate=COST,
         name="product_rows",
-    )(left, right, *(array for _, array in given))
-
-
-def product_cols(left, right, given, low, size, width, kind):
+    )(starts, blocks, *shares, right, *(array for _, array in given))
+
+
+def product_cols(shares, starts, blocks, left, given, low, size, width, kind):
+    count = len(shares)
     tokens, down_to = left.shape
     across = size * width
     tile = min(TILE, down_to)
 
-    def kernel(left_ref, right_ref, *refs):
-        value = dot(left_ref[...], right_ref[...], TN)
-        for ref in refs[:-1]:
+    def kernel(starts_ref, blocks_ref, *refs):
+        share_refs, left_ref, given_refs = refs[:count], refs[count], refs[count + 1 : -3]
+        out_ref, held, sems = refs[-3:]
+        copies = functools.partial(block_copies, share_refs, starts_ref, blocks_ref, held, sems, low, width)
+
+        @pl.when(pl.program_id(0) == 0)
+        def _():
+            for j in range(size):
+                for copy in copies(j):
+                    copy.start()
+            for j in range(size):
+                for copy in copies(j):
+                    copy.wait()
+
+        value = dot(left_ref[...], held[...], TN)
+        for ref in given_refs:
             value = value + ref[...].astype(WIDE)
-        refs[-1][...] = value.astype(kind)
-
-    def at(first):
-        start = (low - first) // size
-        return lambda i: (i, start)
+        out_ref[...] = value.astype(kind)
 
     return pl.pallas_call(
         kernel,
-        grid=(down_to // tile,),
-        in_specs=[
-            pl.BlockSpec((tokens, tile), lambda i: (0, i)),
-            pl.BlockSpec((tokens, across), lambda i: (0, low // size)),
-        ]
-        + [pl.BlockSpec((tile, across), at(first)) for first, _ in given],
-        out_specs=pl.BlockSpec((tile, across), lambda i: (i, 0)),
+        grid_spec=pltpu.PrefetchScalarGridSpec(
+            num_scalar_prefetch=2,
+            grid=(down_to // tile,),
+            in_specs=[pl.BlockSpec(memory_space=pl.ANY)] * count
+            + [pl.BlockSpec((tokens, tile), lambda i, *_: (0, i))]
+            + [
+                pl.BlockSpec((tile, across), lambda i, *_, start=(low - first) // size: (i, start))
+                for first, _ in given
+            ],
+            out_specs=pl.BlockSpec((tile, across), lambda i, *_: (i, 0)),
+            scratch_shapes=[
+                pltpu.VMEM((tokens, across), LOW),
+                pltpu.SemaphoreType.DMA((size, count)),
+            ],
+        ),
         out_shape=jax.ShapeDtypeStruct((down_to, across), kind),
         cost_estimate=COST,
         name="product_cols",
-    )(left, right, *(array for _, array in given))
+    )(starts, blocks, *shares, left, *(array for _, array in given))
 
 
 def half_kernel(axis, at_ref, own_ref, other_ref, out_ref):
@@ -699,13 +824,10 @@
             pltpu.SemaphoreType.DMA((count,)),
             pltpu.SemaphoreType.DMA((count,)),
         ],
-        compiler_params=pltpu.CompilerParams(collective_id=0, has_side_effects=True),
+        compiler_params=pltpu.CompilerParams(collective_id=IDS["sum_all"], has_side_effects=True),
         cost_estimate=COST,
         name="sum_all",
     )(part)
-
-
-NEAR, FAR, PAIR = 1, 2, 2
 
 
 def swap(array, axis, mask):
@@ -746,17 +868,11 @@
 
 
 class GroupSum:
-    def near(self, *chips):
-        return [swap(chip[1], "tensor", NEAR) for chip in chips]
-
     def start_both(self, lane, both):
-        (got,) = self.near(both)
-        low, high = lane(joined, both[0], got)
+        low, high = lane(joined, *both)
         self.low, self.high = swap(low, "tensor", FAR), swap(high, "dp", PAIR)
 
     def start_far_pair(self, lane, own, far, pair):
-        got_own, got_far, got_pair = self.near(own, far, pair)
-
         def relay(own, got_own, far, got_far, high, pair, got_pair, low):
             far, pair = added(far, got_far), added(pair, got_pair)
             rows = low.shape[0]
@@ -766,13 +882,10 @@
 
         self.own, far, pair = lane(
             functools.partial(whole, relay, [(own[0].shape, kind) for kind in (WIDE, LOW, LOW)]),
-            own[0],
-            got_own,
-            far[0],
-            got_far,
+            *own,
+            *far,
             self.high,
-            pair[0],
-            got_pair,
+            *pair,
             self.low,
         )
         self.far, self.pair = swap(far, "tensor", FAR), swap(pair, "dp", PAIR)
@@ -801,23 +914,30 @@
 
 
 class Reduction:
-    def __init__(self, left, right, masks, axis):
-        self.left, self.right, self.masks, self.axis = left, right, list(masks), axis
+    def __init__(self, shares, other, masks, axis):
+        self.shares, self.other_side, self.masks, self.axis = shares, other, list(masks), axis
         self.count = 1 << len(masks)
-        self.width = (right if axis else left).shape[1] // self.count
+        self.width = shares.shape[1] // self.count
         self.low, self.size, self.got = 0, self.count // 2, []
 
     def total(self, lane, low, high):
         firsts = [first for first, _ in self.got]
         width, axis = self.width, self.axis
         kind = WIDE if high == self.count else LOW
-
-        def compute(left, right, *arrays):
-            if (high - low) * width % LANES == 0:
+        arrays = [array for _, array in self.got]
+        if width % LANES == 0:
+
+            def compute(shares, starts, blocks, other, *arrays):
                 product = product_cols if axis else product_rows
-                return product(left, right, list(zip(firsts, arrays)), low, high - low, width, kind)
-            part = slice(low * width, high * width)
-            value = dot(left, right[:, part], TN) if axis else dot(left[:, part], right, TN)
+                given = list(zip(firsts, arrays))
+                return product(shares, starts, blocks, other, given, low, high - low, width, kind)
+
+            source = self.shares
+            return lane(compute, source.shares, source.starts, source.blocks, self.other_side, *arrays)
+
+        def compute(whole, other, *arrays):
+            part = whole[:, low * width : high * width]
+            value = dot(other, part, TN) if axis else dot(part, other, TN)
             for first, array in zip(firsts, arrays):
                 piece = lax.slice_in_dim(
                     array, (low - first) * width, (high - first) * width, axis=axis
@@ -825,7 +945,7 @@
                 value = value + piece.astype(WIDE)
             return value.astype(kind)
 
-        return lane(compute, self.left, self.right, *(array for _, array in self.got))
+        return lane(compute, self.shares.array(), self.other_side, *arrays)
 
     def step(self, lane):
         sent = self.total(lane, self.low, self.low + self.size)
@@ -844,12 +964,12 @@
             self.step(lane)
         sent = self.total(lane, self.low, self.low + self.size)
         self.low += self.size
-        self.other = swap(sent, "dp", self.masks.pop(0))
+        self.partner = swap(sent, "dp", self.masks.pop(0))
         return self
 
     def finish_half(self, lane, at):
         own = self.total(lane, self.low, self.count)
-        return lane(lambda a, b, at: halves(a, b, at, 1 - self.axis), own, self.other, at)
+        return lane(lambda a, b, at: halves(a, b, at, 1 - self.axis), own, self.partner, at)
 
 
 def rows_of(shares):
@@ -895,7 +1015,7 @@
         return (x * inverse * gain.astype(WIDE)).astype(LOW), inverse
 
     n1_own, inverse_one = lane(first_norm, layer_in, gain_attn)
-    n1_far, n1_near = swap(n1_own, "tensor", FAR), swap(n1_own, "tensor", NEAR)
+    n1_far = swap(n1_own, "tensor", FAR)
 
     def prepare(segments, w_query, key_weight, value_weight, cotangent):
         tables = rope_tables(positions_of(segments).reshape(-1))
@@ -908,15 +1028,14 @@
         prepare, segments, w_query, key_weight, value_weight, cotangent
     )
     turned = q_width + kv_width
-    qkv = lane(
-        lambda a, b, order, w, c, s: project([a, b], order, w, rows, NN, turned, (c, s)),
+    qkv, n1_near = lane(
+        lambda a, order, w, c, s: project(a, order, w, rows, NN, "near_in", turned, (c, s)),
         n1_own,
-        n1_near,
         order[:2],
         w_qkv,
         *tables,
     )
-    n1_other = swap(n1_far, "tensor", NEAR)
+    n1_far = after(n1_far, qkv)
     branch_own = after(branch_own, n1_far)
     branch_chips = [
         branch_own,
@@ -924,10 +1043,9 @@
         swap(branch_own, "tensor", FAR),
         swap(branch_own, "dp", PAIR),
     ]
-    qkv = lane(
-        lambda a, b, order, w, c, s, q: project([a, b], order, w, rows, NN, turned, (c, s), (q,)),
+    qkv, n1_other = lane(
+        lambda a, order, w, c, s, q: project(a, order, w, rows, NN, "far_in", turned, (c, s), (q,)),
         n1_far,
-        n1_other,
         order[2:],
         w_qkv,
         *tables,
@@ -936,14 +1054,14 @@
     attended, lse = lane(
         lambda q, c, r: attend(q, q_width, kv_width, c, r, seqs), qkv, seg_col, seg_row
     )
-    parts = lane(lambda a, w, o: pieces(a, w, o, count, False), attended, w_out, order)
-    got_near, got_other = swap(parts[1], "tensor", NEAR), swap(parts[3], "tensor", NEAR)
-    sent = lane(lambda a, b: added(a, b).astype(LOW), parts[2], got_other)
-    got_far = swap(sent, "tensor", FAR)
-
+    own_terms, far_terms = lane(
+        lambda a, w, o: pieces(a, w, o, count, NN, "out_pieces"), attended, w_out, order
+    )
+    got_far = swap(lane(add_low, *far_terms), "tensor", FAR)
+
+    branch_chips = after(tuple(branch_chips), *lane.last)
     branch_shares = [b for a in branch_chips for b in (a, swap(a, "tensor", NEAR))]
     d_mixed = lane(lambda a, w, at: branch(a, w, at), branch_shares, w_down, at_array)
-    branch_spread = lane(lambda a: spread(a, 2 * rows, 0, group_masks, place), branch_shares)
 
     def second_norm(layer_in, mine, near, far, gain):
         hidden = layer_in.astype(WIDE) + RESIDUAL_SCALE * added(mine, near, far)
@@ -951,39 +1069,36 @@
         return hidden, inverse, (hidden * inverse * gain.astype(WIDE)).astype(LOW)
 
     hidden, inverse_two, n2_own = lane(
-        second_norm, layer_in, parts[0], got_near, got_far, gain_ffn
+        second_norm, layer_in, *own_terms, got_far, gain_ffn
     )
     n2_far, n2_pair = swap(n2_own, "tensor", FAR), swap(n2_own, "dp", PAIR)
     n2_own = [n2_own, swap(n2_own, "tensor", NEAR)]
     blend = lambda block: lambda a, g, u, d, at, *m: mix(a, g, u, d, at, block, m)
-    scatter = lambda block: lambda a, *n: spread(a, 2 * rows, block, group_masks, place, *n)
     mixed = lane(blend(0), n2_own, w_gate, w_up, d_mixed, at_array)
-    n2 = lane(scatter(0), n2_own)
-    n2_far, n2_pair = after((n2_far, n2_pair), n2)
+    n2_far, n2_pair = after((n2_far, n2_pair), mixed)
     n2_both = [swap(cut(n2_pair)[0], "tensor", FAR), swap(cut(n2_far)[1], "dp", PAIR)]
     n2_four = [n2_far, swap(n2_far, "tensor", NEAR), n2_pair, swap(n2_pair, "tensor", NEAR)]
     mixed = lane(blend(1), n2_four, w_gate, w_up, d_mixed, at_array, *mixed)
-    n2 = lane(scatter(1), n2_four, n2)
+    n2_both = list(after(tuple(n2_both), *lane.last))
     n2_both = n2_both + [swap(a, "tensor", NEAR) for a in n2_both]
     mixed, d_gate, d_upper = lane(blend(1), n2_both, w_gate, w_up, d_mixed, at_array, *mixed)
 
-    grad_down = Reduction(mixed, branch_spread, group_masks, 1).step(lane)
-    back = lambda block, pieces: lambda dg, du, wg, wu, at: unmix(
-        dg, du, wg, wu, at, block, share, pieces
-    )
-    ffn = (d_gate, d_upper, w_gate, w_up, at_array)
+    n2 = Shares(n2_own + n2_both + n2_four, group_masks, place)
+    grad_down = Reduction(Shares(branch_shares, group_masks, place), mixed, group_masks, 1).step(lane)
+    dn_parts = lane(
+        lambda dg, du, wg, wu, at: unmix(dg, du, wg, wu, at, share),
+        d_gate,
+        d_upper,
+        w_gate,
+        w_up,
+        at_array,
+    )
     d_normed = GroupSum()
-    dn_both = lane(back(1, 2), *ffn)
-    dn_four = lane(back(1, 4), *ffn)
-    d_normed.start_both(lane, dn_both)
-    dn_own = lane(back(0, 2), *ffn)
-    n2 = lane(
-        lambda a, n: spread(a, 2 * rows, 1, group_masks, place, n), n2_both, n2
-    )
-    d_normed.start_far_pair(lane, dn_own, dn_four[:2], dn_four[2:])
+    d_normed.start_both(lane, dn_parts[1])
     grad_gate = Reduction(n2, d_gate, group_masks, 0).step(lane)
+    d_normed.start_far_pair(lane, dn_parts[0], dn_parts[2], dn_parts[3])
+    grad_up = Reduction(n2, d_upper, group_masks, 0).step(lane)
     grad_down.step(lane)
-    grad_up = Reduction(n2, d_upper, group_masks, 0).step(lane)
     ffn_parts = lane(lambda m, w, at: down(m, w, at, share), mixed, w_down, at_array)
     d_hidden, da_own, gain_two_part = lane(
         lambda c, h, i, g, *t: norm_back(c, h, i, g, t, WIDE),
@@ -993,28 +1108,23 @@
         gain_ffn,
         *d_normed.terms(),
     )
-    da_far, da_near = swap(da_own, "tensor", FAR), swap(da_own, "tensor", NEAR)
+    da_far = swap(da_own, "tensor", FAR)
     n1_shares = [n1_own, n1_near, n1_far, n1_other]
-    natural = lambda a, o: spread(a, rows, 0, masks, place, None, o)
-    n1 = lane(natural, n1_shares, order)
+    n1 = Shares(n1_shares, masks, place, order)
+    d_attn, da_near = lane(
+        lambda a, o, w: project(a, o, w, rows, NT, "near_back"), da_own, order[:2], w_out
+    )
     grad_gate.step(lane)
-    grad_down.step_half(lane)
-    out_total = GroupSum()
-    out_total.start_both(lane, ffn_parts[2:4])
-    d_attn = lane(
-        lambda a, b, o, w: project([a, b], o, w, rows, NT), da_own, da_near, order[:2], w_out
-    )
-    da_other = swap(after(da_far, d_attn), "tensor", NEAR)
-    d_attn = lane(
-        lambda a, b, o, w, d: project([a, b], o, w, rows, NT, given=(d,)),
+    d_attn, da_other = lane(
+        lambda a, o, w, d: project(a, o, w, rows, NT, "far_back", given=(d,)),
         da_far,
-        da_other,
         order[2:],
         w_out,
         d_attn,
     )
-    out_total.start_far_pair(lane, ffn_parts[:2], ffn_parts[4:6], ffn_parts[6:8])
-
+    out_total = GroupSum()
+    out_total.start_both(lane, ffn_parts[1])
+    grad_down.step_half(lane)
     d_qkv = lane(
         lambda q, g, l, c, r, a, b: attend_back(q, q_width, kv_width, g, l, c, r, a, b, seqs),
         qkv,
@@ -1024,7 +1134,29 @@
         seg_row,
         *tables,
     )
+    grad_qkv = Reduction(n1, d_qkv, masks, 0).step(lane)
+    grad_up.step(lane)
+    out_total.start_far_pair(lane, ffn_parts[0], ffn_parts[2], ffn_parts[3])
+    own_terms, far_terms = lane(
+        lambda a, w, o: pieces(a, w, o, count, NT, "in_pieces"), d_qkv, w_qkv, order
+    )
+    got_far = swap(lane(add_low, *far_terms), "tensor", FAR)
     grad_gate.step_half(lane)
+    grad_down = grad_down.finish_half(lane, at_array)
+    grad_rows, _, gain_one_part = lane(
+        lambda c, h, i, g, *t: norm_back(c, h, i, g, t, LOW),
+        d_hidden,
+        layer_in,
+        inverse_one,
+        gain_attn,
+        *own_terms,
+        got_far,
+    )
+    grad_gate = grad_gate.finish_half(lane, at_array)
+    grad_qkv.step(lane)
+    da = Shares([da_own, da_near, da_far, da_other], masks, place, order)
+    grad_wout = Reduction(da, attended, masks, 1).step(lane)
+    grad_up.step_half(lane)
     out_rows = lane(
         lambda hidden, *terms: whole(
             lambda hidden, *terms: (hidden + RESIDUAL_SCALE * added(*terms),),
@@ -1035,49 +1167,18 @@
         hidden,
         *out_total.terms(),
     )
-    parts = lane(lambda a, w, o: pieces(a, w, o, count, True), d_qkv, w_qkv, order)
-    got_near, got_other = swap(parts[1], "tensor", NEAR), swap(parts[3], "tensor", NEAR)
-    grad_qkv = Reduction(n1, d_qkv, masks, 0).step(lane)
-    kept, sent = lane(
-        lambda *a: whole(
-            lambda a, b, c, d: (added(a, b), added(c, d)),
-            [(a[0].shape, WIDE), (a[0].shape, LOW)],
-            *a,
-        ),
-        parts[0],
-        got_near,
-        parts[2],
-        got_other,
-    )
-    got_far = swap(sent, "tensor", FAR)
-    grad_up.step(lane)
-    grad_down = grad_down.finish_half(lane, at_array)
-    da = lane(natural, [da_own, da_near, da_far, da_other], order)
-    grad_wout = Reduction(attended, da, masks, 1).step(lane)
-    grad_rows, _, gain_one_part = lane(
-        lambda c, h, i, g, *t: norm_back(c, h, i, g, t, LOW),
-        d_hidden,
-        layer_in,
-        inverse_one,
-        gain_attn,
-        kept,
-        got_far,
-    )
-    grad_gate = grad_gate.finish_half(lane, at_array)
-    grad_qkv.step(lane)
-    grad_up.step_half(lane)
     grad_wout.step(lane)
     grad_qkv.step(lane)
     grad_up = grad_up.finish_half(lane, at_array)
     grad_wout.step(lane)
     grad_qkv = grad_qkv.finish(lane)
-    grad_wout = grad_wout.finish(lane)
     steps = [("tensor", m) for m in powers(count)] + [("dp", m) for m in masks]
     gains = lane(
         lambda a, b: sum_all(jnp.concatenate([a, b], axis=0), steps), gain_one_part, gain_two_part
     )
     block = width // lax.axis_size("dp")
     gains = lax.dynamic_slice_in_dim(gains, place * block, block, 1)
+    grad_wout = grad_wout.finish(lane)
     return (
         out_rows,
         grad_rows,

time: 605 us -> 573 us (0.947)
  waiting for transfers between devices: 84.4 us -> 68.2 us
  starting transfers between devices: 53.3 us -> 43 us
    ppermute x58 -> x42, waiting for transfers between devices: 83.9 us -> 68.2 us  [swap(): return lax.ppermute(array, axis, [(i, i ^ mask) for i in range(size)])]
    ppermute x58 -> x42, starting transfers between devices: 52.8 us -> 40.5 us  [swap(): return lax.ppermute(array, axis, [(i, i ^ mask) for i in range(size)])]
    unnamed x92 -> x84, local copies, waits for them, and re-layouts: 18.2 us -> 16.2 us
    pallas_call x6 -> x7, Pallas kernels: 24.4 us -> 25.8 us  [whole(): pl.pallas_call(kernel, out_shape=[jax.ShapeDtypeStruct(shape, kind) for s...]
    pallas_call x36 -> x28, Pallas kernels: 242 us -> 242 us  [the longest x12 86.4 us: product_rows(): pl.pallas_call(kernel, grid_spec=pltpu.PrefetchScalarGridSpec(num_scalar_...]
  transfers between devices with their start and end apart: 59 -> 43, of which waited for: 22 -> 22; matrix products, arithmetic and copies ran while one was open for 4% -> 4% of each run, Pallas kernels for 60% -> 66%
where the time goes in v3:
time: 573 us; the launch traced here: 563 us
  Pallas kernels  404 us (71%)
  waiting for transfers between devices  68.2 us (12%)
  starting transfers between devices  43 us (8%)
  local copies, waits for them, and re-layouts  29.4 us (5%)
  other arithmetic  16.1 us (3%)
    pallas_call x12, Pallas kernels, product_rows(): pl.pallas_call(kernel, grid_spec=pltpu.PrefetchScalarGridSpec(num_scalar_...  86.4 us
    pallas_call x4, Pallas kernels, paired(): pl.pallas_call(functools.partial(paired_kernel, compute, count, share), g...  69.4 us
    ppermute x42, waiting for transfers between devices, swap(): return lax.ppermute(array, axis, [(i, i ^ mask) for i in range(size)])  68.2 us
    pallas_call x8, Pallas kernels, product_cols(): pl.pallas_call(kernel, grid_spec=pltpu.PrefetchScalarGridSpec(num_scalar_...  52.3 us
    ppermute x42, starting transfers between devices, swap(): return lax.ppermute(array, axis, [(i, i ^ mask) for i in range(size)])  40.5 us
    pallas_call x3, Pallas kernels, mix(): pl.pallas_call(functools.partial(mix_kernel, count), grid_spec=pltpu.Pref...  37.5 us
    pallas_call x4, Pallas kernels, project(): pl.pallas_call(functools.partial(project_kernel, turned, dims), grid_spec...  34.1 us
    pallas_call x1, Pallas kernels, attend_back(): pl.pallas_call(functools.partial(attend_back_kernel, per_kv), grid=(seqs,...  26.9 us
  transfers between devices with their start and end apart: 43, of which 22 were waited for; matrix products, arithmetic and copies ran while one was open for 4% of the time, Pallas kernels for 66%

profile of v3, /device:TPU:16, one launch (start us, length us, event | category | flops | bytes accessed | tf_op | source)
XLA Modules:
  0.0 563.4 jit_solution(8385769284138098285)
XLA Ops:
  17.3 9.1 %near_in.1 = (bf16[1024,768]{1,0:T(8,128)(2,1)}, bf16[256,2048]{1,0:T(8,128)(2,1)}) custom-call(s32[2]{0:T(128)} %get-tuple-element.647.order_ref, bf16[256,2048]{1,0:T(8,128)(2,1)} %fusion.2.share_ref.refs_0_, bf16[2048,768]{1,0:T(8,128)(2,1)} %copy-done.7, f32[1024,128]{1,0:T(8,128)} %get-tuple-element.694.refs_0_.cos_ref, ...), custom_call_target="tpu_custom_call" | custom-call | flops 1 | bytes 1 | tf_op jit(solution)/shard_map/near_in/pallas_call | solution.py:167
  26.4 4.2 collective-permute-done.share_ref.refs_2_
  34.1 9.0 %far_in.1 = (bf16[1024,768]{1,0:T(8,128)(2,1)}, bf16[256,2048]{1,0:T(8,128)(2,1)}) custom-call(s32[2]{0:T(128)} %get-tuple-element.666.order_ref, bf16[256,2048]{1,0:T(8,128)(2,1)} %collective-permute-done.share_ref.refs_2_, bf16[2048,768]{1,0:T(8,128)(2,1)} %copy-done.7, ...), custom_call_target="tpu_custom_call", output_to_operand_aliasing={{0}: (5, {})} | custom-call | flops 1 | bytes 1 | tf_op jit(solution)/shard_map/far_in/pallas_call | solution.py:167
  44.1 20.1 %attend.1 = (bf16[1024,512]{1,0:T(8,128)(2,1)}, f32[4,2,1024]{2,1,0:T(2,128)}) custom-call(bf16[1024,768]{1,0:T(8,128)(2,1)} %get-tuple-element.689.q_ref.k_ref.v_ref, bf16[1024,768]{1,0:T(8,128)(2,1)} %get-tuple-element.689.q_ref.k_ref.v_ref, bf16[1024,768]{1,0:T(8,128)(2,1)} %get-tuple-element.689.q_ref.k_ref.v_ref, s32[1024,1]{1,0:T(8,128)} %copy.42.segq_ref, ...), custom_call_target="tpu_custom_call" | custom-call | flops 1 | bytes 1 | tf_op jit(solution)/shard_map/attend/pallas_call | solution.py:341
  64.1 10.8 %out_pieces.1 = (bf16[256,2048]{1,0:T(8,128)(2,1)}, bf16[256,2048]{1,0:T(8,128)(2,1)}, bf16[256,2048]{1,0:T(8,128)(2,1)}, bf16[256,2048]{1,0:T(8,128)(2,1)}) custom-call(s32[4]{0:T(128)} %copy-done.38, bf16[1024,512]{1,0:T(8,128)(2,1)} %get-tuple-element.891.refs_1_.refs_4_, bf16[512,2048]{1,0:T(8,128)(2,1)} %w_ref.1), custom_call_target="tpu_custom_call" | custom-call | flops 1 | bytes 1 | tf_op jit(solution)/shard_map/out_pieces/pallas_call | solution.py:251
  85.7 15.9 %branch.1.refs_4_.refs_6_ = f32[2048,1024]{1,0:T(8,128)} custom-call(s32[1]{0:T(128)} %bitcast.7.at_ref.refs_0_, bf16[256,2048]{1,0:T(8,128)(2,1)} %multiply_convert_fusion.1.refs_0_, bf16[256,2048]{1,0:T(8,128)(2,1)} %collective-permute-done.5.refs_1_, bf16[256,2048]{1,0:T(8,128)(2,1)} %copy-done.10, bf16[256,2048]{1,0:T(8,128)(2,1)} %collective-permute-done.6.refs_3_, ...), custom_call_target="tpu_custom_call" | custom-call | flops 1 | bytes 1 | tf_op jit(solution)/shard_map/branch/pallas_call | solution.py:495
  111.7 10.8 %mix.3 = (bf16[2048,1024]{1,0:T(8,128)(2,1)}, bf16[2048,1024]{1,0:T(8,128)(2,1)}, bf16[2048,1024]{1,0:T(8,128)(2,1)}) custom-call(s32[1]{0:T(128)} %bitcast.7.at_ref.refs_0_, bf16[256,2048]{1,0:T(8,128)(2,1)} %copy-done, bf16[256,2048]{1,0:T(8,128)(2,1)} %copy-done.3, bf16[2048,2048]{1,0:T(8,128)(2,1)} %refs_3_.1, bf16[2048,2048]{1,0:T(8,128)(2,1)} %refs_4_.2, ...), custom_call_target="tpu_custom_call" | custom-call | flops 1 | bytes 1 | tf_op jit(solution)/shard_map/mix/pallas_call | solution.py:538
  122.5 10.8 %collective-permute-done.10.refs_2_.refs_8_ = bf16[256,2048]{1,0:T(8,128)(2,1)S(1)} collective-permute-done((bf16[256,2048]{1,0:T(8,128)(2,1)S(1)}, bf16[256,2048]{1,0:T(8,128)(2,1)S(1)}, u32[]{:S(2)}, u32[]{:S(2)}) %collective-permute-start.10) | collective-permute-done | bytes 1048608 | tf_op jit(solution)/shard_map/ppermute | solution.py:835
  139.8 16.0 %mix.4 = (bf16[2048,1024]{1,0:T(8,128)(2,1)}, bf16[2048,1024]{1,0:T(8,128)(2,1)}, bf16[2048,1024]{1,0:T(8,128)(2,1)}) custom-call(s32[1]{0:T(128)} %bitcast.7.at_ref.refs_0_, bf16[256,2048]{1,0:T(8,128)(2,1)} %copy-done.2, bf16[256,2048]{1,0:T(8,128)(2,1)} %copy-done.4, ...), custom_call_target="tpu_custom_call", output_to_operand_aliasing={{0}: (8, {}), {1}: (9, {}), {2}: (10, {})} | custom-call | flops 1 | bytes 1 | tf_op jit(solution)/shard_map/mix/pallas_call | solution.py:538
  159.6 10.7 %mix.5 = (bf16[2048,1024]{1,0:T(8,128)(2,1)}, bf16[2048,1024]{1,0:T(8,128)(2,1)}, bf16[2048,1024]{1,0:T(8,128)(2,1)}) custom-call(s32[1]{0:T(128)} %bitcast.7.at_ref.refs_0_, bf16[128,2048]{1,0:T(8,128)(2,1)} %collective-permute-done.12.refs_0_.refs_2_, ...), custom_call_target="tpu_custom_call", output_to_operand_aliasing={{0}: (8, {}), {1}: (9, {}), {2}: (10, {})} | custom-call | flops 1 | bytes 1 | tf_op jit(solution)/shard_map/mix/pallas_call | solution.py:538
  170.2 10.6 %product_cols.8 = bf16[1024,1024]{1,0:T(8,128)(2,1)} custom-call(s32[8]{0:T(128)} %iota_multiply_fusion.starts_ref, s32[8]{0:T(128)} %broadcast_xor_fusion.1.blocks_ref, bf16[256,2048]{1,0:T(8,128)(2,1)} %multiply_convert_fusion.1.refs_0_, bf16[256,2048]{1,0:T(8,128)(2,1)} %collective-permute-done.5.refs_1_, bf16[256,2048]{1,0:T(8,128)(2,1)} %copy-done.10, ...), custom_call_target="tpu_custom_call" | custom-call | flops 1 | bytes 1 | tf_op jit(solution)/shard_map/product_cols/pallas_call | solution.py:684
  182.4 28.6 %unmix.1 = (bf16[256,2048]{1,0:T(8,128)(2,1)}, bf16[256,2048]{1,0:T(8,128)(2,1)}, bf16[256,2048]{1,0:T(8,128)(2,1)}, bf16[256,2048]{1,0:T(8,128)(2,1)}, bf16[256...) custom-call(s32[1]{0:T(128)} %bitcast.7.at_ref.refs_0_, ...), custom_call_target="tpu_custom_call" | custom-call | flops 1 | bytes 1 | tf_op jit(solution)/shard_map/unmix/pallas_call | solution.py:251
  215.8 11.0 %product_rows.12 = bf16[1024,1024]{1,0:T(8,128)(2,1)} custom-call(s32[10]{0:T(128)} %constant.73.clone.starts_ref, s32[8]{0:T(128)} %broadcast_xor_fusion.1.blocks_ref, bf16[256,2048]{1,0:T(8,128)(2,1)} %copy-done, bf16[256,2048]{1,0:T(8,128)(2,1)} %copy-done.3, bf16[128,2048]{1,0:T(8,128)(2,1)} %collective-permute-done.12.refs_0_.refs_2_, ...), custom_call_target="tpu_custom_call" | custom-call | flops 1 | bytes 1 | tf_op jit(solution)/shard_map/product_rows/pallas_call | solution.py:636
  229.7 5.4 whole.9
  237.6 10.7 %product_rows.13 = bf16[1024,1024]{1,0:T(8,128)(2,1)} custom-call(s32[10]{0:T(128)} %constant.73.clone.starts_ref, s32[8]{0:T(128)} %broadcast_xor_fusion.1.blocks_ref, bf16[256,2048]{1,0:T(8,128)(2,1)} %copy-done, bf16[256,2048]{1,0:T(8,128)(2,1)} %copy-done.3, bf16[128,2048]{1,0:T(8,128)(2,1)} %collective-permute-done.12.refs_0_.refs_2_, ...), custom_call_target="tpu_custom_call" | custom-call | flops 1 | bytes 1 | tf_op jit(solution)/shard_map/product_rows/pallas_call | solution.py:636
  249.8 8.2 %product_cols.9 = bf16[1024,512]{1,0:T(8,128)(2,1)} custom-call(s32[8]{0:T(128)} %iota_multiply_fusion.starts_ref, s32[8]{0:T(128)} %broadcast_xor_fusion.1.blocks_ref, bf16[256,2048]{1,0:T(8,128)(2,1)} %multiply_convert_fusion.1.refs_0_, bf16[256,2048]{1,0:T(8,128)(2,1)} %collective-permute-done.5.refs_1_, bf16[256,2048]{1,0:T(8,128)(2,1)} %copy-done.10, ...), custom_call_target="tpu_custom_call" | custom-call | flops 1 | bytes 1 | tf_op jit(solution)/shard_map/product_cols/pallas_call | solution.py:684
  258.0 18.3 %down.1 = (bf16[256,2048]{1,0:T(8,128)(2,1)}, bf16[256,2048]{1,0:T(8,128)(2,1)}, bf16[256,2048]{1,0:T(8,128)(2,1)}, bf16[256,2048]{1,0:T(8,128)(2,1)}, bf16[256,...) custom-call(s32[1]{0:T(128)} %bitcast.7.at_ref.refs_0_, ...), custom_call_target="tpu_custom_call" | custom-call | flops 1 | bytes 1 | tf_op jit(solution)/shard_map/down/pallas_call | solution.py:251
  277.9 5.9 %norm_back.2 = (f32[256,2048]{1,0:T(8,128)}, bf16[256,2048]{1,0:T(8,128)(2,1)}, f32[1,2048]{1,0:T(1,128)}) custom-call(bf16[256,2048]{1,0:T(8,128)(2,1)} %d_ref, f32[256,2048]{1,0:T(8,128)} %copy-done.9, f32[256,1]{1,0:T(8,128)} %copy.43.inverse_ref, bf16[1,2048]{1,0:T(2,128)(2,1)} %reshape.136.gain_ref, f32[256,2048]{1,0:T(8,128)} %get-tuple-element.641.refs_0_, ...), custom_call_target="tpu_custom_call" | custom-call | flops 1 | bytes 1 | tf_op jit(solution)/shard_map/norm_back/pallas_call | solution.py:773
  285.9 8.0 %near_back.1 = (bf16[1024,512]{1,0:T(8,128)(2,1)}, bf16[256,2048]{1,0:T(8,128)(2,1)}) custom-call(s32[2]{0:T(128)} %get-tuple-element.647.order_ref, bf16[256,2048]{1,0:T(8,128)(2,1)} %get-tuple-element.887.share_ref.refs_0_, bf16[512,2048]{1,0:T(8,128)(2,1)} %w_ref.1), custom_call_target="tpu_custom_call" | custom-call | flops 1 | bytes 1 | tf_op jit(solution)/shard_map/near_back/pallas_call | solution.py:167
  293.9 7.9 %product_rows.14 = bf16[512,1024]{1,0:T(8,128)(2,1)} custom-call(s32[10]{0:T(128)} %constant.73.clone.starts_ref, s32[8]{0:T(128)} %broadcast_xor_fusion.1.blocks_ref, bf16[256,2048]{1,0:T(8,128)(2,1)} %copy-done, bf16[256,2048]{1,0:T(8,128)(2,1)} %copy-done.3, bf16[128,2048]{1,0:T(8,128)(2,1)} %collective-permute-done.12.refs_0_.refs_2_, ...), custom_call_target="tpu_custom_call" | custom-call | flops 1 | bytes 1 | tf_op jit(solution)/shard_map/product_rows/pallas_call | solution.py:636
  301.8 7.5 %collective-permute-done.23.share_ref.refs_2_ = bf16[256,2048]{1,0:T(8,128)(2,1)S(1)} collective-permute-done((bf16[256,2048]{1,0:T(8,128)(2,1)}, bf16[256,2048]{1,0:T(8,128)(2,1)S(1)}, u32[]{:S(2)}, u32[]{:S(2)}) %collective-permute-start.23) | collective-permute-done | bytes 1048608 | tf_op jit(solution)/shard_map/ppermute | solution.py:835
  310.3 8.0 %far_back.1 = (bf16[1024,512]{1,0:T(8,128)(2,1)}, bf16[256,2048]{1,0:T(8,128)(2,1)}) custom-call(s32[2]{0:T(128)} %get-tuple-element.666.order_ref, bf16[256,2048]{1,0:T(8,128)(2,1)} %copy-done.12, bf16[512,2048]{1,0:T(8,128)(2,1)} %w_ref.1, bf16[1024,512]{1,0:T(8,128)(2,1)} %get-tuple-element.669.refs_0_), custom_call_target="tpu_custom_call", output_to_operand_aliasing={{0}: (3, {})} | custom-call | flops 1 | bytes 1 | tf_op jit(solution)/shard_map/far_back/pallas_call | solution.py:167
  323.9 7.2 %collective-permute-done.28.refs_10_ = bf16[1024,512]{1,0:T(8,128)(2,1)} collective-permute-done((bf16[1024,512]{1,0:T(8,128)(2,1)}, bf16[1024,512]{1,0:T(8,128)(2,1)}, u32[]{:S(2)}, u32[]{:S(2)}) %collective-permute-start.28) | collective-permute-done | bytes 1048608 | tf_op jit(solution)/shard_map/ppermute | solution.py:835
  331.1 7.0 %product_cols.10 = bf16[1024,256]{1,0:T(8,128)(2,1)} custom-call(s32[8]{0:T(128)} %iota_multiply_fusion.starts_ref, s32[8]{0:T(128)} %broadcast_xor_fusion.1.blocks_ref, bf16[256,2048]{1,0:T(8,128)(2,1)} %multiply_convert_fusion.1.refs_0_, bf16[256,2048]{1,0:T(8,128)(2,1)} %collective-permute-done.5.refs_1_, bf16[256,2048]{1,0:T(8,128)(2,1)} %copy-done.10, ...), custom_call_target="tpu_custom_call" | custom-call | flops 1 | bytes 1 | tf_op jit(solution)/shard_map/product_cols/pallas_call | solution.py:684
  339.2 26.9 %attend_back.1.refs_4_.refs_1_ = bf16[1024,768]{1,0:T(8,128)(2,1)} custom-call(bf16[1024,768]{1,0:T(8,128)(2,1)} %get-tuple-element.689.q_ref.k_ref.v_ref, bf16[1024,768]{1,0:T(8,128)(2,1)} %get-tuple-element.689.q_ref.k_ref.v_ref, bf16[1024,768]{1,0:T(8,128)(2,1)} %get-tuple-element.689.q_ref.k_ref.v_ref, bf16[1024,512]{1,0:T(8,128)(2,1)} %get-tuple-element.690.g_ref, ...), custom_call_target="tpu_custom_call" | custom-call | flops 1 | bytes 1 | tf_op jit(solution)/shard_map/attend_back/pallas_call | solution.py:454
  366.1 6.9 %product_rows.15 = bf16[1024,768]{1,0:T(8,128)(2,1)} custom-call(s32[4]{0:T(128)} %broadcast_multiply_fusion.starts_ref, s32[8]{0:T(128)} %broadcast_xor_fusion.blocks_ref, bf16[256,2048]{1,0:T(8,128)(2,1)} %fusion.2.share_ref.refs_0_, bf16[256,2048]{1,0:T(8,128)(2,1)} %get-tuple-element.876.refs_1_, ...), custom_call_target="tpu_custom_call" | custom-call | flops 1 | bytes 1 | tf_op jit(solution)/shard_map/product_rows/pallas_call | solution.py:636
  374.8 7.9 %product_rows.16 = bf16[512,1024]{1,0:T(8,128)(2,1)} custom-call(s32[10]{0:T(128)} %constant.73.clone.starts_ref, s32[8]{0:T(128)} %broadcast_xor_fusion.1.blocks_ref, bf16[256,2048]{1,0:T(8,128)(2,1)} %copy-done, bf16[256,2048]{1,0:T(8,128)(2,1)} %copy-done.3, bf16[128,2048]{1,0:T(8,128)(2,1)} %collective-permute-done.12.refs_0_.refs_2_, ...), custom_call_target="tpu_custom_call" | custom-call | flops 1 | bytes 1 | tf_op jit(solution)/shard_map/product_rows/pallas_call | solution.py:636
  382.8 5.4 whole.11
  388.1 11.7 %in_pieces.1 = (bf16[256,2048]{1,0:T(8,128)(2,1)}, bf16[256,2048]{1,0:T(8,128)(2,1)}, bf16[256,2048]{1,0:T(8,128)(2,1)}, bf16[256,2048]{1,0:T(8,128)(2,1)}) custom-call(s32[4]{0:T(128)} %copy-done.38, bf16[1024,768]{1,0:T(8,128)(2,1)} %attend_back.1.refs_4_.refs_1_, bf16[2048,768]{1,0:T(8,128)(2,1)} %copy-done.7), custom_call_target="tpu_custom_call" | custom-call | flops 1 | bytes 1 | tf_op jit(solution)/shard_map/in_pieces/pallas_call | solution.py:251
  403.6 4.0 collective-permute-start.35
  408.6 6.6 %product_rows.17 = bf16[256,1024]{1,0:T(8,128)(2,1)} custom-call(s32[10]{0:T(128)} %constant.73.clone.starts_ref, s32[8]{0:T(128)} %broadcast_xor_fusion.1.blocks_ref, bf16[256,2048]{1,0:T(8,128)(2,1)} %copy-done, bf16[256,2048]{1,0:T(8,128)(2,1)} %copy-done.3, bf16[128,2048]{1,0:T(8,128)(2,1)} %collective-permute-done.12.refs_0_.refs_2_, ...), custom_call_target="tpu_custom_call" | custom-call | flops 1 | bytes 1 | tf_op jit(solution)/shard_map/product_rows/pallas_call | solution.py:636
  416.7 7.3 %product_cols.11.own_ref = f32[1024,256]{1,0:T(8,128)} custom-call(s32[8]{0:T(128)} %iota_multiply_fusion.starts_ref, s32[8]{0:T(128)} %broadcast_xor_fusion.1.blocks_ref, bf16[256,2048]{1,0:T(8,128)(2,1)} %multiply_convert_fusion.1.refs_0_, bf16[256,2048]{1,0:T(8,128)(2,1)} %collective-permute-done.5.refs_1_, bf16[256,2048]{1,0:T(8,128)(2,1)} %copy-done.10, ...), custom_call_target="tpu_custom_call" | custom-call | flops 1 | bytes 1 | tf_op jit(solution)/shard_map/product_cols/pallas_call | solution.py:684
  424.0 7.8 %collective-permute-done.35.other_ref = bf16[1024,256]{1,0:T(8,128)(2,1)} collective-permute-done((bf16[1024,256]{1,0:T(8,128)(2,1)}, bf16[1024,256]{1,0:T(8,128)(2,1)}, u32[]{:S(2)}, u32[]{:S(2)}) %collective-permute-start.35) | collective-permute-done | bytes 524320 | tf_op jit(solution)/shard_map/ppermute | solution.py:835
  439.6 5.2 norm_back.3
  444.8 6.8 %product_rows.18.own_ref = f32[256,1024]{1,0:T(8,128)} custom-call(s32[10]{0:T(128)} %constant.73.clone.starts_ref, s32[8]{0:T(128)} %broadcast_xor_fusion.1.blocks_ref, bf16[256,2048]{1,0:T(8,128)(2,1)} %copy-done, bf16[256,2048]{1,0:T(8,128)(2,1)} %copy-done.3, bf16[128,2048]{1,0:T(8,128)(2,1)} %collective-permute-done.12.refs_0_.refs_2_, ...), custom_call_target="tpu_custom_call" | custom-call | flops 1 | bytes 1 | tf_op jit(solution)/shard_map/product_rows/pallas_call | solution.py:636
  455.2 5.4 product_rows.19
  460.6 5.8 %product_cols.12 = bf16[512,1024]{1,0:T(8,128)(2,1)} custom-call(s32[4]{0:T(128)} %broadcast_multiply_fusion.starts_ref, s32[8]{0:T(128)} %broadcast_xor_fusion.blocks_ref, bf16[256,2048]{1,0:T(8,128)(2,1)} %get-tuple-element.887.share_ref.refs_0_, bf16[256,2048]{1,0:T(8,128)(2,1)} %get-tuple-element.888.refs_1_, bf16[256,2048]{1,0:T(8,128)(2,1)} %copy-done.12, ...), custom_call_target="tpu_custom_call" | custom-call | flops 1 | bytes 1 | tf_op jit(solution)/shard_map/product_cols/pallas_call | solution.py:684
  469.2 6.6 %product_rows.20 = bf16[256,1024]{1,0:T(8,128)(2,1)} custom-call(s32[10]{0:T(128)} %constant.73.clone.starts_ref, s32[8]{0:T(128)} %broadcast_xor_fusion.1.blocks_ref, bf16[256,2048]{1,0:T(8,128)(2,1)} %copy-done, bf16[256,2048]{1,0:T(8,128)(2,1)} %copy-done.3, bf16[128,2048]{1,0:T(8,128)(2,1)} %collective-permute-done.12.refs_0_.refs_2_, ...), custom_call_target="tpu_custom_call" | custom-call | flops 1 | bytes 1 | tf_op jit(solution)/shard_map/product_rows/pallas_call | solution.py:636
  477.7 4.2 whole.13
  485.9 4.8 product_cols.13
  494.5 4.8 product_rows.21
  500.8 6.8 %product_rows.22.own_ref = f32[256,1024]{1,0:T(8,128)} custom-call(s32[10]{0:T(128)} %constant.73.clone.starts_ref, s32[8]{0:T(128)} %broadcast_xor_fusion.1.blocks_ref, bf16[256,2048]{1,0:T(8,128)(2,1)} %copy-done, bf16[256,2048]{1,0:T(8,128)(2,1)} %copy-done.3, bf16[128,2048]{1,0:T(8,128)(2,1)} %collective-permute-done.12.refs_0_.refs_2_, ...), custom_call_target="tpu_custom_call" | custom-call | flops 1 | bytes 1 | tf_op jit(solution)/shard_map/product_rows/pallas_call | solution.py:636
  507.6 5.3 collective-permute-done.41.other_ref
  516.5 6.5 %collective-permute-done.40.refs_6_ = bf16[512,512]{1,0:T(8,128)(2,1)S(1)} collective-permute-done((bf16[512,512]{1,0:T(8,128)(2,1)}, bf16[512,512]{1,0:T(8,128)(2,1)S(1)}, u32[]{:S(2)}, u32[]{:S(2)}) %collective-permute-start.40) | collective-permute-done | bytes 524320 | tf_op jit(solution)/shard_map/ppermute | solution.py:835
  523.9 4.3 product_cols.14
  529.0 5.0 product_rows.23
  536.5 16.5 %sum_all.1 = f32[2,2048]{1,0:T(2,128)} custom-call(f32[2,2048]{1,0:T(2,128)} %pad_maximum_fusion.2.part_ref), custom_call_target="tpu_custom_call" | custom-call | flops 1 | bytes 1 | tf_op jit(solution)/shard_map/sum_all/pallas_call | solution.py:816
  558.7 4.4 product_cols.15
  (208 shorter events, 122.7 us)
Async XLA Ops:
  5.4 25.2 %collective-permute-start = (bf16[256,2048]{1,0:T(8,128)(2,1)}, bf16[256,2048]{1,0:T(8,128)(2,1)}, u32[]{:S(2)}, u32[]{:S(2)}) collective-permute-start(bf16[256,2048]{1,0:T(8,128)(2,1)} %fusion.2.share_ref.refs_0_), channel_id=1, source_target_pairs={{0,2},{1,3},{2,0},{3,1},{4,6},{5,7},{6,4},{7,5},{8,10},{9,11},{10,... | collective-permute-start | bytes 3145736 | tf_op jit(solution)/shard_map/ppermute | solution.py:835
  30.6 47.3 %collective-permute-start.2 = (bf16[256,2048]{1,0:T(8,128)(2,1)}, bf16[256,2048]{1,0:T(8,128)(2,1)S(1)}, u32[]{:S(2)}, u32[]{:S(2)}) collective-permute-start(bf16[256,2048]{1,0:T(8,128)(2,1)} %multiply_convert_fusion.1.refs_0_), channel_id=1, source_target_pairs={{0,10},{1,11},{2,8},{3,9},{4,14},{5,15},{6,12},{7,13},{8,2},{9,3},... | collective-permute-start | bytes 3145736 | tf_op jit(solution)/shard_map/ppermute | solution.py:846
  33.1 45.1 %collective-permute-start.3 = (bf16[256,2048]{1,0:T(8,128)(2,1)}, bf16[256,2048]{1,0:T(8,128)(2,1)S(1)}, u32[]{:S(2)}, u32[]{:S(2)}) collective-permute-start(bf16[256,2048]{1,0:T(8,128)(2,1)} %multiply_convert_fusion.1.refs_0_), channel_id=1, source_target_pairs={{0,2},{1,3},{2,0},{3,1},{4,6},{5,7},{6,4},{7,5},{8,10},{9,11},{10,... | collective-permute-start | bytes 3145736 | tf_op jit(solution)/shard_map/ppermute | solution.py:835
  33.6 44.7 %collective-permute-start.4 = (bf16[256,2048]{1,0:T(8,128)(2,1)}, bf16[256,2048]{1,0:T(8,128)(2,1)}, u32[]{:S(2)}, u32[]{:S(2)}) collective-permute-start(bf16[256,2048]{1,0:T(8,128)(2,1)} %multiply_convert_fusion.1.refs_0_), channel_id=1, source_target_pairs={{0,8},{4,12},{8,0},{12,4},{16,24},{20,28},{24,16},{28,20},{1,9},{5... | collective-permute-start | bytes 3145736 | tf_op jit(solution)/shard_map/ppermute | solution.py:835
  77.8 7.8 %copy-start.10 = (bf16[256,2048]{1,0:T(8,128)(2,1)}, bf16[256,2048]{1,0:T(8,128)(2,1)S(1)}, u32[]{:S(2)}) copy-start(bf16[256,2048]{1,0:T(8,128)(2,1)S(1)} %collective-permute-done.2.refs_2_) | copy-start | bytes 3145732
  78.4 2.8 collective-permute-start.5
  78.4 5.8 %collective-permute-start.6 = (bf16[256,2048]{1,0:T(8,128)(2,1)S(1)}, bf16[256,2048]{1,0:T(8,128)(2,1)}, u32[]{:S(2)}, u32[]{:S(2)}) collective-permute-start(bf16[256,2048]{1,0:T(8,128)(2,1)S(1)} %collective-permute-done.2.refs_2_), channel_id=1, source_target_pairs={{0,1},{1,0},{2,3},{3,2},{4,5},{5,4},{6,7},{7,6},{8,9},{9,8},{10,11... | collective-permute-start | bytes 3145736 | tf_op jit(solution)/shard_map/ppermute | solution.py:835
  78.9 6.8 %collective-permute-start.7 = (bf16[256,2048]{1,0:T(8,128)(2,1)S(1)}, bf16[256,2048]{1,0:T(8,128)(2,1)}, u32[]{:S(2)}, u32[]{:S(2)}) collective-permute-start(bf16[256,2048]{1,0:T(8,128)(2,1)S(1)} %collective-permute-done.3.refs_4_), channel_id=1, source_target_pairs={{0,1},{1,0},{2,3},{3,2},{4,5},{5,4},{6,7},{7,6},{8,9},{9,8},{10,11... | collective-permute-start | bytes 3145736 | tf_op jit(solution)/shard_map/ppermute | solution.py:835
  78.9 6.8 %collective-permute-start.8 = (bf16[256,2048]{1,0:T(8,128)(2,1)}, bf16[256,2048]{1,0:T(8,128)(2,1)}, u32[]{:S(2)}, u32[]{:S(2)}) collective-permute-start(bf16[256,2048]{1,0:T(8,128)(2,1)} %collective-permute-done.4.refs_6_), channel_id=1, source_target_pairs={{0,1},{1,0},{2,3},{3,2},{4,5},{5,4},{6,7},{7,6},{8,9},{9,8},{10,11... | collective-permute-start | bytes 3145736 | tf_op jit(solution)/shard_map/ppermute | solution.py:835
  79.4 25.4 %collective-permute-start.1 = (bf16[256,2048]{1,0:T(8,128)(2,1)}, bf16[256,2048]{1,0:T(8,128)(2,1)}, u32[]{:S(2)}, u32[]{:S(2)}) collective-permute-start(bf16[256,2048]{1,0:T(8,128)(2,1)} %whole.7), channel_id=1, source_target_pairs={{0,2},{1,3},{2,0},{3,1},{4,6},{5,7},{6,4},{7,5},{8,10},{9,11},{10,... | collective-permute-start | bytes 3145736 | tf_op jit(solution)/shard_map/ppermute | solution.py:835
  85.7 19.1 %copy-start.14 = (bf16[256,2048]{1,0:T(8,128)(2,1)S(1)}, bf16[256,2048]{1,0:T(8,128)(2,1)}, u32[]{:S(2)}) copy-start(bf16[256,2048]{1,0:T(8,128)(2,1)} %value_ref) | copy-start | bytes 3145732
  107.7 2.9 collective-permute-start.11
  107.8 25.6 %collective-permute-start.10 = (bf16[256,2048]{1,0:T(8,128)(2,1)S(1)}, bf16[256,2048]{1,0:T(8,128)(2,1)S(1)}, u32[]{:S(2)}, u32[]{:S(2)}) collective-permute-start(bf16[256,2048]{1,0:T(8,128)(2,1)S(1)} %multiply_convert_fusion.refs_0_), channel_id=1, source_target_pairs={{0,8},{4,12},{8,0},{12,4},{16,24},{20,28},{24,16},{28,20},{1,9},{5... | collective-permute-start | bytes 3145736 | tf_op jit(solution)/shard_map/ppermute | solution.py:835
  109.4 25.2 %collective-permute-start.9 = (bf16[256,2048]{1,0:T(8,128)(2,1)S(1)}, bf16[256,2048]{1,0:T(8,128)(2,1)S(1)}, u32[]{:S(2)}, u32[]{:S(2)}) collective-permute-start(bf16[256,2048]{1,0:T(8,128)(2,1)S(1)} %multiply_convert_fusion.refs_0_), channel_id=1, source_target_pairs={{0,2},{1,3},{2,0},{3,1},{4,6},{5,7},{6,4},{7,5},{8,10},{9,11},{10,... | collective-permute-start | bytes 3145736 | tf_op jit(solution)/shard_map/ppermute | solution.py:835
  134.7 4.1 collective-permute-start.14
  134.7 4.3 collective-permute-start.15
  136.8 20.0 %copy-start.40 = (s32[8]{0:T(128)S(1)}, s32[8]{0:T(128)}, u32[]{:S(2)}) copy-start(s32[8]{0:T(128)} %constant.72.clone) | copy-start | bytes 100
  136.8 18.9 %collective-permute-start.12 = (bf16[128,2048]{1,0:T(8,128)(2,1)}, bf16[128,2048]{1,0:T(8,128)(2,1)}, u32[]{:S(2)}, u32[]{:S(2)}) collective-permute-start(bf16[128,2048]{1,0:T(8,128)(2,1)} %slice.47), channel_id=1, source_target_pairs={{0,2},{1,3},{2,0},{3,1},{4,6},{5,7},{6,4},{7,5},{8,10},{9,11},{10,... | collective-permute-start | bytes 1572872 | tf_op jit(solution)/shard_map/ppermute | solution.py:835
  138.1 17.7 %collective-permute-start.13 = (bf16[128,2048]{1,0:T(8,128)(2,1)}, bf16[128,2048]{1,0:T(8,128)(2,1)}, u32[]{:S(2)}, u32[]{:S(2)}) collective-permute-start(bf16[128,2048]{1,0:T(8,128)(2,1)} %slice.48), channel_id=1, source_target_pairs={{0,8},{4,12},{8,0},{12,4},{16,24},{20,28},{24,16},{28,20},{1,9},{5... | collective-permute-start | bytes 1572872 | tf_op jit(solution)/shard_map/ppermute | solution.py:835
  155.8 2.2 collective-permute-start.16
  156.0 2.7 collective-permute-start.17
  180.8 69.0 %collective-permute-start.18 = (bf16[1024,1024]{1,0:T(8,128)(2,1)}, bf16[1024,1024]{1,0:T(8,128)(2,1)}, u32[]{:S(2)}, u32[]{:S(2)}) collective-permute-start(bf16[1024,1024]{1,0:T(8,128)(2,1)} %product_cols.8), channel_id=1, source_target_pairs={{0,4},{4,0},{8,12},{12,8},{16,20},{20,16},{24,28},{28,24},{1,5},{5... | collective-permute-start | bytes 6291464 | tf_op jit(solution)/shard_map/ppermute | solution.py:835
  213.7 14.2 %collective-permute-start.19 = (bf16[128,2048]{1,0:T(8,128)(2,1)}, bf16[128,2048]{1,0:T(8,128)(2,1)S(1)}, u32[]{:S(2)}, u32[]{:S(2)}) collective-permute-start(bf16[128,2048]{1,0:T(8,128)(2,1)} %get-tuple-element.575), channel_id=1, source_target_pairs={{0,8},{4,12},{8,0},{12,4},{16,24},{20,28},{24,16},{28,20},{1,9},{5... | collective-permute-start | bytes 1572872 | tf_op jit(solution)/shard_map/ppermute | solution.py:835
  215.0 13.9 %collective-permute-start.20 = (bf16[128,2048]{1,0:T(8,128)(2,1)}, bf16[128,2048]{1,0:T(8,128)(2,1)S(1)}, u32[]{:S(2)}, u32[]{:S(2)}) collective-permute-start(bf16[128,2048]{1,0:T(8,128)(2,1)} %get-tuple-element.576), channel_id=1, source_target_pairs={{0,2},{1,3},{2,0},{3,1},{4,6},{5,7},{6,4},{7,5},{8,10},{9,11},{10,... | collective-permute-start | bytes 1572872 | tf_op jit(solution)/shard_map/ppermute | solution.py:835
  235.1 41.2 %collective-permute-start.21 = (bf16[256,2048]{1,0:T(8,128)(2,1)}, bf16[256,2048]{1,0:T(8,128)(2,1)S(1)}, u32[]{:S(2)}, u32[]{:S(2)}) collective-permute-start(bf16[256,2048]{1,0:T(8,128)(2,1)} %get-tuple-element.599), channel_id=1, source_target_pairs={{0,2},{1,3},{2,0},{3,1},{4,6},{5,7},{6,4},{7,5},{8,10},{9,11},{10,... | collective-permute-start | bytes 3145736 | tf_op jit(solution)/shard_map/ppermute | solution.py:835
  236.1 40.2 %collective-permute-start.22 = (bf16[256,2048]{1,0:T(8,128)(2,1)}, bf16[256,2048]{1,0:T(8,128)(2,1)}, u32[]{:S(2)}, u32[]{:S(2)}) collective-permute-start(bf16[256,2048]{1,0:T(8,128)(2,1)} %get-tuple-element.600), channel_id=1, source_target_pairs={{0,8},{4,12},{8,0},{12,4},{16,24},{20,28},{24,16},{28,20},{1,9},{5... | collective-permute-start | bytes 3145736 | tf_op jit(solution)/shard_map/ppermute | solution.py:835
  237.1 56.8 %collective-permute-start.24 = (bf16[1024,1024]{1,0:T(8,128)(2,1)}, bf16[1024,1024]{1,0:T(8,128)(2,1)}, u32[]{:S(2)}, u32[]{:S(2)}) collective-permute-start(bf16[1024,1024]{1,0:T(8,128)(2,1)} %product_rows.12), channel_id=1, source_target_pairs={{0,4},{4,0},{8,12},{12,8},{16,20},{20,16},{24,28},{28,24},{1,5},{5... | collective-permute-start | bytes 6291464 | tf_op jit(solution)/shard_map/ppermute | solution.py:835
  248.2 125.3 %collective-permute-start.27 = (bf16[1024,1024]{1,0:T(8,128)(2,1)}, bf16[1024,1024]{1,0:T(8,128)(2,1)S(1)}, u32[]{:S(2)}, u32[]{:S(2)}) collective-permute-start(bf16[1024,1024]{1,0:T(8,128)(2,1)} %product_rows.13), channel_id=1, source_target_pairs={{0,4},{4,0},{8,12},{12,8},{16,20},{20,16},{24,28},{28,24},{1,5},{5... | collective-permute-start | bytes 6291464 | tf_op jit(solution)/shard_map/ppermute | solution.py:835
  283.8 25.5 %collective-permute-start.23 = (bf16[256,2048]{1,0:T(8,128)(2,1)}, bf16[256,2048]{1,0:T(8,128)(2,1)S(1)}, u32[]{:S(2)}, u32[]{:S(2)}) collective-permute-start(bf16[256,2048]{1,0:T(8,128)(2,1)} %get-tuple-element.887.share_ref.refs_0_), channel_id=1, source_target_pairs={{0,2},{1,3},{2,0},{3,1},{4,6},{5,7},{6,4},{7,5},{8,10},{9,11},{10,... | collective-permute-start | bytes 3145736 | tf_op jit(solution)/shard_map/ppermute | solution.py:835
  285.0 46.2 %collective-permute-start.28 = (bf16[1024,512]{1,0:T(8,128)(2,1)}, bf16[1024,512]{1,0:T(8,128)(2,1)}, u32[]{:S(2)}, u32[]{:S(2)}) collective-permute-start(bf16[1024,512]{1,0:T(8,128)(2,1)} %product_cols.9), channel_id=1, source_target_pairs={{0,16},{4,20},{8,24},{12,28},{16,0},{20,4},{24,8},{28,12},{1,17},{... | collective-permute-start | bytes 3145736 | tf_op jit(solution)/shard_map/ppermute | solution.py:835
  320.9 61.8 %collective-permute-start.25 = (bf16[128,2048]{1,0:T(8,128)(2,1)}, bf16[128,2048]{1,0:T(8,128)(2,1)}, u32[]{:S(2)}, u32[]{:S(2)}) collective-permute-start(bf16[128,2048]{1,0:T(8,128)(2,1)} %get-tuple-element.674), channel_id=1, source_target_pairs={{0,8},{4,12},{8,0},{12,4},{16,24},{20,28},{24,16},{28,20},{1,9},{5... | collective-permute-start | bytes 1572872 | tf_op jit(solution)/shard_map/ppermute | solution.py:835
  322.0 60.8 %collective-permute-start.26 = (bf16[128,2048]{1,0:T(8,128)(2,1)}, bf16[128,2048]{1,0:T(8,128)(2,1)}, u32[]{:S(2)}, u32[]{:S(2)}) collective-permute-start(bf16[128,2048]{1,0:T(8,128)(2,1)} %get-tuple-element.675), channel_id=1, source_target_pairs={{0,2},{1,3},{2,0},{3,1},{4,6},{5,7},{6,4},{7,5},{8,10},{9,11},{10,... | collective-permute-start | bytes 1572872 | tf_op jit(solution)/shard_map/ppermute | solution.py:835
  323.6 14.5 %copy-start.33 = (s32[1,1024]{1,0:T(1,128)S(1)}, s32[1,1024]{1,0:T(1,128)}, u32[]{:S(2)}) copy-start(s32[1,1024]{1,0:T(1,128)} %param.20) | copy-start | bytes 12292
  323.6 84.0 %collective-permute-start.33 = (bf16[512,1024]{1,0:T(8,128)(2,1)}, bf16[512,1024]{1,0:T(8,128)(2,1)S(1)}, u32[]{:S(2)}, u32[]{:S(2)}) collective-permute-start(bf16[512,1024]{1,0:T(8,128)(2,1)} %product_rows.14), channel_id=1, source_target_pairs={{0,16},{4,20},{8,24},{12,28},{16,0},{20,4},{24,8},{28,12},{1,17},{... | collective-permute-start | bytes 3145736 | tf_op jit(solution)/shard_map/ppermute | solution.py:835
  372.9 82.3 %collective-permute-start.32 = (bf16[1024,768]{1,0:T(8,128)(2,1)}, bf16[1024,768]{1,0:T(8,128)(2,1)}, u32[]{:S(2)}, u32[]{:S(2)}) collective-permute-start(bf16[1024,768]{1,0:T(8,128)(2,1)} %product_rows.15), channel_id=1, source_target_pairs={{0,4},{4,0},{8,12},{12,8},{16,20},{20,16},{24,28},{28,24},{1,5},{5... | collective-permute-start | bytes 4718600 | tf_op jit(solution)/shard_map/ppermute | solution.py:835
  402.6 33.1 %collective-permute-start.34 = (bf16[256,2048]{1,0:T(8,128)(2,1)}, bf16[256,2048]{1,0:T(8,128)(2,1)S(1)}, u32[]{:S(2)}, u32[]{:S(2)}) collective-permute-start(bf16[256,2048]{1,0:T(8,128)(2,1)} %whole.12), channel_id=1, source_target_pairs={{0,2},{1,3},{2,0},{3,1},{4,6},{5,7},{6,4},{7,5},{8,10},{9,11},{10,... | collective-permute-start | bytes 3145736 | tf_op jit(solution)/shard_map/ppermute | solution.py:835
  403.6 28.3 %collective-permute-start.35 = (bf16[1024,256]{1,0:T(8,128)(2,1)}, bf16[1024,256]{1,0:T(8,128)(2,1)}, u32[]{:S(2)}, u32[]{:S(2)}) collective-permute-start(bf16[1024,256]{1,0:T(8,128)(2,1)} %product_cols.10), channel_id=1, source_target_pairs={{0,8},{4,12},{8,0},{12,4},{16,24},{20,28},{24,16},{28,20},{1,9},{5... | collective-permute-start | bytes 1572872 | tf_op jit(solution)/shard_map/ppermute | solution.py:835
  415.2 36.4 %collective-permute-start.36 = (bf16[256,1024]{1,0:T(8,128)(2,1)}, bf16[256,1024]{1,0:T(8,128)(2,1)S(1)}, u32[]{:S(2)}, u32[]{:S(2)}) collective-permute-start(bf16[256,1024]{1,0:T(8,128)(2,1)} %product_rows.17), channel_id=1, source_target_pairs={{0,8},{4,12},{8,0},{12,4},{16,24},{20,28},{24,16},{28,20},{1,9},{5... | collective-permute-start | bytes 1572872 | tf_op jit(solution)/shard_map/ppermute | solution.py:835
  415.3 52.9 %collective-permute-start.31 = (bf16[512,1024]{1,0:T(8,128)(2,1)}, bf16[512,1024]{1,0:T(8,128)(2,1)S(1)}, u32[]{:S(2)}, u32[]{:S(2)}) collective-permute-start(bf16[512,1024]{1,0:T(8,128)(2,1)} %product_rows.16), channel_id=1, source_target_pairs={{0,16},{4,20},{8,24},{12,28},{16,0},{20,4},{24,8},{28,12},{1,17},{... | collective-permute-start | bytes 3145736 | tf_op jit(solution)/shard_map/ppermute | solution.py:835
  424.0 15.0 %copy-start.35 = (bf16[2048]{0:T(1024)(128)(2,1)S(1)}, bf16[2048]{0:T(1024)(128)(2,1)}, u32[]{:S(2)}) copy-start(bf16[2048]{0:T(1024)(128)(2,1)} %param.21) | copy-start | bytes 12292
  431.8 45.9 %collective-permute-start.29 = (bf16[256,2048]{1,0:T(8,128)(2,1)}, bf16[256,2048]{1,0:T(8,128)(2,1)}, u32[]{:S(2)}, u32[]{:S(2)}) collective-permute-start(bf16[256,2048]{1,0:T(8,128)(2,1)} %get-tuple-element.726), channel_id=1, source_target_pairs={{0,2},{1,3},{2,0},{3,1},{4,6},{5,7},{6,4},{7,5},{8,10},{9,11},{10,... | collective-permute-start | bytes 3145736 | tf_op jit(solution)/shard_map/ppermute | solution.py:835
  435.7 42.0 %collective-permute-start.30 = (bf16[256,2048]{1,0:T(8,128)(2,1)}, bf16[256,2048]{1,0:T(8,128)(2,1)}, u32[]{:S(2)}, u32[]{:S(2)}) collective-permute-start(bf16[256,2048]{1,0:T(8,128)(2,1)} %get-tuple-element.727), channel_id=1, source_target_pairs={{0,8},{4,12},{8,0},{12,4},{16,24},{20,28},{24,16},{28,20},{1,9},{5... | collective-permute-start | bytes 3145736 | tf_op jit(solution)/shard_map/ppermute | solution.py:835
  466.4 18.5 %collective-permute-start.38 = (bf16[512,1024]{1,0:T(8,128)(2,1)}, bf16[512,1024]{1,0:T(8,128)(2,1)S(1)}, u32[]{:S(2)}, u32[]{:S(2)}) collective-permute-start(bf16[512,1024]{1,0:T(8,128)(2,1)} %product_cols.12), channel_id=1, source_target_pairs={{0,4},{4,0},{8,12},{12,8},{16,20},{20,16},{24,28},{28,24},{1,5},{5... | collective-permute-start | bytes 3145736 | tf_op jit(solution)/shard_map/ppermute | solution.py:835
  468.0 25.6 %collective-permute-start.37 = (bf16[512,768]{1,0:T(8,128)(2,1)}, bf16[512,768]{1,0:T(8,128)(2,1)S(1)}, u32[]{:S(2)}, u32[]{:S(2)}) collective-permute-start(bf16[512,768]{1,0:T(8,128)(2,1)} %product_rows.19), channel_id=1, source_target_pairs={{0,8},{4,12},{8,0},{12,4},{16,24},{20,28},{24,16},{28,20},{1,9},{5... | collective-permute-start | bytes 2359304 | tf_op jit(solution)/shard_map/ppermute | solution.py:835
  475.8 37.1 %collective-permute-start.41 = (bf16[256,1024]{1,0:T(8,128)(2,1)}, bf16[256,1024]{1,0:T(8,128)(2,1)S(1)}, u32[]{:S(2)}, u32[]{:S(2)}) collective-permute-start(bf16[256,1024]{1,0:T(8,128)(2,1)} %product_rows.20), channel_id=1, source_target_pairs={{0,8},{4,12},{8,0},{12,4},{16,24},{20,28},{24,16},{28,20},{1,9},{5... | collective-permute-start | bytes 1572872 | tf_op jit(solution)/shard_map/ppermute | solution.py:835
  490.7 32.4 %collective-permute-start.40 = (bf16[512,512]{1,0:T(8,128)(2,1)}, bf16[512,512]{1,0:T(8,128)(2,1)S(1)}, u32[]{:S(2)}, u32[]{:S(2)}) collective-permute-start(bf16[512,512]{1,0:T(8,128)(2,1)} %product_cols.13), channel_id=1, source_target_pairs={{0,8},{4,12},{8,0},{12,4},{16,24},{20,28},{24,16},{28,20},{1,9},{5... | collective-permute-start | bytes 1572872 | tf_op jit(solution)/shard_map/ppermute | solution.py:835
  499.3 28.9 %collective-permute-start.39 = (bf16[256,768]{1,0:T(8,128)(2,1)}, bf16[256,768]{1,0:T(8,128)(2,1)S(1)}, u32[]{:S(2)}, u32[]{:S(2)}) collective-permute-start(bf16[256,768]{1,0:T(8,128)(2,1)} %product_rows.21), channel_id=1, source_target_pairs={{0,16},{4,20},{8,24},{12,28},{16,0},{20,4},{24,8},{28,12},{1,17},{... | collective-permute-start | bytes 1179656 | tf_op jit(solution)/shard_map/ppermute | solution.py:835
  534.7 23.2 %collective-permute-start.42 = (bf16[512,256]{1,0:T(8,128)(2,1)S(1)}, bf16[512,256]{1,0:T(8,128)(2,1)S(1)}, u32[]{:S(2)}, u32[]{:S(2)}) collective-permute-start(bf16[512,256]{1,0:T(8,128)(2,1)S(1)} %copy-done.31), channel_id=1, source_target_pairs={{0,16},{4,20},{8,24},{12,28},{16,0},{20,4},{24,8},{28,12},{1,17},{... | collective-permute-start | bytes 786440 | tf_op jit(solution)/shard_map/ppermute | solution.py:835
  (36 other events, 101.0 us)

commit v4 on v3

--- a/solution.py
+++ b/solution.py
@@ -302,34 +302,42 @@
     return jnp.where(low == (half == 0), pair, swapped)
 
 
-def attend_kernel(per_kv, q_ref, k_ref, v_ref, segq_ref, segk_ref, o_ref, lse_ref):
+def attend_kernel(per_kv, q_ref, k_ref, v_ref, segc_ref, segr_ref, o_ref, lse_ref, s_buf):
     half = (pl.program_id(1) // per_kv) % 2
     length = k_ref.shape[0]
     k, v = doubled(k_ref[...], half), doubled(v_ref[...], half)
     low = lane_index((TILE, LANES)) < HEAD_SIZE
-    q_at = lax.broadcasted_iota(jnp.int32, (TILE, TILE), 0)
-    k_at = lax.broadcasted_iota(jnp.int32, (TILE, TILE), 1)
+    k_at = lax.broadcasted_iota(jnp.int32, (TILE, TILE), 0)
+    q_at = lax.broadcasted_iota(jnp.int32, (TILE, TILE), 1)
     for i in range(length // TILE):
         rows = slice(i * TILE, (i + 1) * TILE)
-        reach = (i + 1) * TILE
         q = q_ref[rows, :]
-        same = segq_ref[rows, :] == segk_ref[:, :reach]
-        last = same[:, i * TILE :] & (k_at <= q_at)
-        allowed = jnp.concatenate([same[:, : i * TILE], last], axis=1) if i else last
         outs = []
         for head in range(2):
             mine = jnp.where(low == (head == 0), q, jnp.zeros_like(q))
-            raw = dot(mine, k[:reach], NT)
-            scores = jnp.where(allowed, MULTIPLIER * raw, MASK_VALUE)
-            top = jnp.max(scores, axis=1, keepdims=True)
-            e = jnp.exp(scores - top)
-            total = jnp.sum(e, axis=1, keepdims=True)
-            p = (e * (1.0 / total)).astype(LOW)
-            outs.append(dot(p, v[:reach]))
-            lse = top + jnp.log(total)
-            lse_ref[0, head : head + 1, rows] = jnp.transpose(
-                jnp.broadcast_to(lse, (TILE, LANES))
-            )[:1]
+            top = jnp.full((1, TILE), MASK_VALUE, WIDE)
+            for j in range(i + 1):
+                keys = slice(j * TILE, (j + 1) * TILE)
+                allowed = segc_ref[keys, :] == segr_ref[:, rows]
+                if i == j:
+                    allowed = allowed & (k_at <= q_at)
+                raw = dot(k[keys], mine, NT)
+                scores = jnp.where(allowed, MULTIPLIER * raw, MASK_VALUE)
+                top = jnp.maximum(top, jnp.max(scores, axis=0, keepdims=True))
+                s_buf[head, keys, :] = scores
+            total = jnp.zeros((1, TILE), WIDE)
+            for j in range(i + 1):
+                keys = slice(j * TILE, (j + 1) * TILE)
+                e = jnp.exp(s_buf[head, keys, :] - top)
+                total = total + jnp.sum(e, axis=0, keepdims=True)
+                s_buf[head, keys, :] = e
+            scale = 1.0 / total
+            out = jnp.zeros((TILE, LANES), WIDE)
+            for j in range(i + 1):
+                keys = slice(j * TILE, (j + 1) * TILE)
+                out = out + dot((s_buf[head, keys, :] * scale).astype(LOW), v[keys], TN)
+            outs.append(out)
+            lse_ref[0, head : head + 1, rows] = top + jnp.log(total)
         o_ref[rows, :] = jnp.where(low, outs[0], outs[1]).astype(LOW)
 
 
@@ -356,6 +364,7 @@
             jax.ShapeDtypeStruct((rows, q_width), LOW),
             jax.ShapeDtypeStruct((pairs, 2, rows), WIDE),
         ],
+        scratch_shapes=[pltpu.VMEM((2, length, TILE), WIDE)],
         cost_estimate=COST,
         name="attend",
     )(qkv, qkv, qkv, seg_col, seg_row)
@@ -1085,6 +1094,8 @@
 
     n2 = Shares(n2_own + n2_both + n2_four, group_masks, place)
     grad_down = Reduction(Shares(branch_shares, group_masks, place), mixed, group_masks, 1).step(lane)
+    grad_down = Reduction(Shares(branch_shares, group_masks, place), mixed, group_masks, 1).step(lane)
+    ffn_parts = lane(lambda m, w, at: down(m, w, at, share), mixed, w_down, at_array)
     dn_parts = lane(
         lambda dg, du, wg, wu, at: unmix(dg, du, wg, wu, at, share),
         d_gate,
@@ -1099,7 +1110,6 @@
     d_normed.start_far_pair(lane, dn_parts[0], dn_parts[2], dn_parts[3])
     grad_up = Reduction(n2, d_upper, group_masks, 0).step(lane)
     grad_down.step(lane)
-    ffn_parts = lane(lambda m, w, at: down(m, w, at, share), mixed, w_down, at_array)
     d_hidden, da_own, gain_two_part = lane(
         lambda c, h, i, g, *t: norm_back(c, h, i, g, t, WIDE),
         cotangent,
@@ -1134,14 +1144,16 @@
         seg_row,
         *tables,
     )
-    grad_qkv = Reduction(n1, d_qkv, masks, 0).step(lane)
-    grad_up.step(lane)
     out_total.start_far_pair(lane, ffn_parts[0], ffn_parts[2], ffn_parts[3])
     own_terms, far_terms = lane(
         lambda a, w, o: pieces(a, w, o, count, NT, "in_pieces"), d_qkv, w_qkv, order
     )
+    grad_qkv = Reduction(n1, d_qkv, masks, 0).step(lane)
     got_far = swap(lane(add_low, *far_terms), "tensor", FAR)
     grad_gate.step_half(lane)
+    grad_up.step(lane)
+    da = Shares([da_own, da_near, da_far, da_other], masks, place, order)
+    grad_wout = Reduction(da, attended, masks, 1).step(lane)
     grad_down = grad_down.finish_half(lane, at_array)
     grad_rows, _, gain_one_part = lane(
         lambda c, h, i, g, *t: norm_back(c, h, i, g, t, LOW),
@@ -1154,8 +1166,6 @@
     )
     grad_gate = grad_gate.finish_half(lane, at_array)
     grad_qkv.step(lane)
-    da = Shares([da_own, da_near, da_far, da_other], masks, place, order)
-    grad_wout = Reduction(da, attended, masks, 1).step(lane)
     grad_up.step_half(lane)
     out_rows = lane(
         lambda hidden, *terms: whole(

time: 573 us -> 564 us (0.984)
    unnamed x84 -> x82, local copies, waits for them, and re-layouts: 16.2 us -> 16.1 us
  transfers between devices with their start and end apart: 43 -> 43, of which waited for: 22 -> 24; matrix products, arithmetic and copies ran while one was open for 4% -> 4% of each run, Pallas kernels for 66% -> 68%
where the time goes in v4:
time: 564 us; the launch traced here: 555 us
  Pallas kernels  402 us (71%)
  waiting for transfers between devices  62.7 us (11%)
  starting transfers between devices  42.2 us (7%)
  local copies, waits for them, and re-layouts  29.1 us (5%)
  other arithmetic  16.2 us (3%)
    pallas_call x12, Pallas kernels, product_rows(): pl.pallas_call(kernel, grid_spec=pltpu.PrefetchScalarGridSpec(num_scalar_...  86.3 us
    pallas_call x4, Pallas kernels, paired(): pl.pallas_call(functools.partial(paired_kernel, compute, count, share), g...  70 us
    ppermute x42, waiting for transfers between devices, swap(): return lax.ppermute(array, axis, [(i, i ^ mask) for i in range(size)])  62.7 us
    pallas_call x8, Pallas kernels, product_cols(): pl.pallas_call(kernel, grid_spec=pltpu.PrefetchScalarGridSpec(num_scalar_...  52.1 us
    ppermute x42, starting transfers between devices, swap(): return lax.ppermute(array, axis, [(i, i ^ mask) for i in range(size)])  39.6 us
    pallas_call x3, Pallas kernels, mix(): pl.pallas_call(functools.partial(mix_kernel, count), grid_spec=pltpu.Pref...  37.4 us
    pallas_call x4, Pallas kernels, project(): pl.pallas_call(functools.partial(project_kernel, turned, dims), grid_spec...  34.3 us
    pallas_call x1, Pallas kernels, attend_back(): pl.pallas_call(functools.partial(attend_back_kernel, per_kv), grid=(seqs,...  26.7 us
  transfers between devices with their start and end apart: 43, of which 24 were waited for; matrix products, arithmetic and copies ran while one was open for 4% of the time, Pallas kernels for 68%

profile of v4, /device:TPU:16, one launch (start us, length us, event | category | flops | bytes accessed | tf_op | source)
XLA Modules:
  0.0 554.7 jit_solution(3047869336662453625)
XLA Ops:
  17.2 9.1 %near_in.1 = (bf16[1024,768]{1,0:T(8,128)(2,1)}, bf16[256,2048]{1,0:T(8,128)(2,1)}) custom-call(s32[2]{0:T(128)} %get-tuple-element.647.order_ref, bf16[256,2048]{1,0:T(8,128)(2,1)} %fusion.2.share_ref.refs_0_, bf16[2048,768]{1,0:T(8,128)(2,1)} %copy-done.7, f32[1024,128]{1,0:T(8,128)} %get-tuple-element.694.refs_0_.cos_ref, ...), custom_call_target="tpu_custom_call" | custom-call | flops 1 | bytes 1 | tf_op jit(solution)/shard_map/near_in/pallas_call | solution.py:167
  26.4 4.2 collective-permute-done.share_ref.refs_2_
  34.1 9.0 %far_in.1 = (bf16[1024,768]{1,0:T(8,128)(2,1)}, bf16[256,2048]{1,0:T(8,128)(2,1)}) custom-call(s32[2]{0:T(128)} %get-tuple-element.666.order_ref, bf16[256,2048]{1,0:T(8,128)(2,1)} %collective-permute-done.share_ref.refs_2_, bf16[2048,768]{1,0:T(8,128)(2,1)} %copy-done.7, ...), custom_call_target="tpu_custom_call", output_to_operand_aliasing={{0}: (5, {})} | custom-call | flops 1 | bytes 1 | tf_op jit(solution)/shard_map/far_in/pallas_call | solution.py:167
  44.1 18.5 %attend.1 = (bf16[1024,512]{1,0:T(8,128)(2,1)}, f32[4,2,1024]{2,1,0:T(2,128)}) custom-call(bf16[1024,768]{1,0:T(8,128)(2,1)} %get-tuple-element.689.q_ref.k_ref.v_ref, bf16[1024,768]{1,0:T(8,128)(2,1)} %get-tuple-element.689.q_ref.k_ref.v_ref, bf16[1024,768]{1,0:T(8,128)(2,1)} %get-tuple-element.689.q_ref.k_ref.v_ref, s32[1024,1]{1,0:T(8,128)} %copy.42.segc_ref, ...), custom_call_target="tpu_custom_call" | custom-call | flops 1 | bytes 1 | tf_op jit(solution)/shard_map/attend/pallas_call | solution.py:349
  62.6 10.9 %out_pieces.1 = (bf16[256,2048]{1,0:T(8,128)(2,1)}, bf16[256,2048]{1,0:T(8,128)(2,1)}, bf16[256,2048]{1,0:T(8,128)(2,1)}, bf16[256,2048]{1,0:T(8,128)(2,1)}) custom-call(s32[4]{0:T(128)} %copy-done.37, bf16[1024,512]{1,0:T(8,128)(2,1)} %get-tuple-element.891.refs_1_.refs_4_, bf16[512,2048]{1,0:T(8,128)(2,1)} %w_ref.1), custom_call_target="tpu_custom_call" | custom-call | flops 1 | bytes 1 | tf_op jit(solution)/shard_map/out_pieces/pallas_call | solution.py:251
  85.7 15.9 %branch.1.refs_4_.refs_6_ = f32[2048,1024]{1,0:T(8,128)} custom-call(s32[1]{0:T(128)} %bitcast.7.at_ref.refs_0_, bf16[256,2048]{1,0:T(8,128)(2,1)} %multiply_convert_fusion.1.refs_0_, bf16[256,2048]{1,0:T(8,128)(2,1)} %collective-permute-done.5.refs_1_, bf16[256,2048]{1,0:T(8,128)(2,1)} %copy-done.10, bf16[256,2048]{1,0:T(8,128)(2,1)} %collective-permute-done.6.refs_3_, ...), custom_call_target="tpu_custom_call" | custom-call | flops 1 | bytes 1 | tf_op jit(solution)/shard_map/branch/pallas_call | solution.py:504
  111.5 10.8 %mix.3 = (bf16[2048,1024]{1,0:T(8,128)(2,1)}, bf16[2048,1024]{1,0:T(8,128)(2,1)}, bf16[2048,1024]{1,0:T(8,128)(2,1)}) custom-call(s32[1]{0:T(128)} %bitcast.7.at_ref.refs_0_, bf16[256,2048]{1,0:T(8,128)(2,1)} %copy-done, bf16[256,2048]{1,0:T(8,128)(2,1)} %copy-done.3, bf16[2048,2048]{1,0:T(8,128)(2,1)} %refs_3_.1, bf16[2048,2048]{1,0:T(8,128)(2,1)} %refs_4_.2, ...), custom_call_target="tpu_custom_call" | custom-call | flops 1 | bytes 1 | tf_op jit(solution)/shard_map/mix/pallas_call | solution.py:547
  122.3 11.1 %collective-permute-done.10.refs_2_.refs_8_ = bf16[256,2048]{1,0:T(8,128)(2,1)S(1)} collective-permute-done((bf16[256,2048]{1,0:T(8,128)(2,1)S(1)}, bf16[256,2048]{1,0:T(8,128)(2,1)S(1)}, u32[]{:S(2)}, u32[]{:S(2)}) %collective-permute-start.10) | collective-permute-done | bytes 1048608 | tf_op jit(solution)/shard_map/ppermute | solution.py:844
  139.8 16.0 %mix.4 = (bf16[2048,1024]{1,0:T(8,128)(2,1)}, bf16[2048,1024]{1,0:T(8,128)(2,1)}, bf16[2048,1024]{1,0:T(8,128)(2,1)}) custom-call(s32[1]{0:T(128)} %bitcast.7.at_ref.refs_0_, bf16[256,2048]{1,0:T(8,128)(2,1)} %copy-done.2, bf16[256,2048]{1,0:T(8,128)(2,1)} %copy-done.4, ...), custom_call_target="tpu_custom_call", output_to_operand_aliasing={{0}: (8, {}), {1}: (9, {}), {2}: (10, {})} | custom-call | flops 1 | bytes 1 | tf_op jit(solution)/shard_map/mix/pallas_call | solution.py:547
  159.6 10.6 %mix.5 = (bf16[2048,1024]{1,0:T(8,128)(2,1)}, bf16[2048,1024]{1,0:T(8,128)(2,1)}, bf16[2048,1024]{1,0:T(8,128)(2,1)}) custom-call(s32[1]{0:T(128)} %bitcast.7.at_ref.refs_0_, bf16[128,2048]{1,0:T(8,128)(2,1)} %collective-permute-done.12.refs_0_.refs_2_, ...), custom_call_target="tpu_custom_call", output_to_operand_aliasing={{0}: (8, {}), {1}: (9, {}), {2}: (10, {})} | custom-call | flops 1 | bytes 1 | tf_op jit(solution)/shard_map/mix/pallas_call | solution.py:547
  170.2 10.6 %product_cols.9 = bf16[1024,1024]{1,0:T(8,128)(2,1)} custom-call(s32[8]{0:T(128)} %iota_multiply_fusion.starts_ref, s32[8]{0:T(128)} %broadcast_xor_fusion.1.blocks_ref, bf16[256,2048]{1,0:T(8,128)(2,1)} %multiply_convert_fusion.1.refs_0_, bf16[256,2048]{1,0:T(8,128)(2,1)} %collective-permute-done.5.refs_1_, bf16[256,2048]{1,0:T(8,128)(2,1)} %copy-done.10, ...), custom_call_target="tpu_custom_call" | custom-call | flops 1 | bytes 1 | tf_op jit(solution)/shard_map/product_cols/pallas_call | solution.py:693
  182.4 18.2 %down.1 = (bf16[256,2048]{1,0:T(8,128)(2,1)}, bf16[256,2048]{1,0:T(8,128)(2,1)}, bf16[256,2048]{1,0:T(8,128)(2,1)}, bf16[256,2048]{1,0:T(8,128)(2,1)}, bf16[256,...) custom-call(s32[1]{0:T(128)} %bitcast.7.at_ref.refs_0_, ...), custom_call_target="tpu_custom_call" | custom-call | flops 1 | bytes 1 | tf_op jit(solution)/shard_map/down/pallas_call | solution.py:251
  200.6 29.1 %unmix.1 = (bf16[256,2048]{1,0:T(8,128)(2,1)}, bf16[256,2048]{1,0:T(8,128)(2,1)}, bf16[256,2048]{1,0:T(8,128)(2,1)}, bf16[256,2048]{1,0:T(8,128)(2,1)}, bf16[256...) custom-call(s32[1]{0:T(128)} %bitcast.7.at_ref.refs_0_, ...), custom_call_target="tpu_custom_call" | custom-call | flops 1 | bytes 1 | tf_op jit(solution)/shard_map/unmix/pallas_call | solution.py:251
  234.5 10.7 %product_rows.12 = bf16[1024,1024]{1,0:T(8,128)(2,1)} custom-call(s32[10]{0:T(128)} %constant.73.clone.starts_ref, s32[8]{0:T(128)} %broadcast_xor_fusion.1.blocks_ref, bf16[256,2048]{1,0:T(8,128)(2,1)} %copy-done, bf16[256,2048]{1,0:T(8,128)(2,1)} %copy-done.3, bf16[128,2048]{1,0:T(8,128)(2,1)} %collective-permute-done.12.refs_0_.refs_2_, ...), custom_call_target="tpu_custom_call" | custom-call | flops 1 | bytes 1 | tf_op jit(solution)/shard_map/product_rows/pallas_call | solution.py:645
  248.2 5.4 whole.9
  255.6 10.7 %product_rows.13 = bf16[1024,1024]{1,0:T(8,128)(2,1)} custom-call(s32[10]{0:T(128)} %constant.73.clone.starts_ref, s32[8]{0:T(128)} %broadcast_xor_fusion.1.blocks_ref, bf16[256,2048]{1,0:T(8,128)(2,1)} %copy-done, bf16[256,2048]{1,0:T(8,128)(2,1)} %copy-done.3, bf16[128,2048]{1,0:T(8,128)(2,1)} %collective-permute-done.12.refs_0_.refs_2_, ...), custom_call_target="tpu_custom_call" | custom-call | flops 1 | bytes 1 | tf_op jit(solution)/shard_map/product_rows/pallas_call | solution.py:645
  267.7 8.2 %product_cols.10 = bf16[1024,512]{1,0:T(8,128)(2,1)} custom-call(s32[8]{0:T(128)} %iota_multiply_fusion.starts_ref, s32[8]{0:T(128)} %broadcast_xor_fusion.1.blocks_ref, bf16[256,2048]{1,0:T(8,128)(2,1)} %multiply_convert_fusion.1.refs_0_, bf16[256,2048]{1,0:T(8,128)(2,1)} %collective-permute-done.5.refs_1_, bf16[256,2048]{1,0:T(8,128)(2,1)} %copy-done.10, ...), custom_call_target="tpu_custom_call" | custom-call | flops 1 | bytes 1 | tf_op jit(solution)/shard_map/product_cols/pallas_call | solution.py:693
  280.1 5.9 %norm_back.2 = (f32[256,2048]{1,0:T(8,128)}, bf16[256,2048]{1,0:T(8,128)(2,1)}, f32[1,2048]{1,0:T(1,128)}) custom-call(bf16[256,2048]{1,0:T(8,128)(2,1)} %d_ref, f32[256,2048]{1,0:T(8,128)} %copy-done.9, f32[256,1]{1,0:T(8,128)} %copy.43.inverse_ref, bf16[1,2048]{1,0:T(2,128)(2,1)} %reshape.136.gain_ref, f32[256,2048]{1,0:T(8,128)} %get-tuple-element.641.refs_0_, ...), custom_call_target="tpu_custom_call" | custom-call | flops 1 | bytes 1 | tf_op jit(solution)/shard_map/norm_back/pallas_call | solution.py:782
  288.3 8.0 %near_back.1 = (bf16[1024,512]{1,0:T(8,128)(2,1)}, bf16[256,2048]{1,0:T(8,128)(2,1)}) custom-call(s32[2]{0:T(128)} %get-tuple-element.647.order_ref, bf16[256,2048]{1,0:T(8,128)(2,1)} %get-tuple-element.887.share_ref.refs_0_, bf16[512,2048]{1,0:T(8,128)(2,1)} %w_ref.1), custom_call_target="tpu_custom_call" | custom-call | flops 1 | bytes 1 | tf_op jit(solution)/shard_map/near_back/pallas_call | solution.py:167
  296.4 7.9 %product_rows.14 = bf16[512,1024]{1,0:T(8,128)(2,1)} custom-call(s32[10]{0:T(128)} %constant.73.clone.starts_ref, s32[8]{0:T(128)} %broadcast_xor_fusion.1.blocks_ref, bf16[256,2048]{1,0:T(8,128)(2,1)} %copy-done, bf16[256,2048]{1,0:T(8,128)(2,1)} %copy-done.3, bf16[128,2048]{1,0:T(8,128)(2,1)} %collective-permute-done.12.refs_0_.refs_2_, ...), custom_call_target="tpu_custom_call" | custom-call | flops 1 | bytes 1 | tf_op jit(solution)/shard_map/product_rows/pallas_call | solution.py:645
  304.3 5.2 collective-permute-done.23.share_ref.refs_2_
  310.4 8.2 %far_back.1 = (bf16[1024,512]{1,0:T(8,128)(2,1)}, bf16[256,2048]{1,0:T(8,128)(2,1)}) custom-call(s32[2]{0:T(128)} %get-tuple-element.666.order_ref, bf16[256,2048]{1,0:T(8,128)(2,1)} %copy-done.12, bf16[512,2048]{1,0:T(8,128)(2,1)} %w_ref.1, bf16[1024,512]{1,0:T(8,128)(2,1)} %get-tuple-element.669.refs_0_), custom_call_target="tpu_custom_call", output_to_operand_aliasing={{0}: (3, {})} | custom-call | flops 1 | bytes 1 | tf_op jit(solution)/shard_map/far_back/pallas_call | solution.py:167
  324.8 6.5 %collective-permute-done.27.refs_10_ = bf16[1024,512]{1,0:T(8,128)(2,1)} collective-permute-done((bf16[1024,512]{1,0:T(8,128)(2,1)}, bf16[1024,512]{1,0:T(8,128)(2,1)}, u32[]{:S(2)}, u32[]{:S(2)}) %collective-permute-start.27) | collective-permute-done | bytes 1048608 | tf_op jit(solution)/shard_map/ppermute | solution.py:844
  331.3 7.0 %product_cols.11 = bf16[1024,256]{1,0:T(8,128)(2,1)} custom-call(s32[8]{0:T(128)} %iota_multiply_fusion.starts_ref, s32[8]{0:T(128)} %broadcast_xor_fusion.1.blocks_ref, bf16[256,2048]{1,0:T(8,128)(2,1)} %multiply_convert_fusion.1.refs_0_, bf16[256,2048]{1,0:T(8,128)(2,1)} %collective-permute-done.5.refs_1_, bf16[256,2048]{1,0:T(8,128)(2,1)} %copy-done.10, ...), custom_call_target="tpu_custom_call" | custom-call | flops 1 | bytes 1 | tf_op jit(solution)/shard_map/product_cols/pallas_call | solution.py:693
  339.4 26.7 %attend_back.1.refs_1_.refs_4_ = bf16[1024,768]{1,0:T(8,128)(2,1)} custom-call(bf16[1024,768]{1,0:T(8,128)(2,1)} %get-tuple-element.689.q_ref.k_ref.v_ref, bf16[1024,768]{1,0:T(8,128)(2,1)} %get-tuple-element.689.q_ref.k_ref.v_ref, bf16[1024,768]{1,0:T(8,128)(2,1)} %get-tuple-element.689.q_ref.k_ref.v_ref, bf16[1024,512]{1,0:T(8,128)(2,1)} %get-tuple-element.690.g_ref, ...), custom_call_target="tpu_custom_call" | custom-call | flops 1 | bytes 1 | tf_op jit(solution)/shard_map/attend_back/pallas_call | solution.py:463
  366.1 5.3 whole.11
  371.4 11.8 %in_pieces.1 = (bf16[256,2048]{1,0:T(8,128)(2,1)}, bf16[256,2048]{1,0:T(8,128)(2,1)}, bf16[256,2048]{1,0:T(8,128)(2,1)}, bf16[256,2048]{1,0:T(8,128)(2,1)}) custom-call(s32[4]{0:T(128)} %copy-done.37, bf16[1024,768]{1,0:T(8,128)(2,1)} %attend_back.1.refs_1_.refs_4_, bf16[2048,768]{1,0:T(8,128)(2,1)} %copy-done.7), custom_call_target="tpu_custom_call" | custom-call | flops 1 | bytes 1 | tf_op jit(solution)/shard_map/in_pieces/pallas_call | solution.py:251
  383.2 7.0 %product_rows.15 = bf16[1024,768]{1,0:T(8,128)(2,1)} custom-call(s32[4]{0:T(128)} %broadcast_multiply_fusion.starts_ref, s32[8]{0:T(128)} %broadcast_xor_fusion.blocks_ref, bf16[256,2048]{1,0:T(8,128)(2,1)} %fusion.2.share_ref.refs_0_, bf16[256,2048]{1,0:T(8,128)(2,1)} %get-tuple-element.876.refs_1_, ...), custom_call_target="tpu_custom_call" | custom-call | flops 1 | bytes 1 | tf_op jit(solution)/shard_map/product_rows/pallas_call | solution.py:645
  394.9 3.9 collective-permute-start.35
  399.8 6.6 %product_rows.16 = bf16[256,1024]{1,0:T(8,128)(2,1)} custom-call(s32[10]{0:T(128)} %constant.73.clone.starts_ref, s32[8]{0:T(128)} %broadcast_xor_fusion.1.blocks_ref, bf16[256,2048]{1,0:T(8,128)(2,1)} %copy-done, bf16[256,2048]{1,0:T(8,128)(2,1)} %copy-done.3, bf16[128,2048]{1,0:T(8,128)(2,1)} %collective-permute-done.12.refs_0_.refs_2_, ...), custom_call_target="tpu_custom_call" | custom-call | flops 1 | bytes 1 | tf_op jit(solution)/shard_map/product_rows/pallas_call | solution.py:645
  407.9 7.9 %product_rows.17 = bf16[512,1024]{1,0:T(8,128)(2,1)} custom-call(s32[10]{0:T(128)} %constant.73.clone.starts_ref, s32[8]{0:T(128)} %broadcast_xor_fusion.1.blocks_ref, bf16[256,2048]{1,0:T(8,128)(2,1)} %copy-done, bf16[256,2048]{1,0:T(8,128)(2,1)} %copy-done.3, bf16[128,2048]{1,0:T(8,128)(2,1)} %collective-permute-done.12.refs_0_.refs_2_, ...), custom_call_target="tpu_custom_call" | custom-call | flops 1 | bytes 1 | tf_op jit(solution)/shard_map/product_rows/pallas_call | solution.py:645
  418.1 5.7 %collective-permute-done.36.other_ref = bf16[256,1024]{1,0:T(8,128)(2,1)S(1)} collective-permute-done((bf16[256,1024]{1,0:T(8,128)(2,1)}, bf16[256,1024]{1,0:T(8,128)(2,1)S(1)}, u32[]{:S(2)}, u32[]{:S(2)}) %collective-permute-start.36) | collective-permute-done | bytes 524320 | tf_op jit(solution)/shard_map/ppermute | solution.py:844
  426.1 5.7 %product_cols.12 = bf16[512,1024]{1,0:T(8,128)(2,1)} custom-call(s32[4]{0:T(128)} %broadcast_multiply_fusion.starts_ref, s32[8]{0:T(128)} %broadcast_xor_fusion.blocks_ref, bf16[256,2048]{1,0:T(8,128)(2,1)} %get-tuple-element.887.share_ref.refs_0_, bf16[256,2048]{1,0:T(8,128)(2,1)} %get-tuple-element.888.refs_1_, bf16[256,2048]{1,0:T(8,128)(2,1)} %copy-done.12, ...), custom_call_target="tpu_custom_call" | custom-call | flops 1 | bytes 1 | tf_op jit(solution)/shard_map/product_cols/pallas_call | solution.py:693
  433.4 7.1 %product_cols.13.own_ref = f32[1024,256]{1,0:T(8,128)} custom-call(s32[8]{0:T(128)} %iota_multiply_fusion.starts_ref, s32[8]{0:T(128)} %broadcast_xor_fusion.1.blocks_ref, bf16[256,2048]{1,0:T(8,128)(2,1)} %multiply_convert_fusion.1.refs_0_, bf16[256,2048]{1,0:T(8,128)(2,1)} %collective-permute-done.5.refs_1_, bf16[256,2048]{1,0:T(8,128)(2,1)} %copy-done.10, ...), custom_call_target="tpu_custom_call" | custom-call | flops 1 | bytes 1 | tf_op jit(solution)/shard_map/product_cols/pallas_call | solution.py:693
  444.7 5.2 norm_back.3
  450.0 6.8 %product_rows.18.own_ref = f32[256,1024]{1,0:T(8,128)} custom-call(s32[10]{0:T(128)} %constant.73.clone.starts_ref, s32[8]{0:T(128)} %broadcast_xor_fusion.1.blocks_ref, bf16[256,2048]{1,0:T(8,128)(2,1)} %copy-done, bf16[256,2048]{1,0:T(8,128)(2,1)} %copy-done.3, bf16[128,2048]{1,0:T(8,128)(2,1)} %collective-permute-done.12.refs_0_.refs_2_, ...), custom_call_target="tpu_custom_call" | custom-call | flops 1 | bytes 1 | tf_op jit(solution)/shard_map/product_rows/pallas_call | solution.py:645
  459.6 5.4 product_rows.19
  466.1 6.6 %product_rows.20 = bf16[256,1024]{1,0:T(8,128)(2,1)} custom-call(s32[10]{0:T(128)} %constant.73.clone.starts_ref, s32[8]{0:T(128)} %broadcast_xor_fusion.1.blocks_ref, bf16[256,2048]{1,0:T(8,128)(2,1)} %copy-done, bf16[256,2048]{1,0:T(8,128)(2,1)} %copy-done.3, bf16[128,2048]{1,0:T(8,128)(2,1)} %collective-permute-done.12.refs_0_.refs_2_, ...), custom_call_target="tpu_custom_call" | custom-call | flops 1 | bytes 1 | tf_op jit(solution)/shard_map/product_rows/pallas_call | solution.py:645
  474.8 4.2 whole.13
  480.0 4.8 product_cols.14
  487.9 4.8 product_rows.21
  494.5 6.8 %product_rows.22.own_ref = f32[256,1024]{1,0:T(8,128)} custom-call(s32[10]{0:T(128)} %constant.73.clone.starts_ref, s32[8]{0:T(128)} %broadcast_xor_fusion.1.blocks_ref, bf16[256,2048]{1,0:T(8,128)(2,1)} %copy-done, bf16[256,2048]{1,0:T(8,128)(2,1)} %copy-done.3, bf16[128,2048]{1,0:T(8,128)(2,1)} %collective-permute-done.12.refs_0_.refs_2_, ...), custom_call_target="tpu_custom_call" | custom-call | flops 1 | bytes 1 | tf_op jit(solution)/shard_map/product_rows/pallas_call | solution.py:645
  501.3 5.3 collective-permute-done.41.other_ref
  510.2 5.4 collective-permute-done.40.refs_6_
  516.4 4.3 product_cols.15
  523.5 5.1 product_rows.23
  529.2 15.9 %sum_all.1 = f32[2,2048]{1,0:T(2,128)} custom-call(f32[2,2048]{1,0:T(2,128)} %pad_maximum_fusion.2.part_ref), custom_call_target="tpu_custom_call" | custom-call | flops 1 | bytes 1 | tf_op jit(solution)/shard_map/sum_all/pallas_call | solution.py:825
  550.0 4.4 product_cols.16
  (206 shorter events, 122.1 us)
Async XLA Ops:
  5.4 25.2 %collective-permute-start = (bf16[256,2048]{1,0:T(8,128)(2,1)}, bf16[256,2048]{1,0:T(8,128)(2,1)}, u32[]{:S(2)}, u32[]{:S(2)}) collective-permute-start(bf16[256,2048]{1,0:T(8,128)(2,1)} %fusion.2.share_ref.refs_0_), channel_id=1, source_target_pairs={{0,2},{1,3},{2,0},{3,1},{4,6},{5,7},{6,4},{7,5},{8,10},{9,11},{10,... | collective-permute-start | bytes 3145736 | tf_op jit(solution)/shard_map/ppermute | solution.py:844
  30.6 45.8 %collective-permute-start.2 = (bf16[256,2048]{1,0:T(8,128)(2,1)}, bf16[256,2048]{1,0:T(8,128)(2,1)S(1)}, u32[]{:S(2)}, u32[]{:S(2)}) collective-permute-start(bf16[256,2048]{1,0:T(8,128)(2,1)} %multiply_convert_fusion.1.refs_0_), channel_id=1, source_target_pairs={{0,10},{1,11},{2,8},{3,9},{4,14},{5,15},{6,12},{7,13},{8,2},{9,3},... | collective-permute-start | bytes 3145736 | tf_op jit(solution)/shard_map/ppermute | solution.py:855
  33.1 45.1 %collective-permute-start.3 = (bf16[256,2048]{1,0:T(8,128)(2,1)}, bf16[256,2048]{1,0:T(8,128)(2,1)S(1)}, u32[]{:S(2)}, u32[]{:S(2)}) collective-permute-start(bf16[256,2048]{1,0:T(8,128)(2,1)} %multiply_convert_fusion.1.refs_0_), channel_id=1, source_target_pairs={{0,2},{1,3},{2,0},{3,1},{4,6},{5,7},{6,4},{7,5},{8,10},{9,11},{10,... | collective-permute-start | bytes 3145736 | tf_op jit(solution)/shard_map/ppermute | solution.py:844
  33.7 44.7 %collective-permute-start.4 = (bf16[256,2048]{1,0:T(8,128)(2,1)}, bf16[256,2048]{1,0:T(8,128)(2,1)}, u32[]{:S(2)}, u32[]{:S(2)}) collective-permute-start(bf16[256,2048]{1,0:T(8,128)(2,1)} %multiply_convert_fusion.1.refs_0_), channel_id=1, source_target_pairs={{0,8},{4,12},{8,0},{12,4},{16,24},{20,28},{24,16},{28,20},{1,9},{5... | collective-permute-start | bytes 3145736 | tf_op jit(solution)/shard_map/ppermute | solution.py:844
  76.4 9.3 %copy-start.10 = (bf16[256,2048]{1,0:T(8,128)(2,1)}, bf16[256,2048]{1,0:T(8,128)(2,1)S(1)}, u32[]{:S(2)}) copy-start(bf16[256,2048]{1,0:T(8,128)(2,1)S(1)} %collective-permute-done.2.refs_2_) | copy-start | bytes 3145732
  78.4 2.8 collective-permute-start.5
  78.4 5.8 %collective-permute-start.6 = (bf16[256,2048]{1,0:T(8,128)(2,1)S(1)}, bf16[256,2048]{1,0:T(8,128)(2,1)}, u32[]{:S(2)}, u32[]{:S(2)}) collective-permute-start(bf16[256,2048]{1,0:T(8,128)(2,1)S(1)} %collective-permute-done.2.refs_2_), channel_id=1, source_target_pairs={{0,1},{1,0},{2,3},{3,2},{4,5},{5,4},{6,7},{7,6},{8,9},{9,8},{10,11... | collective-permute-start | bytes 3145736 | tf_op jit(solution)/shard_map/ppermute | solution.py:844
  78.9 6.8 %collective-permute-start.7 = (bf16[256,2048]{1,0:T(8,128)(2,1)S(1)}, bf16[256,2048]{1,0:T(8,128)(2,1)}, u32[]{:S(2)}, u32[]{:S(2)}) collective-permute-start(bf16[256,2048]{1,0:T(8,128)(2,1)S(1)} %collective-permute-done.3.refs_4_), channel_id=1, source_target_pairs={{0,1},{1,0},{2,3},{3,2},{4,5},{5,4},{6,7},{7,6},{8,9},{9,8},{10,11... | collective-permute-start | bytes 3145736 | tf_op jit(solution)/shard_map/ppermute | solution.py:844
  78.9 6.8 %collective-permute-start.8 = (bf16[256,2048]{1,0:T(8,128)(2,1)}, bf16[256,2048]{1,0:T(8,128)(2,1)}, u32[]{:S(2)}, u32[]{:S(2)}) collective-permute-start(bf16[256,2048]{1,0:T(8,128)(2,1)} %collective-permute-done.4.refs_6_), channel_id=1, source_target_pairs={{0,1},{1,0},{2,3},{3,2},{4,5},{5,4},{6,7},{7,6},{8,9},{9,8},{10,11... | collective-permute-start | bytes 3145736 | tf_op jit(solution)/shard_map/ppermute | solution.py:844
  79.4 25.4 %collective-permute-start.1 = (bf16[256,2048]{1,0:T(8,128)(2,1)}, bf16[256,2048]{1,0:T(8,128)(2,1)}, u32[]{:S(2)}, u32[]{:S(2)}) collective-permute-start(bf16[256,2048]{1,0:T(8,128)(2,1)} %whole.7), channel_id=1, source_target_pairs={{0,2},{1,3},{2,0},{3,1},{4,6},{5,7},{6,4},{7,5},{8,10},{9,11},{10,... | collective-permute-start | bytes 3145736 | tf_op jit(solution)/shard_map/ppermute | solution.py:844
  85.7 19.1 %copy-start.15 = (bf16[256,2048]{1,0:T(8,128)(2,1)S(1)}, bf16[256,2048]{1,0:T(8,128)(2,1)}, u32[]{:S(2)}) copy-start(bf16[256,2048]{1,0:T(8,128)(2,1)} %value_ref) | copy-start | bytes 3145732
  107.7 2.7 collective-permute-start.11
  107.8 25.6 %collective-permute-start.10 = (bf16[256,2048]{1,0:T(8,128)(2,1)S(1)}, bf16[256,2048]{1,0:T(8,128)(2,1)S(1)}, u32[]{:S(2)}, u32[]{:S(2)}) collective-permute-start(bf16[256,2048]{1,0:T(8,128)(2,1)S(1)} %multiply_convert_fusion.refs_0_), channel_id=1, source_target_pairs={{0,8},{4,12},{8,0},{12,4},{16,24},{20,28},{24,16},{28,20},{1,9},{5... | collective-permute-start | bytes 3145736 | tf_op jit(solution)/shard_map/ppermute | solution.py:844
  109.5 25.2 %collective-permute-start.9 = (bf16[256,2048]{1,0:T(8,128)(2,1)S(1)}, bf16[256,2048]{1,0:T(8,128)(2,1)S(1)}, u32[]{:S(2)}, u32[]{:S(2)}) collective-permute-start(bf16[256,2048]{1,0:T(8,128)(2,1)S(1)} %multiply_convert_fusion.refs_0_), channel_id=1, source_target_pairs={{0,2},{1,3},{2,0},{3,1},{4,6},{5,7},{6,4},{7,5},{8,10},{9,11},{10,... | collective-permute-start | bytes 3145736 | tf_op jit(solution)/shard_map/ppermute | solution.py:844
  134.7 4.1 collective-permute-start.14
  134.7 4.3 collective-permute-start.15
  136.9 20.1 %copy-start.39 = (s32[8]{0:T(128)S(1)}, s32[8]{0:T(128)}, u32[]{:S(2)}) copy-start(s32[8]{0:T(128)} %constant.72.clone) | copy-start | bytes 100
  136.9 18.9 %collective-permute-start.12 = (bf16[128,2048]{1,0:T(8,128)(2,1)}, bf16[128,2048]{1,0:T(8,128)(2,1)}, u32[]{:S(2)}, u32[]{:S(2)}) collective-permute-start(bf16[128,2048]{1,0:T(8,128)(2,1)} %slice.47), channel_id=1, source_target_pairs={{0,2},{1,3},{2,0},{3,1},{4,6},{5,7},{6,4},{7,5},{8,10},{9,11},{10,... | collective-permute-start | bytes 1572872 | tf_op jit(solution)/shard_map/ppermute | solution.py:844
  137.6 18.2 %collective-permute-start.13 = (bf16[128,2048]{1,0:T(8,128)(2,1)}, bf16[128,2048]{1,0:T(8,128)(2,1)}, u32[]{:S(2)}, u32[]{:S(2)}) collective-permute-start(bf16[128,2048]{1,0:T(8,128)(2,1)} %slice.48), channel_id=1, source_target_pairs={{0,8},{4,12},{8,0},{12,4},{16,24},{20,28},{24,16},{28,20},{1,9},{5... | collective-permute-start | bytes 1572872 | tf_op jit(solution)/shard_map/ppermute | solution.py:844
  155.8 2.2 collective-permute-start.16
  156.0 2.7 collective-permute-start.17
  180.8 85.6 %collective-permute-start.22 = (bf16[1024,1024]{1,0:T(8,128)(2,1)}, bf16[1024,1024]{1,0:T(8,128)(2,1)S(1)}, u32[]{:S(2)}, u32[]{:S(2)}) collective-permute-start(bf16[1024,1024]{1,0:T(8,128)(2,1)} %product_cols.9), channel_id=1, source_target_pairs={{0,4},{4,0},{8,12},{12,8},{16,20},{20,16},{24,28},{28,24},{1,5},{5... | collective-permute-start | bytes 6291464 | tf_op jit(solution)/shard_map/ppermute | solution.py:844
  232.4 14.2 %collective-permute-start.18 = (bf16[128,2048]{1,0:T(8,128)(2,1)}, bf16[128,2048]{1,0:T(8,128)(2,1)S(1)}, u32[]{:S(2)}, u32[]{:S(2)}) collective-permute-start(bf16[128,2048]{1,0:T(8,128)(2,1)} %get-tuple-element.586), channel_id=1, source_target_pairs={{0,8},{4,12},{8,0},{12,4},{16,24},{20,28},{24,16},{28,20},{1,9},{5... | collective-permute-start | bytes 1572872 | tf_op jit(solution)/shard_map/ppermute | solution.py:844
  233.1 13.9 %collective-permute-start.19 = (bf16[128,2048]{1,0:T(8,128)(2,1)}, bf16[128,2048]{1,0:T(8,128)(2,1)S(1)}, u32[]{:S(2)}, u32[]{:S(2)}) collective-permute-start(bf16[128,2048]{1,0:T(8,128)(2,1)} %get-tuple-element.587), channel_id=1, source_target_pairs={{0,2},{1,3},{2,0},{3,1},{4,6},{5,7},{6,4},{7,5},{8,10},{9,11},{10,... | collective-permute-start | bytes 1572872 | tf_op jit(solution)/shard_map/ppermute | solution.py:844
  245.2 51.2 %collective-permute-start.24 = (bf16[1024,1024]{1,0:T(8,128)(2,1)}, bf16[1024,1024]{1,0:T(8,128)(2,1)}, u32[]{:S(2)}, u32[]{:S(2)}) collective-permute-start(bf16[1024,1024]{1,0:T(8,128)(2,1)} %product_rows.12), channel_id=1, source_target_pairs={{0,4},{4,0},{8,12},{12,8},{16,20},{20,16},{24,28},{28,24},{1,5},{5... | collective-permute-start | bytes 6291464 | tf_op jit(solution)/shard_map/ppermute | solution.py:844
  253.5 24.6 %collective-permute-start.20 = (bf16[256,2048]{1,0:T(8,128)(2,1)}, bf16[256,2048]{1,0:T(8,128)(2,1)S(1)}, u32[]{:S(2)}, u32[]{:S(2)}) collective-permute-start(bf16[256,2048]{1,0:T(8,128)(2,1)} %get-tuple-element.610), channel_id=1, source_target_pairs={{0,2},{1,3},{2,0},{3,1},{4,6},{5,7},{6,4},{7,5},{8,10},{9,11},{10,... | collective-permute-start | bytes 3145736 | tf_op jit(solution)/shard_map/ppermute | solution.py:844
  254.6 24.1 %collective-permute-start.21 = (bf16[256,2048]{1,0:T(8,128)(2,1)}, bf16[256,2048]{1,0:T(8,128)(2,1)}, u32[]{:S(2)}, u32[]{:S(2)}) collective-permute-start(bf16[256,2048]{1,0:T(8,128)(2,1)} %get-tuple-element.611), channel_id=1, source_target_pairs={{0,8},{4,12},{8,0},{12,4},{16,24},{20,28},{24,16},{28,20},{1,9},{5... | collective-permute-start | bytes 3145736 | tf_op jit(solution)/shard_map/ppermute | solution.py:844
  286.0 23.5 %collective-permute-start.23 = (bf16[256,2048]{1,0:T(8,128)(2,1)}, bf16[256,2048]{1,0:T(8,128)(2,1)S(1)}, u32[]{:S(2)}, u32[]{:S(2)}) collective-permute-start(bf16[256,2048]{1,0:T(8,128)(2,1)} %get-tuple-element.887.share_ref.refs_0_), channel_id=1, source_target_pairs={{0,2},{1,3},{2,0},{3,1},{4,6},{5,7},{6,4},{7,5},{8,10},{9,11},{10,... | collective-permute-start | bytes 3145736 | tf_op jit(solution)/shard_map/ppermute | solution.py:844
  287.3 44.0 %collective-permute-start.27 = (bf16[1024,512]{1,0:T(8,128)(2,1)}, bf16[1024,512]{1,0:T(8,128)(2,1)}, u32[]{:S(2)}, u32[]{:S(2)}) collective-permute-start(bf16[1024,512]{1,0:T(8,128)(2,1)} %product_cols.10), channel_id=1, source_target_pairs={{0,16},{4,20},{8,24},{12,28},{16,0},{20,4},{24,8},{28,12},{1,17},{... | collective-permute-start | bytes 3145736 | tf_op jit(solution)/shard_map/ppermute | solution.py:844
  287.7 118.9 %collective-permute-start.30 = (bf16[1024,1024]{1,0:T(8,128)(2,1)}, bf16[1024,1024]{1,0:T(8,128)(2,1)S(1)}, u32[]{:S(2)}, u32[]{:S(2)}) collective-permute-start(bf16[1024,1024]{1,0:T(8,128)(2,1)} %product_rows.13), channel_id=1, source_target_pairs={{0,4},{4,0},{8,12},{12,8},{16,20},{20,16},{24,28},{28,24},{1,5},{5... | collective-permute-start | bytes 6291464 | tf_op jit(solution)/shard_map/ppermute | solution.py:844
  321.2 44.8 %collective-permute-start.25 = (bf16[128,2048]{1,0:T(8,128)(2,1)}, bf16[128,2048]{1,0:T(8,128)(2,1)}, u32[]{:S(2)}, u32[]{:S(2)}) collective-permute-start(bf16[128,2048]{1,0:T(8,128)(2,1)} %get-tuple-element.674), channel_id=1, source_target_pairs={{0,8},{4,12},{8,0},{12,4},{16,24},{20,28},{24,16},{28,20},{1,9},{5... | collective-permute-start | bytes 1572872 | tf_op jit(solution)/shard_map/ppermute | solution.py:844
  322.6 43.5 %collective-permute-start.26 = (bf16[128,2048]{1,0:T(8,128)(2,1)}, bf16[128,2048]{1,0:T(8,128)(2,1)}, u32[]{:S(2)}, u32[]{:S(2)}) collective-permute-start(bf16[128,2048]{1,0:T(8,128)(2,1)} %get-tuple-element.675), channel_id=1, source_target_pairs={{0,2},{1,3},{2,0},{3,1},{4,6},{5,7},{6,4},{7,5},{8,10},{9,11},{10,... | collective-permute-start | bytes 1572872 | tf_op jit(solution)/shard_map/ppermute | solution.py:844
  323.4 75.4 %collective-permute-start.31 = (bf16[512,1024]{1,0:T(8,128)(2,1)}, bf16[512,1024]{1,0:T(8,128)(2,1)S(1)}, u32[]{:S(2)}, u32[]{:S(2)}) collective-permute-start(bf16[512,1024]{1,0:T(8,128)(2,1)} %product_rows.14), channel_id=1, source_target_pairs={{0,16},{4,20},{8,24},{12,28},{16,0},{20,4},{24,8},{28,12},{1,17},{... | collective-permute-start | bytes 3145736 | tf_op jit(solution)/shard_map/ppermute | solution.py:844
  324.8 13.5 %copy-start.32 = (s32[1,1024]{1,0:T(1,128)S(1)}, s32[1,1024]{1,0:T(1,128)}, u32[]{:S(2)}) copy-start(s32[1,1024]{1,0:T(1,128)} %param.20) | copy-start | bytes 12292
  390.3 69.3 %collective-permute-start.33 = (bf16[1024,768]{1,0:T(8,128)(2,1)}, bf16[1024,768]{1,0:T(8,128)(2,1)}, u32[]{:S(2)}, u32[]{:S(2)}) collective-permute-start(bf16[1024,768]{1,0:T(8,128)(2,1)} %product_rows.15), channel_id=1, source_target_pairs={{0,4},{4,0},{8,12},{12,8},{16,20},{20,16},{24,28},{28,24},{1,5},{5... | collective-permute-start | bytes 4718600 | tf_op jit(solution)/shard_map/ppermute | solution.py:844
  393.6 38.2 %collective-permute-start.34 = (bf16[256,2048]{1,0:T(8,128)(2,1)}, bf16[256,2048]{1,0:T(8,128)(2,1)}, u32[]{:S(2)}, u32[]{:S(2)}) collective-permute-start(bf16[256,2048]{1,0:T(8,128)(2,1)} %whole.12), channel_id=1, source_target_pairs={{0,2},{1,3},{2,0},{3,1},{4,6},{5,7},{6,4},{7,5},{8,10},{9,11},{10,... | collective-permute-start | bytes 3145736 | tf_op jit(solution)/shard_map/ppermute | solution.py:844
  394.9 22.5 %collective-permute-start.35 = (bf16[1024,256]{1,0:T(8,128)(2,1)}, bf16[1024,256]{1,0:T(8,128)(2,1)}, u32[]{:S(2)}, u32[]{:S(2)}) collective-permute-start(bf16[1024,256]{1,0:T(8,128)(2,1)} %product_cols.11), channel_id=1, source_target_pairs={{0,8},{4,12},{8,0},{12,4},{16,24},{20,28},{24,16},{28,20},{1,9},{5... | collective-permute-start | bytes 1572872 | tf_op jit(solution)/shard_map/ppermute | solution.py:844
  406.4 17.3 %collective-permute-start.36 = (bf16[256,1024]{1,0:T(8,128)(2,1)}, bf16[256,1024]{1,0:T(8,128)(2,1)S(1)}, u32[]{:S(2)}, u32[]{:S(2)}) collective-permute-start(bf16[256,1024]{1,0:T(8,128)(2,1)} %product_rows.16), channel_id=1, source_target_pairs={{0,8},{4,12},{8,0},{12,4},{16,24},{20,28},{24,16},{28,20},{1,9},{5... | collective-permute-start | bytes 1572872 | tf_op jit(solution)/shard_map/ppermute | solution.py:844
  415.8 49.3 %collective-permute-start.32 = (bf16[512,1024]{1,0:T(8,128)(2,1)}, bf16[512,1024]{1,0:T(8,128)(2,1)S(1)}, u32[]{:S(2)}, u32[]{:S(2)}) collective-permute-start(bf16[512,1024]{1,0:T(8,128)(2,1)} %product_rows.17), channel_id=1, source_target_pairs={{0,16},{4,20},{8,24},{12,28},{16,0},{20,4},{24,8},{28,12},{1,17},{... | collective-permute-start | bytes 3145736 | tf_op jit(solution)/shard_map/ppermute | solution.py:844
  417.4 57.4 %collective-permute-start.28 = (bf16[256,2048]{1,0:T(8,128)(2,1)}, bf16[256,2048]{1,0:T(8,128)(2,1)}, u32[]{:S(2)}, u32[]{:S(2)}) collective-permute-start(bf16[256,2048]{1,0:T(8,128)(2,1)} %get-tuple-element.705), channel_id=1, source_target_pairs={{0,2},{1,3},{2,0},{3,1},{4,6},{5,7},{6,4},{7,5},{8,10},{9,11},{10,... | collective-permute-start | bytes 3145736 | tf_op jit(solution)/shard_map/ppermute | solution.py:844
  423.7 8.1 %copy-start.27 = (bf16[256,1024]{1,0:T(8,128)(2,1)}, bf16[256,1024]{1,0:T(8,128)(2,1)S(1)}, u32[]{:S(2)}) copy-start(bf16[256,1024]{1,0:T(8,128)(2,1)S(1)} %collective-permute-done.36.other_ref) | copy-start | bytes 1572868
  423.7 51.0 %collective-permute-start.29 = (bf16[256,2048]{1,0:T(8,128)(2,1)}, bf16[256,2048]{1,0:T(8,128)(2,1)}, u32[]{:S(2)}, u32[]{:S(2)}) collective-permute-start(bf16[256,2048]{1,0:T(8,128)(2,1)} %get-tuple-element.706), channel_id=1, source_target_pairs={{0,8},{4,12},{8,0},{12,4},{16,24},{20,28},{24,16},{28,20},{1,9},{5... | collective-permute-start | bytes 3145736 | tf_op jit(solution)/shard_map/ppermute | solution.py:844
  431.9 47.1 %collective-permute-start.38 = (bf16[512,1024]{1,0:T(8,128)(2,1)}, bf16[512,1024]{1,0:T(8,128)(2,1)S(1)}, u32[]{:S(2)}, u32[]{:S(2)}) collective-permute-start(bf16[512,1024]{1,0:T(8,128)(2,1)} %product_cols.12), channel_id=1, source_target_pairs={{0,4},{4,0},{8,12},{12,8},{16,20},{20,16},{24,28},{28,24},{1,5},{5... | collective-permute-start | bytes 3145736 | tf_op jit(solution)/shard_map/ppermute | solution.py:844
  465.0 21.9 %collective-permute-start.37 = (bf16[512,768]{1,0:T(8,128)(2,1)}, bf16[512,768]{1,0:T(8,128)(2,1)S(1)}, u32[]{:S(2)}, u32[]{:S(2)}) collective-permute-start(bf16[512,768]{1,0:T(8,128)(2,1)} %product_rows.19), channel_id=1, source_target_pairs={{0,8},{4,12},{8,0},{12,4},{16,24},{20,28},{24,16},{28,20},{1,9},{5... | collective-permute-start | bytes 2359304 | tf_op jit(solution)/shard_map/ppermute | solution.py:844
  472.7 33.9 %collective-permute-start.41 = (bf16[256,1024]{1,0:T(8,128)(2,1)}, bf16[256,1024]{1,0:T(8,128)(2,1)S(1)}, u32[]{:S(2)}, u32[]{:S(2)}) collective-permute-start(bf16[256,1024]{1,0:T(8,128)(2,1)} %product_rows.20), channel_id=1, source_target_pairs={{0,8},{4,12},{8,0},{12,4},{16,24},{20,28},{24,16},{28,20},{1,9},{5... | collective-permute-start | bytes 1572872 | tf_op jit(solution)/shard_map/ppermute | solution.py:844
  484.8 30.8 %collective-permute-start.40 = (bf16[512,512]{1,0:T(8,128)(2,1)}, bf16[512,512]{1,0:T(8,128)(2,1)S(1)}, u32[]{:S(2)}, u32[]{:S(2)}) collective-permute-start(bf16[512,512]{1,0:T(8,128)(2,1)} %product_cols.14), channel_id=1, source_target_pairs={{0,8},{4,12},{8,0},{12,4},{16,24},{20,28},{24,16},{28,20},{1,9},{5... | collective-permute-start | bytes 1572872 | tf_op jit(solution)/shard_map/ppermute | solution.py:844
  492.6 30.1 %collective-permute-start.39 = (bf16[256,768]{1,0:T(8,128)(2,1)}, bf16[256,768]{1,0:T(8,128)(2,1)S(1)}, u32[]{:S(2)}, u32[]{:S(2)}) collective-permute-start(bf16[256,768]{1,0:T(8,128)(2,1)} %product_rows.21), channel_id=1, source_target_pairs={{0,16},{4,20},{8,24},{12,28},{16,0},{20,4},{24,8},{28,12},{1,17},{... | collective-permute-start | bytes 1179656 | tf_op jit(solution)/shard_map/ppermute | solution.py:844
  520.8 27.9 %collective-permute-start.42 = (bf16[512,256]{1,0:T(8,128)(2,1)}, bf16[512,256]{1,0:T(8,128)(2,1)S(1)}, u32[]{:S(2)}, u32[]{:S(2)}) collective-permute-start(bf16[512,256]{1,0:T(8,128)(2,1)} %product_cols.15), channel_id=1, source_target_pairs={{0,16},{4,20},{8,24},{12,28},{16,0},{20,4},{24,8},{28,12},{1,17},{... | collective-permute-start | bytes 786440 | tf_op jit(solution)/shard_map/ppermute | solution.py:844
  (35 other events, 98.6 us)
